TPU v7x, 32 devices: a whole 2x2x4 slice. The times are simulated.
32 devices in a mesh: gx: 8 (over z, y), gz: 4 (over x, core).
Axes of the slice: x: 2, y: 2, z: 4, core: 2. Of those that a mesh axis runs over, the one named last changes fastest.
Arguments:
- flow_state: float32 [4, 128, 128, 128], P(None, 'gx', 'gz'), may hold values from -6 to 6
- slot_ids: int32 [256], P(('gx', 'gz')), may hold values from -1 to 127, as said below
- corners: int32 [3, 256], P(None, ('gx', 'gz')), may hold values from 0 to 127, as said below
- marker_cells: int32 [3, 256, 512], P(None, ('gx', 'gz')), may hold values from 1 to 21
- marker_frac: float32 [3, 256, 512], P(None, ('gx', 'gz')), may hold values from 0 to 1
- particle_velocity: float32 [3, 128], replicated, may hold values from -4 to 4
- particle_spin: float32 [3, 128], replicated, may hold values from -0.6 to 0.6
Outputs:
- velocity: float32 [3, 128, 128, 128], P(None, 'gx', 'gz')
- source: float32 [2, 128, 128, 128], P(None, 'gz', 'gx')
Inputs may be any that keep to these rules, and one draw needn't show every extreme that they name: `slot_ids`: the ids of the particles that a tile's device owns stand in its 8 slots and -1 in each empty slot; every id 0 to 127 stands in exactly one slot; some device has all of its slots full. corners[:, s] is the first cell of the box of slot s; the box's x and z ranges wrap around the grid; the cells (corners[0, s] + 12) mod 128 and (corners[2, s] + 12) mod 128 lie in the x and z ranges of the tile whose device holds slot s, and corners[1, s] <= 104.
All inputs are finite; a program needn't handle non-finite values.
Results may differ from a plain program's by a relative error of at most 0.0003.
Values sent between devices are 32-bit elements; how exact they have to be, the bound alone decides.
No kernel may reach another device: no remote copies, remote signals or barrier semaphores. Data moves between devices by JAX's collectives and lax.ppermute only.
A program may use at most 64 MiB of HBM per device.

v0:
```python
import functools
import math

import jax
import jax.numpy as jnp
import numpy as np
from jax import lax
from jax.experimental import pallas as pl
from jax.experimental.pallas import tpu as pltpu
from jax.sharding import PartitionSpec as P


BOX = 24
HALF = 12
WINDOW = 32
LANES = 128
KERNEL_BYTES = 16 * 1024 * 1024

time_step = 0.1
viscosity = 0.2
drive_force = 1.0


IN_VMEM = pl.BlockSpec(memory_space=pltpu.VMEM)
IN_SMEM = pl.BlockSpec(memory_space=pltpu.SMEM)
TRANSPOSED = (((1,), (1,)), ((), ()))


def float32(*shape):
    return jax.ShapeDtypeStruct(shape, jnp.float32)


def call(kernel, out_shape, scalars, arrays, scratch, flops, moved):
    outputs = len(out_shape) if isinstance(out_shape, (list, tuple)) else 0
    return pl.pallas_call(
        kernel,
        out_shape=out_shape,
        in_specs=[IN_SMEM] * len(scalars) + [IN_VMEM] * len(arrays),
        out_specs=[IN_VMEM] * outputs if outputs else IN_VMEM,
        scratch_shapes=scratch,
        compiler_params=pltpu.CompilerParams(vmem_limit_bytes=KERNEL_BYTES),
        cost_estimate=pl.CostEstimate(flops=flops, bytes_accessed=moved, transcendentals=0),
    )(*scalars, *arrays)


def shift(array, axis, step):
    devices = lax.axis_size(axis)
    return lax.ppermute(array, axis, [(i, (i + step) % devices) for i in range(devices)])


def cosine_coefficients():
    samples = 2.0 + 2.0 * np.cos(np.pi * (np.arange(64) + 0.5) / 64)
    values = np.cos(np.pi / 4 * np.sqrt(samples)) * np.sqrt(0.5)
    fit = np.polynomial.chebyshev.Chebyshev.fit(samples, values, 4, domain=[0, 4])
    return [float(v) for v in fit.convert(kind=np.polynomial.Polynomial).coef]


COSINE = cosine_coefficients()


def weight(offset):
    square = jnp.minimum(offset * offset, 4.0)
    value = COSINE[-1] * square + COSINE[-2]
    for coefficient in COSINE[-3::-1]:
        value = value * square + coefficient
    return value * value


def split(value):
    high = value.astype(jnp.bfloat16)
    low = (value - high.astype(jnp.float32)).astype(jnp.bfloat16)
    return high, low


def row_weights(count, position):
    cells = lax.broadcasted_iota(jnp.int32, (count, position.shape[1]), 0)
    return weight(cells.astype(jnp.float32) - position)


def plane_weights(weight_x, weight_z, half_z, high, low):
    count = 0
    for z in range(0, weight_z.shape[0], half_z):
        part = weight_z[z : z + half_z]
        for x in range(weight_x.shape[0]):
            rows = slice(count * half_z, (count + 1) * half_z)
            high[rows], low[rows] = split(weight_x[x : x + 1] * part)
            count += 1


def window_start(first_y, size_y):
    return pl.multiple_of(jnp.minimum((first_y // 8) * 8, size_y - WINDOW), 8)


def quarters(sizes):
    half_x, half_z = sizes[0] // 2, sizes[1] // 2
    for z in range(2):
        for x in range(2):
            yield slice(x * half_x, (x + 1) * half_x), slice(z * half_z, (z + 1) * half_z)


class Layout:
    def __init__(self, sizes, slots, markers):
        self.sizes, self.slots, self.markers = sizes, slots, markers
        self.tiles = markers // LANES
        self.fact_row = 3 * self.tiles * slots
        self.rows = self.fact_row + slots
        self.ghost_x = 4 * sizes[1]
        self.ghost_z = 4 * sizes[0]
        self.plane = sizes[0] * sizes[1]


def marker_row(layout, marks, base, direction, slot):
    first = base + direction * layout.tiles * layout.slots + slot
    rows = [marks[pl.ds(first + t * layout.slots, 1), :] for t in range(layout.tiles)]
    return jnp.concatenate(rows, axis=1)


def slot_visits(layout, facts, marks, saved, blocks, step_z, high, low, visit, skip):
    size_x, size_z, size_y = layout.sizes
    half_x, half_z = size_x // 2, size_z // 2
    slots = layout.slots

    def body(index, carry):
        block, slot = index // slots, index % slots
        block = blocks[0] + block * (blocks[1] - blocks[0] if len(blocks) > 1 else 0)
        fact = (step_z + 1) * 3 * slots + block * slots + slot
        first_x = facts[0, fact] + (block - 1) * size_x
        first_z = facts[1, fact] + step_z * size_z
        first_y = facts[2, fact]
        meets_x = (first_x > -BOX) & (first_x < size_x)
        meets_z = (first_z > -BOX) & (first_z < size_z)
        active = (facts[3, fact] != 0) & meets_x & meets_z
        whole_x = (first_x > half_x - BOX) & (first_x < half_x)
        whole_z = (first_z > half_z - BOX) & (first_z < half_z)
        upper_x = (first_x >= half_x).astype(jnp.int32)
        upper_z = (first_z >= half_z).astype(jnp.int32)

        def part(all_x, all_z):
            start_x = 0 if all_x else upper_x * half_x
            start_z = 0 if all_z else upper_z * half_z
            lanes = [
                ((0 if all_z else upper_z) + z) * 2 * LANES + (0 if all_x else upper_x) * LANES
                for z in range(2 if all_z else 1)
            ]
            width = (2 if all_x else 1) * LANES
            if all_x and all_z:
                pieces = [(0, 4 * LANES)]
            else:
                pieces = [(pl.multiple_of(lane, LANES), width) for lane in lanes]
            first = window_start(first_y, size_y)
            rows_x = slice(0, size_x if all_x else half_x)
            rows_z = slice(size_x, size_x + (size_z if all_z else half_z))
            rows_y = slice(size_x + size_z, size_x + size_z + WINDOW)
            if marks is not None:
                base = block * layout.rows
                starts = (first_x - start_x, first_z - start_z, first_y - first)
                for direction, rows in enumerate((rows_x, rows_z, rows_y)):
                    position = marker_row(layout, marks, base, direction, slot)
                    position += starts[direction].astype(jnp.float32)
                    saved[index, rows, :] = row_weights(rows.stop - rows.start, position)
            plane_weights(saved[index, rows_x, :], saved[index, rows_z, :], half_z, high, low)
            weight_y = saved[index, rows_y, :]
            visit(index, block * slots + slot, first, weight_y, pieces)

        for all_x in (True, False):
            for all_z in (True, False):
                one = whole_x if all_x else jnp.logical_not(whole_x)
                two = whole_z if all_z else jnp.logical_not(whole_z)
                pl.when(active & one & two)(functools.partial(part, all_x, all_z))

        if skip is not None:

            @pl.when(jnp.logical_not(active))
            def _():
                skip(index)

        return carry

    lax.fori_loop(0, len(blocks) * slots, body, 0)


def rigid_motion(layout, facts, marks, motion, block, slot):
    particle = facts[3, (3 + block) * layout.slots + slot] - 1
    chosen = lax.broadcasted_iota(jnp.int32, motion[0].shape, 1) == particle
    moving, turning = [
        jnp.sum(jnp.where(chosen, part[...], 0.0), axis=1, keepdims=True) for part in motion
    ]
    lever = [
        marker_row(layout, marks, block * layout.rows, direction, slot) - HALF
        for direction in (0, 2, 1)
    ]
    for c in range(3):
        a, b = (c + 1) % 3, (c + 2) % 3
        turned = turning[a : a + 1] * lever[b] - turning[b : b + 1] * lever[a]
        yield moving[c : c + 1] + turned


def sample_slots(
    layout, facts, marks, motion, field_high, field_low, out, saved, blocks, step_z, high, low
):
    def visit(index, row, first, weight_y, pieces):
        rows = pl.ds(first, WINDOW)

        def window(field):
            parts = [
                jnp.concatenate([field[c, rows, pl.ds(lane, width)] for c in range(3)], axis=0)
                for lane, width in pieces
            ]
            return jnp.concatenate(parts, axis=1).astype(jnp.bfloat16)

        window_high, window_low = window(field_high), window(field_low)
        count = window_high.shape[1]
        both = jnp.concatenate([window_high, window_low], axis=0)
        value = jnp.dot(both, high[:count], preferred_element_type=jnp.float32)
        rest = jnp.dot(window_high, low[:count], preferred_element_type=jnp.float32)
        value = value[: 3 * WINDOW] + value[3 * WINDOW :] + rest
        target = None
        if motion:
            target = list(rigid_motion(layout, facts, marks, motion, blocks[0], index))
        for c in range(3):
            part = value[c * WINDOW : (c + 1) * WINDOW] * weight_y
            sampled = jnp.sum(part, axis=0, keepdims=True)
            out[c, pl.ds(index, 1), :] = sampled if target is None else target[c] - sampled

    def skip(index):
        for c in range(3):
            out[c, pl.ds(index, 1), :] = jnp.zeros((1, layout.markers), jnp.float32)

    slot_visits(layout, facts, marks, saved, blocks, step_z, high, low, visit, skip)


def sample_kernel(layout, groups, moved, facts, *refs):
    count = len(groups)
    marks, refs = refs[:count], refs[count:]
    (field_high, field_low), refs = refs[:2], refs[2:]
    motion, refs = refs[:moved], refs[moved:]
    outs, refs = refs[:count], refs[count:]
    saved, (high, low) = refs[:count], refs[count:]
    for i, (blocks, step_z) in enumerate(groups):
        sample_slots(
            layout,
            facts,
            marks[i],
            motion,
            field_high,
            field_low,
            outs[i],
            saved[i],
            blocks,
            step_z,
            high,
            low,
        )


def visit_cost(layout, blocks):
    return len(blocks) * layout.slots * 18 * WINDOW * layout.plane * layout.markers


def weight_scratch(layout):
    return [pltpu.VMEM((layout.plane, layout.markers), jnp.bfloat16)] * 2


def sample(layout, groups, facts, marks, fields, motion):
    markers, weights = layout.markers, layout.sizes[0] + layout.sizes[1] + WINDOW
    counts = [len(blocks) * layout.slots for blocks, _ in groups]
    results = call(
        functools.partial(sample_kernel, layout, groups, len(motion)),
        [float32(3, count, markers) for count in counts]
        + [float32(count, weights, markers) for count in counts],
        [facts],
        [*marks, *fields, *motion],
        weight_scratch(layout),
        sum(visit_cost(layout, blocks) for blocks, _ in groups),
        8 * fields[0].size,
    )
    return results[: len(groups)], results[len(groups) :]


def spread_slots(layout, blocks, step_z, facts, saved, push, own_rows, total, high, low):
    def visit(index, row, first, weight_y, pieces):
        slot = index if own_rows else row
        count = sum(width for _, width in pieces)
        value = jnp.concatenate(
            [weight_y * push[c, pl.ds(slot, 1), :] for c in range(3)], axis=0
        )
        value_high, value_low = split(value)
        both = jnp.concatenate([value_high, value_low], axis=0)
        added = lax.dot_general(
            both, high[:count], TRANSPOSED, preferred_element_type=jnp.float32
        )
        rest = lax.dot_general(
            value_high, low[:count], TRANSPOSED, preferred_element_type=jnp.float32
        )
        added = added[: 3 * WINDOW] + added[3 * WINDOW :] + rest
        column = 0
        for lane, width in pieces:
            for c in range(3):
                part = added[c * WINDOW : (c + 1) * WINDOW, column : column + width]
                total[c, pl.ds(first, WINDOW), pl.ds(lane, width)] += part
            column += width

    slot_visits(layout, facts, None, saved, blocks, step_z, high, low, visit, None)


def spread_own_kernel(layout, facts, saved, push, total, high, low):
    total[...] = jnp.zeros(total.shape, jnp.float32)
    spread_slots(layout, (1,), 0, facts, saved, push, True, total, high, low)


def spread_own(layout, facts, saved, push):
    return call(
        functools.partial(spread_own_kernel, layout),
        float32(3, layout.sizes[2], layout.plane),
        [facts],
        [saved, push],
        weight_scratch(layout),
        visit_cost(layout, (1,)),
        12 * layout.sizes[2] * layout.plane,
    )


def spread_side_kernel(layout, facts, saved, push, before, total, high, low):
    total[...] = before[...]
    spread_slots(layout, (0, 2), 0, facts, saved, push, False, total, high, low)


def spread_side(layout, facts, saved, push, before):
    return call(
        functools.partial(spread_side_kernel, layout),
        float32(*before.shape),
        [facts],
        [saved, push, before],
        weight_scratch(layout),
        visit_cost(layout, (0, 2)),
        8 * before.size,
    )


def spread_rest_kernel(
    layout,
    facts,
    lower_saved,
    upper_saved,
    lower_push,
    upper_push,
    before,
    predicted,
    velocity,
    u_first,
    u_last,
    w_first,
    w_last,
    inner,
    total,
    high,
    low,
):
    size_x, size_z, size_y = layout.sizes
    total[...] = before[...]
    row = (0, 1, 2)
    spread_slots(layout, row, -1, facts, lower_saved, lower_push, False, total, high, low)
    spread_slots(layout, row, 1, facts, upper_saved, upper_push, False, total, high, low)
    for c in range(3):
        for q, (xs, zs) in enumerate(quarters(layout.sizes)):
            part = jnp.transpose(total[c, :, q * LANES : (q + 1) * LANES])
            part = part.reshape(size_x // 2, size_z // 2, size_y)
            velocity[c, xs, zs] = predicted[c, xs, zs] + part
    u_first[...] = velocity[0, 0]
    u_last[...] = velocity[0, size_x - 1]
    for x in range(size_x):
        w_first[x : x + 1] = velocity[2, x, 0:1]
        w_last[x : x + 1] = velocity[2, x, size_z - 1 : size_z]
    row = lax.broadcasted_iota(jnp.int32, (size_z, size_y), 0)
    lane = lax.broadcasted_iota(jnp.int32, (size_z, size_y), 1)
    for x in range(size_x):
        y_minus, y_plus = y_neighbours(velocity[1, x], lane, 0.0, 0.0)
        z_minus, z_plus = z_neighbours(velocity[2, x], row, 0.0, 0.0)
        change = y_plus - y_minus + z_plus - z_minus
        if x > 0:
            change -= velocity[0, x - 1]
        if x < size_x - 1:
            change += velocity[0, x + 1]
        inner[x] = change * 0.5


def spread_rest(layout, facts, saved, pushes, before, predicted):
    size_x, size_z, size_y = layout.sizes
    return call(
        functools.partial(spread_rest_kernel, layout),
        [float32(3, size_x, size_z, size_y)]
        + [float32(size_z, size_y)] * 2
        + [float32(size_x, size_y)] * 2
        + [float32(size_x, size_z, size_y)],
        [facts],
        [*saved, *pushes, before, predicted],
        [pltpu.VMEM(before.shape, jnp.float32)] + weight_scratch(layout),
        2 * visit_cost(layout, (0, 1, 2)),
        12 * before.size,
    )


def pack_kernel(
    layout,
    slot_ids_hbm,
    corners_hbm,
    flow,
    cells_hbm,
    fraction_hbm,
    own,
    x_last,
    x_first,
    z_last,
    z_first,
    slot_ids,
    corners,
    cells,
    fraction,
    edges,
    done,
):
    size_x, size_z, _ = layout.sizes
    slots = layout.slots
    moves = [
        (slot_ids_hbm, slot_ids),
        (corners_hbm, corners),
        (cells_hbm, cells),
        (fraction_hbm, fraction),
    ]
    for c in range(4):
        moves.append((flow.at[c, :, pl.ds(size_z - 8, 8)], edges.at[0, c]))
        moves.append((flow.at[c, :, pl.ds(0, 8)], edges.at[1, c]))
    for c in range(4):
        rows = pl.ds(c * size_z, size_z)
        moves.append((flow.at[c, size_x - 1], x_last.at[rows]))
        moves.append((flow.at[c, 0], x_first.at[rows]))
    copies = [pltpu.make_async_copy(a, b, done.at[i]) for i, (a, b) in enumerate(moves)]
    for copy in copies:
        copy.start()
    for copy in copies[:4]:
        copy.wait()
    length_x = size_x * lax.axis_size("gx")
    length_z = size_z * lax.axis_size("gz")
    offset_x = length_x + HALF - lax.axis_index("gx") * size_x
    offset_z = length_z + HALF - lax.axis_index("gz") * size_z
    targets = ((own, 0), (z_last, layout.ghost_z), (z_first, layout.ghost_z))
    for a, direction in enumerate((0, 2, 1)):
        for t in range(layout.tiles):
            lanes = slice(t * LANES, (t + 1) * LANES)
            place = cells[direction, :, lanes].astype(jnp.float32) + fraction[direction, :, lanes]
            for target, base in targets:
                first = base + (a * layout.tiles + t) * slots
                target[first : first + slots] = place
    lane = lax.broadcasted_iota(jnp.int32, (1, LANES), 1)
    for slot in range(slots):
        first_x = lax.rem(corners[0, slot] + offset_x, length_x) - HALF
        first_z = lax.rem(corners[2, slot] + offset_z, length_z) - HALF
        fact = jnp.where(lane == 0, first_x, slot_ids[slot] + 1)
        fact = jnp.where(lane == 1, first_z, fact)
        fact = jnp.where(lane == 2, corners[1, slot], fact)
        for target, base in targets:
            row = base + layout.fact_row + slot
            target[row : row + 1] = fact.astype(jnp.float32)
    for copy in copies[4:]:
        copy.wait()
    for c in range(4):
        for x in range(size_x):
            row = c * size_x + x
            z_last[row : row + 1] = edges[0, c, x, 7:8]
            z_first[row : row + 1] = edges[1, c, x, 0:1]


def pack(layout, slot_ids, corners, flow, cells, fraction):
    in_hbm = pl.BlockSpec(memory_space=pltpu.HBM)
    size_x, _, size_y = layout.sizes
    return pl.pallas_call(
        functools.partial(pack_kernel, layout),
        out_shape=[float32(layout.rows, LANES)]
        + [float32(layout.ghost_x, LANES)] * 2
        + [float32(layout.ghost_z + layout.rows, LANES)] * 2,
        in_specs=[in_hbm] * 5,
        out_specs=[IN_VMEM] * 5,
        scratch_shapes=[
            pltpu.SMEM(slot_ids.shape, jnp.int32),
            pltpu.SMEM(corners.shape, jnp.int32),
            pltpu.VMEM(cells.shape, jnp.int32),
            pltpu.VMEM(fraction.shape, jnp.float32),
            pltpu.VMEM((2, 4, size_x, 8, size_y), jnp.float32),
            pltpu.SemaphoreType.DMA((20,)),
        ],
        name="pack",
        cost_estimate=pl.CostEstimate(
            flops=flow.size, bytes_accessed=flow.size, transcendentals=0
        ),
    )(slot_ids, corners, flow, cells, fraction)


def join_kernel(left, right, both):
    rows = left.shape[0]
    both[:rows] = left[...]
    both[rows:] = right[...]


def join(left, right):
    return call(
        join_kernel,
        float32(2 * left.shape[0], LANES),
        [],
        [left, right],
        [],
        left.size,
        16 * left.size,
    )


def collect_kernel(layout, own, left, right, below, above, corners_below, corners_above, *refs):
    rows, (facts, table) = refs[:3], refs[3:]
    count = layout.rows
    for row, middle, base, sides in (
        (rows[0], below, layout.ghost_z, corners_below),
        (rows[1], own, 0, None),
        (rows[2], above, layout.ghost_z, corners_above),
    ):
        row[:count] = left[...] if sides is None else sides[:count]
        row[count : 2 * count] = middle[base : base + count]
        row[2 * count :] = right[...] if sides is None else sides[count:]
    for block in range(9):
        first = (block % 3) * count + layout.fact_row
        out = slice(block * layout.slots, (block + 1) * layout.slots)
        table[out] = rows[block // 3][first : first + layout.slots]
    facts[...] = jnp.transpose(table[...])[:8].astype(jnp.int32)


def collect(layout, *tiles):
    return call(
        functools.partial(collect_kernel, layout),
        [float32(3 * layout.rows, LANES)] * 3 + [jax.ShapeDtypeStruct((8, LANES), jnp.int32)],
        [],
        tiles,
        [pltpu.VMEM((LANES, LANES), jnp.float32)],
        layout.rows * LANES,
        72 * layout.rows * LANES,
    )


def y_neighbours(value, lane, below, above):
    size_y = value.shape[-1]
    minus = jnp.where(lane == 0, below, pltpu.roll(value, 1, 1))
    plus = jnp.where(lane == size_y - 1, above, pltpu.roll(value, size_y - 1, 1))
    return minus, plus


def z_neighbours(value, row, below, above):
    size_z = value.shape[0]
    minus = jnp.where(row == 0, below, pltpu.roll(value, 1, 0))
    plus = jnp.where(row == size_z - 1, above, pltpu.roll(value, size_z - 1, 0))
    return minus, plus


def predict_inner_kernel(sizes, flow, inner, u_first, u_last, w_first, w_last):
    size_x, size_z, size_y = sizes
    row = lax.broadcasted_iota(jnp.int32, (size_z, size_y), 0)
    lane = lax.broadcasted_iota(jnp.int32, (size_z, size_y), 1)
    nothing = jnp.zeros((size_z, size_y), jnp.float32)

    def around(c, x):
        value = flow[c, x]
        x_minus = flow[c, x - 1] if x > 0 else nothing
        x_plus = flow[c, x + 1] if x < size_x - 1 else nothing
        z_minus, z_plus = z_neighbours(value, row, 0.0, 0.0)
        edges = (0.0, 0.0) if c < 3 else (value, value)
        y_minus, y_plus = y_neighbours(value, lane, *edges)
        return value, x_minus, x_plus, z_minus, z_plus, y_minus, y_plus

    for x in range(size_x):
        _, x_minus, x_plus, z_minus, z_plus, y_minus, y_plus = around(3, x)
        gradient = (
            (x_plus - x_minus) * 0.5 - drive_force,
            (y_plus - y_minus) * 0.5,
            (z_plus - z_minus) * 0.5,
        )
        carried = (flow[0, x], flow[1, x], flow[2, x])
        for c in range(3):
            value, x_minus, x_plus, z_minus, z_plus, y_minus, y_plus = around(c, x)
            laplace = x_plus + x_minus + z_plus + z_minus + y_plus + y_minus - 6.0 * value
            advect = (
                carried[0] * (x_plus - x_minus)
                + carried[1] * (y_plus - y_minus)
                + carried[2] * (z_plus - z_minus)
            ) * 0.5
            inner[c, x] = value + time_step * (viscosity * laplace - advect - gradient[c])
        w_first[x : x + 1] = flow[2, x, 0:1]
        w_last[x : x + 1] = flow[2, x, size_z - 1 : size_z]
    u_first[...] = flow[0, 0]
    u_last[...] = flow[0, size_x - 1]


def predict_inner(sizes, flow):
    size_x, size_z, size_y = sizes
    return call(
        functools.partial(predict_inner_kernel, sizes),
        [float32(3, *sizes)] + [float32(size_z, size_y)] * 2 + [float32(size_x, size_y)] * 2,
        [],
        [flow],
        [],
        200 * flow.size,
        8 * flow.size,
    )


def predict_outer_kernel(
    layout,
    inner,
    u_first,
    u_last,
    w_first,
    w_last,
    left,
    right,
    lower,
    upper,
    predicted,
    field_high,
    field_low,
):
    size_x, size_z, size_y = layout.sizes
    row = lax.broadcasted_iota(jnp.int32, (8, size_y), 0)
    for x in range(size_x):
        carried_low = w_first[x : x + 1]
        carried_high = w_last[x : x + 1]
        for c in range(3):
            ghost = c * size_x + x
            change_low = (viscosity + 0.5 * carried_low) * lower[ghost : ghost + 1]
            change_high = (viscosity - 0.5 * carried_high) * upper[ghost : ghost + 1]
            if c == 2:
                ghost = 3 * size_x + x
                change_low += 0.5 * lower[ghost : ghost + 1]
                change_high -= 0.5 * upper[ghost : ghost + 1]
            if x in (0, size_x - 1):
                sign, layer, carried = (0.5, left, u_first) if x == 0 else (-0.5, right, u_last)
                ghost = slice(c * size_z, (c + 1) * size_z)
                change = (viscosity + sign * carried[...]) * layer[ghost]
                if c == 0:
                    change += sign * layer[3 * size_z : 4 * size_z]
                predicted[c, x] = inner[c, x] + time_step * change
            else:
                predicted[c, x] = inner[c, x]
            predicted[c, x, 0:8] += jnp.where(row == 0, time_step * change_low, 0.0)
            predicted[c, x, size_z - 8 : size_z] += jnp.where(
                row == 7, time_step * change_high, 0.0
            )
    for c in range(3):
        for q, (xs, zs) in enumerate(quarters(layout.sizes)):
            part = jnp.transpose(predicted[c, xs, zs].reshape(LANES, size_y))
            high = part.astype(jnp.bfloat16).astype(jnp.float32)
            field_high[c, :, q * LANES : (q + 1) * LANES] = high
            field_low[c, :, q * LANES : (q + 1) * LANES] = part - high


def predict_outer(layout, inner, left, right, lower, upper):
    _, _, size_y = layout.sizes
    return call(
        functools.partial(predict_outer_kernel, layout),
        [float32(3, *layout.sizes)] + [float32(3, size_y, layout.plane)] * 2,
        [],
        [*inner, left, right, lower, upper],
        [],
        10 * inner[0].size,
        16 * inner[0].size,
    )


def divergence_kernel(sizes, parts, inner, u_below, u_above, w_below, w_above, *rest):
    outs, whole = rest[:parts], rest[parts]
    size_x, size_z, size_y = sizes
    row = lax.broadcasted_iota(jnp.int32, (size_z, size_y), 0)
    group = LANES // size_z
    for q in range(size_x // group):
        pieces = []
        for x in range(q * group, (q + 1) * group):
            piece = inner[x]
            if x == 0:
                piece -= 0.5 * u_below[...]
            if x == size_x - 1:
                piece += 0.5 * u_above[...]
            piece -= jnp.where(row == 0, 0.5 * w_below[x : x + 1], 0.0)
            piece += jnp.where(row == size_z - 1, 0.5 * w_above[x : x + 1], 0.0)
            pieces.append(piece)
        part = jnp.concatenate(pieces, axis=0)
        whole[:, q * LANES : (q + 1) * LANES] = jnp.transpose(part)
    height = size_y // parts
    for step in range(parts):
        first = pl.multiple_of(lax.rem(lax.axis_index("gz") + step, parts) * height, 8)
        outs[step][...] = whole[pl.ds(first, height), :]


def divergence(sizes, parts, inner, ghosts):
    size_x, size_z, size_y = sizes
    plane = size_x * size_z
    return call(
        functools.partial(divergence_kernel, sizes, parts),
        [float32(size_y // parts, plane)] * parts,
        [],
        [inner, *ghosts],
        [pltpu.VMEM((size_y, plane), jnp.float32)],
        10 * inner.size,
        8 * inner.size,
    )


def swap_groups(values, width):
    count = LANES // width
    lane = lax.broadcasted_iota(jnp.int32, values[0].shape, 1)
    values = list(values)
    step = count // 2
    while step:
        reach = step * width
        keep = lane % (2 * reach) < reach
        for i in range(count):
            if i & step == 0:
                a, b = values[i], values[i + step]
                values[i] = jnp.where(keep, a, pltpu.roll(b, reach, 1))
                values[i + step] = jnp.where(keep, pltpu.roll(a, LANES - reach, 1), b)
        step //= 2
    return values


def transform_z_kernel(sizes, counts, table_high, table_low, *refs):
    size_x, size_z, size_y = sizes
    parts_x, parts_z = counts
    pieces, refs = refs[:parts_z], refs[parts_z:]
    outs, (gathered, turned, whole) = refs[:parts_x], refs[parts_x:]
    height = size_y // parts_z
    group = LANES // size_z
    for step in range(parts_z):
        gathered[lax.rem(lax.axis_index("gz") + parts_z - step, parts_z)] = pieces[step][...]
    for block in range(parts_z // group):
        for q in range(size_x // group):
            lanes = slice(q * LANES, (q + 1) * LANES)
            values = [gathered[block * group + i, :, lanes] for i in range(group)]
            for j, value in enumerate(swap_groups(values, size_z)):
                turned[block, pl.ds(q * group + j, height, stride=size_x), :] = value
    lines = jnp.concatenate([turned[b] for b in range(turned.shape[0])], axis=1)
    high, low = split(lines)
    result = lax.dot_general(
        table_high[...], high, TRANSPOSED, preferred_element_type=jnp.float32
    )
    result += lax.dot_general(
        table_low[...], high, TRANSPOSED, preferred_element_type=jnp.float32
    )
    result += lax.dot_general(
        table_high[...], low, TRANSPOSED, preferred_element_type=jnp.float32
    )
    whole[...] = result
    rows = whole.shape[0] // parts_x
    for step in range(parts_x):
        first = pl.multiple_of(lax.rem(lax.axis_index("gx") + step, parts_x) * rows, 8)
        outs[step][...] = whole[pl.ds(first, rows), :]


def transform_z(sizes, counts, table, pieces):
    size_x, size_z, size_y = sizes
    parts_x, parts_z = counts
    length_z = size_z * parts_z
    height = size_y // parts_z
    columns = height * size_x
    return call(
        functools.partial(transform_z_kernel, sizes, counts),
        [float32(2 * length_z // parts_x, columns)] * parts_x,
        [],
        [*table, *pieces],
        [
            pltpu.VMEM((parts_z, height, size_x * size_z), jnp.float32),
            pltpu.VMEM((length_z // LANES, columns, LANES), jnp.float32),
            pltpu.VMEM((2 * length_z, columns), jnp.float32),
        ],
        12 * length_z * length_z * columns,
        12 * length_z * columns,
    )


def transform_x_kernel(sizes, counts, table_high, table_low, *refs):
    size_x, size_z, size_y = sizes
    parts_x, parts_z = counts
    pieces, (source, gathered, turned) = refs[:parts_x], refs[parts_x:]
    length_x = size_x * parts_x
    modes = size_z * parts_z // parts_x
    height = size_y // parts_z
    group = LANES // size_x
    for step in range(parts_x):
        gathered[lax.rem(lax.axis_index("gx") + parts_x - step, parts_x)] = pieces[step][...]
    for block in range(parts_x // group):
        for q in range(height // group):
            lanes = slice(q * LANES, (q + 1) * LANES)
            values = [gathered[block * group + i, :, lanes] for i in range(group)]
            for j, value in enumerate(swap_groups(values, size_x)):
                first = (q * group + j) * modes
                for c in range(2):
                    column = c * length_x + block * LANES
                    turned[first : first + modes, column : column + LANES] = value[
                        c * modes : (c + 1) * modes
                    ]
    high, low = split(turned[...])
    result = jnp.dot(high, table_high[...], preferred_element_type=jnp.float32)
    result += jnp.dot(low, table_high[...], preferred_element_type=jnp.float32)
    result += jnp.dot(high, table_low[...], preferred_element_type=jnp.float32)
    source[0] = result[:, :length_x].reshape(height, modes, length_x)
    source[1] = result[:, length_x:].reshape(height, modes, length_x)


def transform_x(sizes, counts, table, pieces):
    size_x, size_z, size_y = sizes
    parts_x, parts_z = counts
    length_x = size_x * parts_x
    modes = size_z * parts_z // parts_x
    height = size_y // parts_z
    return call(
        functools.partial(transform_x_kernel, sizes, counts),
        float32(2, height, modes, length_x),
        [],
        [*table, *pieces],
        [
            pltpu.VMEM((parts_x, *pieces[0].shape), jnp.float32),
            pltpu.VMEM((height * modes, 2 * length_x), jnp.float32),
        ],
        24 * length_x * length_x * height * modes,
        24 * length_x * height * modes,
    )


def split_table(table):
    high = table.astype(np.float32).astype(jnp.bfloat16)
    low = (table - high.astype(np.float64)).astype(np.float32).astype(jnp.bfloat16)
    return jnp.asarray(high), jnp.asarray(low)


def angles(length):
    counter = np.arange(length)
    turn = (counter[:, None] * counter[None, :] % length) * (2.0 * np.pi / length)
    return np.cos(turn), np.sin(turn)


def table_z(length, blocks):
    cosine, sine = angles(length)
    modes = length // blocks
    table = np.stack([cosine, -sine]).reshape(2, blocks, modes, length)
    return split_table(table.transpose(1, 0, 2, 3).reshape(2 * length, length))


def table_x(length, scale):
    cosine, sine = angles(length)
    return split_table(np.block([[cosine, -sine], [sine, cosine]]) * scale)


def exchange(pieces, axis):
    return [pieces[0]] + [shift(pieces[d], axis, d) for d in range(1, len(pieces))]


def on_device(
    flow_state, slot_ids, corners, marker_cells, marker_frac, particle_velocity, particle_spin
):
    sizes = flow_state.shape[1:]
    size_x, size_z, _ = sizes
    counts = (lax.axis_size("gx"), lax.axis_size("gz"))
    length_x, length_z = (size_x * counts[0], size_z * counts[1])
    slots, markers = marker_cells.shape[1:]
    layout = Layout(sizes, slots, markers)

    own, x_last, x_first, z_last, z_first = pack(
        layout, slot_ids, corners, flow_state, marker_cells, marker_frac
    )
    left = shift(own, "gx", 1)
    right = shift(own, "gx", -1)
    below, above = shift(z_last, "gz", 1), shift(z_first, "gz", -1)
    x_below, x_above = shift(x_last, "gx", 1), shift(x_first, "gx", -1)
    inner = predict_inner(sizes, flow_state)
    sides = join(left, right)
    corners_below, corners_above = shift(sides, "gz", 1), shift(sides, "gz", -1)
    predicted, *fields = predict_outer(layout, inner, x_below, x_above, below, above)
    lower, row, upper, facts = collect(
        layout, own, left, right, below, above, corners_below, corners_above
    )

    tiles = (0, 1, 2)
    parts, (lower_saved, upper_saved) = sample(
        layout, ((tiles, -1), (tiles, 1)), facts, (lower, upper), fields, ()
    )
    from_upper = shift(parts[0], "gz", -1)
    from_lower = shift(parts[1], "gz", 1)
    (side_part,), (side_saved,) = sample(layout, (((0, 2), 0),), facts, (row,), fields, ())
    from_z = from_upper + from_lower
    from_right = shift(side_part[:, :slots] + from_z[:, :slots], "gx", -1)
    from_left = shift(side_part[:, slots:] + from_z[:, 2 * slots :], "gx", 1)
    motion = (particle_velocity, particle_spin)
    (own_part,), (own_saved,) = sample(layout, (((1,), 0),), facts, (row,), fields, motion)
    push = own_part - (from_z[:, slots : 2 * slots] + from_right + from_left)

    left_push = shift(push, "gx", 1)
    right_push = shift(push, "gx", -1)
    row_push = jnp.concatenate([left_push, push, right_push], axis=1)
    lower_push = shift(row_push, "gz", 1)
    upper_push = shift(row_push, "gz", -1)
    forcing = spread_own(layout, facts, own_saved, push)
    forcing = spread_side(layout, facts, side_saved, row_push, forcing)
    velocity, u_first, u_last, w_first, w_last, change = spread_rest(
        layout, facts, (lower_saved, upper_saved), (lower_push, upper_push), forcing, predicted
    )

    ghosts = (
        shift(u_last, "gx", 1),
        shift(u_first, "gx", -1),
        shift(w_last, "gz", 1),
        shift(w_first, "gz", -1),
    )
    pieces = divergence(sizes, counts[1], change, ghosts)
    pieces = exchange(pieces, "gz")
    pieces = transform_z(sizes, counts, table_z(length_z, counts[0]), pieces)
    pieces = exchange(pieces, "gx")
    scale = 1.0 / math.sqrt(length_x * length_z)
    source = transform_x(sizes, counts, table_x(length_x, scale), pieces)
    return velocity, source


def solution(mesh):
    return jax.shard_map(
        on_device,
        mesh=mesh,
        in_specs=(
            P(None, "gx", "gz", None),
            P(("gx", "gz")),
            P(None, ("gx", "gz")),
            P(None, ("gx", "gz"), None),
            P(None, ("gx", "gz"), None),
            P(),
            P(),
        ),
        out_specs=(P(None, "gx", "gz", None), P(None, "gz", "gx", None)),
        check_vma=False,
    )
```

profile of v0, /device:TPU:0, one launch (start us, length us, event | category | flops | bytes accessed | tf_op | source)
XLA Modules:
  0.0 95.1 jit_solution(3627968278948417638)
XLA Ops:
  0.6 2.0 %pack.1 = (f32[104,128]{1,0:T(8,128)}, f32[128,128]{1,0:T(8,128)}, f32[128,128]{1,0:T(8,128)}, f32[168,128]{1,0:T(8,128)}, f32[168,128]{1,0:T(8,128)}) custom-call(s32[8]{0:T(128)} %slot_ids_hbm.1, s32[3,8]{1,0:T(4,128)} %corners_hbm.1, f32[4,16,32,128]{3,2,1,0:T(8,128)} %flow.3, s32[3,8,512]{2,1,0:T(8,128)} %cells_hbm.1, f32[3,8,512]{2,1,0:T(8,128)} %fraction_hbm.1), custom_call_target="tpu_custom_call" | custom-call | flops 262144 | bytes 262144 | tf_op jit(solution)/shard_map/pack/pallas_call | solution.py:476
  2.7 3.0 %collective-permute-start = (f32[104,128]{1,0:T(8,128)}, f32[104,128]{1,0:T(8,128)S(1)}, u32[]{:S(2)}, u32[]{:S(2)}) collective-permute-start(f32[104,128]{1,0:T(8,128)} %get-tuple-element.45.own), channel_id=1, source_target_pairs={{0,4},{4,8},{8,12},{12,16},{16,20},{20,24},{24,28},{28,0},{1,5},{5... | collective-permute-start | bytes 159752 | tf_op jit(solution)/shard_map/ppermute | solution.py:48
  5.7 3.1 %collective-permute-start.1 = (f32[104,128]{1,0:T(8,128)}, f32[104,128]{1,0:T(8,128)S(1)}, u32[]{:S(2)}, u32[]{:S(2)}) collective-permute-start(f32[104,128]{1,0:T(8,128)} %get-tuple-element.45.own), channel_id=1, source_target_pairs={{0,28},{4,0},{8,4},{12,8},{16,12},{20,16},{24,20},{28,24},{1,29},{... | collective-permute-start | bytes 159752 | tf_op jit(solution)/shard_map/ppermute | solution.py:48
  8.8 2.3 %collective-permute-done.left = f32[104,128]{1,0:T(8,128)S(1)} collective-permute-done((f32[104,128]{1,0:T(8,128)}, f32[104,128]{1,0:T(8,128)S(1)}, u32[]{:S(2)}, u32[]{:S(2)}) %collective-permute-start) | collective-permute-done | bytes 53280 | tf_op jit(solution)/shard_map/ppermute | solution.py:48
  11.1 0.1 collective-permute-done.1.right
  11.3 1.7 %collective-permute-start.5 = (f32[208,128]{1,0:T(8,128)S(1)}, f32[208,128]{1,0:T(8,128)S(1)}, u32[]{:S(2)}, u32[]{:S(2)}) collective-permute-start(f32[208,128]{1,0:T(8,128)S(1)} %shard_map.122), channel_id=1, source_target_pairs={{0,3},{1,0},{2,1},{3,2},{4,7},{5,4},{6,5},{7,6},{8,11},{9,8},{10,9... | collective-permute-start | bytes 319496 | tf_op jit(solution)/shard_map/ppermute | solution.py:48
  13.0 1.7 %collective-permute-start.3 = (f32[168,128]{1,0:T(8,128)}, f32[168,128]{1,0:T(8,128)S(1)}, u32[]{:S(2)}, u32[]{:S(2)}) collective-permute-start(f32[168,128]{1,0:T(8,128)} %get-tuple-element.47), channel_id=1, source_target_pairs={{0,3},{1,0},{2,1},{3,2},{4,7},{5,4},{6,5},{7,6},{8,11},{9,8},{10,9... | collective-permute-start | bytes 258056 | tf_op jit(solution)/shard_map/ppermute | solution.py:48
  14.8 1.2 %collective-permute-done.6.left = f32[128,128]{1,0:T(8,128)S(1)} collective-permute-done((f32[128,128]{1,0:T(8,128)}, f32[128,128]{1,0:T(8,128)S(1)}, u32[]{:S(2)}, u32[]{:S(2)}) %collective-permute-start.6) | collective-permute-done | bytes 65568 | tf_op jit(solution)/shard_map/ppermute | solution.py:48
  16.0 3.5 %collective-permute-start.7 = (f32[128,128]{1,0:T(8,128)}, f32[128,128]{1,0:T(8,128)S(1)}, u32[]{:S(2)}, u32[]{:S(2)}) collective-permute-start(f32[128,128]{1,0:T(8,128)} %get-tuple-element.57), channel_id=1, source_target_pairs={{0,28},{4,0},{8,4},{12,8},{16,12},{20,16},{24,20},{28,24},{1,29},{... | collective-permute-start | bytes 196616 | tf_op jit(solution)/shard_map/ppermute | solution.py:48
  19.5 1.2 %copy-done = f32[4,16,32,128]{3,2,1,0:T(8,128)S(1)} copy-done((f32[4,16,32,128]{3,2,1,0:T(8,128)S(1)}, f32[4,16,32,128]{3,2,1,0:T(8,128)}, u32[]{:S(2)}) %copy-start) | copy-done | bytes 1048600
  20.8 0.9 shard_map.124
  21.6 0.1 collective-permute-done.7.right
  21.8 0.3 shard_map.125
  22.1 0.8 copy-done.5
  22.9 0.1 shard_map.123
  23.0 5.3 %shard_map.126 = (f32[3,24,512]{2,1,0:T(8,128)S(1)}, f32[3,24,512]{2,1,0:T(8,128)S(1)}, f32[24,80,512]{2,1,0:T(8,128)S(1)}, f32[24,80,512]{2,1,0:T(8,128)S(1)}) custom-call(s32[8,128]{1,0:T(8,128)S(1)} %get-tuple-element.48.facts, f32[312,128]{1,0:T(8,128)S(1)} %get-tuple-element.49.refs_0_, f32[312,128]{1,0:T(8,128)S(1)} %get-tuple-element.50.refs_1_, ...), custom_call_target="tpu_custom_call" | custom-call | flops 7247757312 | bytes 1572864 | tf_op jit(solution)/shard_map/pallas_call | solution.py:35
  28.4 0.5 collective-permute-start.9
  28.9 2.8 %shard_map.128 = (f32[3,16,512]{2,1,0:T(8,128)S(1)}, f32[16,80,512]{2,1,0:T(8,128)S(1)}) custom-call(s32[8,128]{1,0:T(8,128)S(1)} %get-tuple-element.48.facts, f32[312,128]{1,0:T(8,128)S(1)} %get-tuple-element.62.refs_0_, f32[3,128,512]{2,1,0:T(8,128)S(1)} %get-tuple-element.58.refs_2_.refs_1_, f32[3,128,512]{2,1,0:T(8,128)S(1)} %get-tuple-element.59.refs_3_.refs_2_), custom_call_target="tpu_custom_call" | custom-call | flops 2415919104 | bytes 1572864 | tf_op jit(solution)/shard_map/pallas_call | solution.py:35
  31.7 0.8 collective-permute-done.8
  32.5 1.0 %collective-permute-done.9 = f32[3,24,512]{2,1,0:T(8,128)S(1)} collective-permute-done((f32[3,24,512]{2,1,0:T(8,128)S(1)}, f32[3,24,512]{2,1,0:T(8,128)S(1)}, u32[]{:S(2)}, u32[]{:S(2)}) %collective-permute-start.9) | collective-permute-done | bytes 147488 | tf_op jit(solution)/shard_map/ppermute | solution.py:48
  33.6 0.5 collective-permute-start.11
  34.1 5.6 %collective-permute-start.10 = (f32[3,8,512]{2,1,0:T(8,128)S(1)}, f32[3,8,512]{2,1,0:T(8,128)S(1)}, u32[]{:S(2)}, u32[]{:S(2)}) collective-permute-start(f32[3,8,512]{2,1,0:T(8,128)S(1)} %get-tuple-element.88), channel_id=1, source_target_pairs={{0,28},{4,0},{8,4},{12,8},{16,12},{20,16},{24,20},{28,24},{1,29},{... | collective-permute-start | bytes 147464 | tf_op jit(solution)/shard_map/ppermute | solution.py:48
  39.8 1.0 %shard_map.127 = (f32[3,8,512]{2,1,0:T(8,128)S(1)}, f32[8,80,512]{2,1,0:T(8,128)S(1)}) custom-call(s32[8,128]{1,0:T(8,128)S(1)} %get-tuple-element.48.facts, f32[312,128]{1,0:T(8,128)S(1)} %get-tuple-element.62.refs_0_, f32[3,128,512]{2,1,0:T(8,128)S(1)} %get-tuple-element.58.refs_2_.refs_1_, f32[3,128,512]{2,1,0:T(8,128)S(1)} %get-tuple-element.59.refs_3_.refs_2_, ...), custom_call_target="tpu_custom_call" | custom-call | flops 1207959552 | bytes 1572864 | tf_op jit(solution)/shard_map/pallas_call | solution.py:35
  40.7 1.0 %collective-permute-done.11 = f32[3,8,512]{2,1,0:T(8,128)S(1)} collective-permute-done((f32[3,8,512]{2,1,0:T(8,128)S(1)}, f32[3,8,512]{2,1,0:T(8,128)S(1)}, u32[]{:S(2)}, u32[]{:S(2)}) %collective-permute-start.11) | collective-permute-done | bytes 49184 | tf_op jit(solution)/shard_map/ppermute | solution.py:48
  41.8 5.0 %collective-permute-start.13 = (f32[3,8,512]{2,1,0:T(8,128)S(1)}, f32[3,8,512]{2,1,0:T(8,128)S(1)}, u32[]{:S(2)}, u32[]{:S(2)}) collective-permute-start(f32[3,8,512]{2,1,0:T(8,128)S(1)} %fusion.1.push), channel_id=1, source_target_pairs={{0,28},{4,0},{8,4},{12,8},{16,12},{20,16},{24,20},{28,24},{1,29},{... | collective-permute-start | bytes 147464 | tf_op jit(solution)/shard_map/ppermute | solution.py:48
  46.8 1.0 %shard_map.129.before = f32[3,128,512]{2,1,0:T(8,128)S(1)} custom-call(s32[8,128]{1,0:T(8,128)S(1)} %get-tuple-element.48.facts, f32[8,80,512]{2,1,0:T(8,128)S(1)} %get-tuple-element.68.saved, f32[3,8,512]{2,1,0:T(8,128)S(1)} %fusion.1.push), custom_call_target="tpu_custom_call" | custom-call | flops 1207959552 | bytes 786432 | tf_op jit(solution)/shard_map/pallas_call | solution.py:35
  47.8 0.8 collective-permute-done.13
  48.5 5.0 %collective-permute-done.12 = f32[3,8,512]{2,1,0:T(8,128)S(1)} collective-permute-done((f32[3,8,512]{2,1,0:T(8,128)S(1)}, f32[3,8,512]{2,1,0:T(8,128)S(1)}, u32[]{:S(2)}, u32[]{:S(2)}) %collective-permute-start.12) | collective-permute-done | bytes 49184 | tf_op jit(solution)/shard_map/ppermute | solution.py:48
  53.6 1.7 %collective-permute-start.15 = (f32[3,24,512]{2,1,0:T(8,128)S(1)}, f32[3,24,512]{2,1,0:T(8,128)S(1)}, u32[]{:S(2)}, u32[]{:S(2)}) collective-permute-start(f32[3,24,512]{2,1,0:T(8,128)S(1)} %pad_maximum_fusion.push), channel_id=1, source_target_pairs={{0,3},{1,0},{2,1},{3,2},{4,7},{5,4},{6,5},{7,6},{8,11},{9,8},{10,9... | collective-permute-start | bytes 442376 | tf_op jit(solution)/shard_map/ppermute | solution.py:48
  55.4 2.8 %shard_map.130.before = f32[3,128,512]{2,1,0:T(8,128)S(1)} custom-call(s32[8,128]{1,0:T(8,128)S(1)} %get-tuple-element.48.facts, f32[16,80,512]{2,1,0:T(8,128)S(1)} %get-tuple-element.67.saved, f32[3,24,512]{2,1,0:T(8,128)S(1)} %pad_maximum_fusion.push, f32[3,128,512]{2,1,0:T(8,128)S(1)} %shard_map.129.before), custom_call_target="tpu_custom_call" | custom-call | flops 2415919104 | bytes 1572864 | tf_op jit(solution)/shard_map/pallas_call | solution.py:35
  58.2 0.8 collective-permute-done.14.lower_push
  59.0 6.4 %shard_map.131 = (f32[3,16,32,128]{3,2,1,0:T(8,128)}, f32[32,128]{1,0:T(8,128)S(1)}, f32[32,128]{1,0:T(8,128)S(1)}, f32[16,128]{1,0:T(8,128)S(1)}, f32[16,128]{1,0:T(8,128)S(1)}, /*index=5*/f32[16,32,128]{2,1,0:T(8,128)S(1)}) custom-call(s32[8,128]{1,0:T(8,128)S(1)} %get-tuple-element.48.facts, f32[24,80,512]{2,1,0:T(8,128)S(1)} %get-tuple-element.60.lower_saved, ...), custom_call_target="tpu_custom_call" | custom-call | flops 7247757312 | bytes 2359296 | tf_op jit(solution)/shard_map/pallas_call | solution.py:35
  65.5 4.7 %collective-permute-start.17 = (f32[32,128]{1,0:T(8,128)S(1)}, f32[32,128]{1,0:T(8,128)S(1)}, u32[]{:S(2)}, u32[]{:S(2)}) collective-permute-start(f32[32,128]{1,0:T(8,128)S(1)} %get-tuple-element.73), channel_id=1, source_target_pairs={{0,28},{4,0},{8,4},{12,8},{16,12},{20,16},{24,20},{28,24},{1,29},{... | collective-permute-start | bytes 49160 | tf_op jit(solution)/shard_map/ppermute | solution.py:48
  70.2 1.7 %collective-permute-start.19 = (f32[16,128]{1,0:T(8,128)S(1)}, f32[16,128]{1,0:T(8,128)S(1)}, u32[]{:S(2)}, u32[]{:S(2)}) collective-permute-start(f32[16,128]{1,0:T(8,128)S(1)} %get-tuple-element.75), channel_id=1, source_target_pairs={{0,3},{1,0},{2,1},{3,2},{4,7},{5,4},{6,5},{7,6},{8,11},{9,8},{10,9... | collective-permute-start | bytes 24584 | tf_op jit(solution)/shard_map/ppermute | solution.py:48
  72.0 1.3 %collective-permute-done.18.w_below = f32[16,128]{1,0:T(8,128)S(1)} collective-permute-done((f32[16,128]{1,0:T(8,128)S(1)}, f32[16,128]{1,0:T(8,128)S(1)}, u32[]{:S(2)}, u32[]{:S(2)}) %collective-permute-start.18) | collective-permute-done | bytes 8224 | tf_op jit(solution)/shard_map/ppermute | solution.py:48
  73.3 0.2 shard_map.132
  73.6 2.1 %collective-permute-start.21 = (f32[32,512]{1,0:T(8,128)S(1)}, f32[32,512]{1,0:T(8,128)S(1)}, u32[]{:S(2)}, u32[]{:S(2)}) collective-permute-start(f32[32,512]{1,0:T(8,128)S(1)} %get-tuple-element.78), channel_id=1, source_target_pairs={{0,2},{1,3},{2,0},{3,1},{4,6},{5,7},{6,4},{7,5},{8,10},{9,11},{10,... | collective-permute-start | bytes 196616 | tf_op jit(solution)/shard_map/ppermute | solution.py:48
  75.7 1.6 %collective-permute-done.20.refs_1_ = f32[32,512]{1,0:T(8,128)S(1)} collective-permute-done((f32[32,512]{1,0:T(8,128)S(1)}, f32[32,512]{1,0:T(8,128)S(1)}, u32[]{:S(2)}, u32[]{:S(2)}) %collective-permute-start.20) | collective-permute-done | bytes 65568 | tf_op jit(solution)/shard_map/ppermute | solution.py:48
  77.3 1.3 %collective-permute-done.21.refs_2_ = f32[32,512]{1,0:T(8,128)S(1)} collective-permute-done((f32[32,512]{1,0:T(8,128)S(1)}, f32[32,512]{1,0:T(8,128)S(1)}, u32[]{:S(2)}, u32[]{:S(2)}) %collective-permute-start.21) | collective-permute-done | bytes 65568 | tf_op jit(solution)/shard_map/ppermute | solution.py:48
  78.6 0.7 shard_map.133
  79.3 0.1 collective-permute-start.24
  79.4 1.1 %collective-permute-start.25 = (f32[32,512]{1,0:T(8,128)S(1)}, f32[32,512]{1,0:T(8,128)S(1)}, u32[]{:S(2)}, u32[]{:S(2)}) collective-permute-start(f32[32,512]{1,0:T(8,128)S(1)} %get-tuple-element.83), channel_id=1, source_target_pairs={{0,12},{4,16},{8,20},{12,24},{16,28},{20,0},{24,4},{28,8},{1,13},{... | collective-permute-start | bytes 196616 | tf_op jit(solution)/shard_map/ppermute | solution.py:48
  80.5 4.1 %collective-permute-start.26 = (f32[32,512]{1,0:T(8,128)S(1)}, f32[32,512]{1,0:T(8,128)S(1)}, u32[]{:S(2)}, u32[]{:S(2)}) collective-permute-start(f32[32,512]{1,0:T(8,128)S(1)} %get-tuple-element.84), channel_id=1, source_target_pairs={{0,16},{4,20},{8,24},{12,28},{16,0},{20,4},{24,8},{28,12},{1,17},{... | collective-permute-start | bytes 196616 | tf_op jit(solution)/shard_map/ppermute | solution.py:48
  84.6 3.0 %collective-permute-start.27 = (f32[32,512]{1,0:T(8,128)S(1)}, f32[32,512]{1,0:T(8,128)S(1)}, u32[]{:S(2)}, u32[]{:S(2)}) collective-permute-start(f32[32,512]{1,0:T(8,128)S(1)} %get-tuple-element.85), channel_id=1, source_target_pairs={{0,20},{4,24},{8,28},{12,0},{16,4},{20,8},{24,12},{28,16},{1,21},{... | collective-permute-start | bytes 196616 | tf_op jit(solution)/shard_map/ppermute | solution.py:48
  87.6 2.0 %collective-permute-start.29 = (f32[32,512]{1,0:T(8,128)S(1)}, f32[32,512]{1,0:T(8,128)S(1)}, u32[]{:S(2)}, u32[]{:S(2)}) collective-permute-start(f32[32,512]{1,0:T(8,128)S(1)} %get-tuple-element.87), channel_id=1, source_target_pairs={{0,28},{4,0},{8,4},{12,8},{16,12},{20,16},{24,20},{28,24},{1,29},{... | collective-permute-start | bytes 196616 | tf_op jit(solution)/shard_map/ppermute | solution.py:48
  89.6 2.7 %collective-permute-done.25.refs_3_ = f32[32,512]{1,0:T(8,128)S(1)} collective-permute-done((f32[32,512]{1,0:T(8,128)S(1)}, f32[32,512]{1,0:T(8,128)S(1)}, u32[]{:S(2)}, u32[]{:S(2)}) %collective-permute-start.25) | collective-permute-done | bytes 65568 | tf_op jit(solution)/shard_map/ppermute | solution.py:48
  92.3 1.2 %collective-permute-done.28.refs_6_ = f32[32,512]{1,0:T(8,128)S(1)} collective-permute-done((f32[32,512]{1,0:T(8,128)S(1)}, f32[32,512]{1,0:T(8,128)S(1)}, u32[]{:S(2)}, u32[]{:S(2)}) %collective-permute-start.28) | collective-permute-done | bytes 65568 | tf_op jit(solution)/shard_map/ppermute | solution.py:48
  93.5 1.6 %shard_map.134 = f32[2,32,16,128]{3,2,1,0:T(8,128)} custom-call(bf16[256,256]{1,0:T(8,128)(2,1)S(1)} %copy-done.1, bf16[256,256]{1,0:T(8,128)(2,1)S(1)} %copy-done.2, f32[32,512]{1,0:T(8,128)S(1)} %get-tuple-element.80.refs_0_, f32[32,512]{1,0:T(8,128)S(1)} %collective-permute-done.23.refs_1_, f32[32,512]{1,0:T(8,128)S(1)} %collective-permute-done.24.refs_2_, ...), custom_call_target="tpu_custom_call" | custom-call | flops 201326592 | bytes 1572864 | tf_op jit(solution)/shard_map/pallas_call | solution.py:35
  (46 shorter events, 0.5 us)
Async XLA Ops:
  2.7 8.4 %collective-permute-start = (f32[104,128]{1,0:T(8,128)}, f32[104,128]{1,0:T(8,128)S(1)}, u32[]{:S(2)}, u32[]{:S(2)}) collective-permute-start(f32[104,128]{1,0:T(8,128)} %get-tuple-element.45.own), channel_id=1, source_target_pairs={{0,4},{4,8},{8,12},{12,16},{16,20},{20,24},{24,28},{28,0},{1,5},{5... | collective-permute-start | bytes 159752 | tf_op jit(solution)/shard_map/ppermute | solution.py:48
  5.7 5.5 %collective-permute-start.1 = (f32[104,128]{1,0:T(8,128)}, f32[104,128]{1,0:T(8,128)S(1)}, u32[]{:S(2)}, u32[]{:S(2)}) collective-permute-start(f32[104,128]{1,0:T(8,128)} %get-tuple-element.45.own), channel_id=1, source_target_pairs={{0,28},{4,0},{8,4},{12,8},{16,12},{20,16},{24,20},{28,24},{1,29},{... | collective-permute-start | bytes 159752 | tf_op jit(solution)/shard_map/ppermute | solution.py:48
  8.8 7.2 %collective-permute-start.6 = (f32[128,128]{1,0:T(8,128)}, f32[128,128]{1,0:T(8,128)S(1)}, u32[]{:S(2)}, u32[]{:S(2)}) collective-permute-start(f32[128,128]{1,0:T(8,128)} %get-tuple-element.56), channel_id=1, source_target_pairs={{0,4},{4,8},{8,12},{12,16},{16,20},{20,24},{24,28},{28,0},{1,5},{5... | collective-permute-start | bytes 196616 | tf_op jit(solution)/shard_map/ppermute | solution.py:48
  11.2 10.9 %collective-permute-start.4 = (f32[208,128]{1,0:T(8,128)S(1)}, f32[208,128]{1,0:T(8,128)S(1)}, u32[]{:S(2)}, u32[]{:S(2)}) collective-permute-start(f32[208,128]{1,0:T(8,128)S(1)} %shard_map.122), channel_id=1, source_target_pairs={{0,1},{1,2},{2,3},{3,0},{4,5},{5,6},{6,7},{7,4},{8,9},{9,10},{10,1... | collective-permute-start | bytes 319496 | tf_op jit(solution)/shard_map/ppermute | solution.py:48
  11.3 10.8 %collective-permute-start.5 = (f32[208,128]{1,0:T(8,128)S(1)}, f32[208,128]{1,0:T(8,128)S(1)}, u32[]{:S(2)}, u32[]{:S(2)}) collective-permute-start(f32[208,128]{1,0:T(8,128)S(1)} %shard_map.122), channel_id=1, source_target_pairs={{0,3},{1,0},{2,1},{3,2},{4,7},{5,4},{6,5},{7,6},{8,11},{9,8},{10,9... | collective-permute-start | bytes 319496 | tf_op jit(solution)/shard_map/ppermute | solution.py:48
  13.0 8.7 %collective-permute-start.2 = (f32[168,128]{1,0:T(8,128)}, f32[168,128]{1,0:T(8,128)S(1)}, u32[]{:S(2)}, u32[]{:S(2)}) collective-permute-start(f32[168,128]{1,0:T(8,128)} %get-tuple-element.46), channel_id=1, source_target_pairs={{0,1},{1,2},{2,3},{3,0},{4,5},{5,6},{6,7},{7,4},{8,9},{9,10},{10,1... | collective-permute-start | bytes 258056 | tf_op jit(solution)/shard_map/ppermute | solution.py:48
  13.0 8.7 %collective-permute-start.3 = (f32[168,128]{1,0:T(8,128)}, f32[168,128]{1,0:T(8,128)S(1)}, u32[]{:S(2)}, u32[]{:S(2)}) collective-permute-start(f32[168,128]{1,0:T(8,128)} %get-tuple-element.47), channel_id=1, source_target_pairs={{0,3},{1,0},{2,1},{3,2},{4,7},{5,4},{6,5},{7,6},{8,11},{9,8},{10,9... | collective-permute-start | bytes 258056 | tf_op jit(solution)/shard_map/ppermute | solution.py:48
  16.0 5.8 %collective-permute-start.7 = (f32[128,128]{1,0:T(8,128)}, f32[128,128]{1,0:T(8,128)S(1)}, u32[]{:S(2)}, u32[]{:S(2)}) collective-permute-start(f32[128,128]{1,0:T(8,128)} %get-tuple-element.57), channel_id=1, source_target_pairs={{0,28},{4,0},{8,4},{12,8},{16,12},{20,16},{24,20},{28,24},{1,29},{... | collective-permute-start | bytes 196616 | tf_op jit(solution)/shard_map/ppermute | solution.py:48
  19.5 1.2 %copy-start = (f32[4,16,32,128]{3,2,1,0:T(8,128)S(1)}, f32[4,16,32,128]{3,2,1,0:T(8,128)}, u32[]{:S(2)}) copy-start(f32[4,16,32,128]{3,2,1,0:T(8,128)} %flow.3) | copy-start | bytes 3145732
  22.1 0.8 copy-start.5
  28.3 4.2 %collective-permute-start.8 = (f32[3,24,512]{2,1,0:T(8,128)S(1)}, f32[3,24,512]{2,1,0:T(8,128)S(1)}, u32[]{:S(2)}, u32[]{:S(2)}) collective-permute-start(f32[3,24,512]{2,1,0:T(8,128)S(1)} %get-tuple-element.64), channel_id=1, source_target_pairs={{0,3},{1,0},{2,1},{3,2},{4,7},{5,4},{6,5},{7,6},{8,11},{9,8},{10,9... | collective-permute-start | bytes 442376 | tf_op jit(solution)/shard_map/ppermute | solution.py:48
  28.4 5.1 %collective-permute-start.9 = (f32[3,24,512]{2,1,0:T(8,128)S(1)}, f32[3,24,512]{2,1,0:T(8,128)S(1)}, u32[]{:S(2)}, u32[]{:S(2)}) collective-permute-start(f32[3,24,512]{2,1,0:T(8,128)S(1)} %get-tuple-element.65), channel_id=1, source_target_pairs={{0,1},{1,2},{2,3},{3,0},{4,5},{5,6},{6,7},{7,4},{8,9},{9,10},{10,1... | collective-permute-start | bytes 442376 | tf_op jit(solution)/shard_map/ppermute | solution.py:48
  28.9 10.9 %copy-start.6 = (f32[3,128]{1,0:T(4,128)S(1)}, f32[3,128]{1,0:T(4,128)}, u32[]{:S(2)}) copy-start(f32[3,128]{1,0:T(4,128)} %refs_3_.1) | copy-start | bytes 4612
  28.9 10.9 %copy-start.7 = (f32[3,128]{1,0:T(4,128)S(1)}, f32[3,128]{1,0:T(4,128)}, u32[]{:S(2)}) copy-start(f32[3,128]{1,0:T(4,128)} %refs_4_.1) | copy-start | bytes 4612
  33.6 8.2 %collective-permute-start.11 = (f32[3,8,512]{2,1,0:T(8,128)S(1)}, f32[3,8,512]{2,1,0:T(8,128)S(1)}, u32[]{:S(2)}, u32[]{:S(2)}) collective-permute-start(f32[3,8,512]{2,1,0:T(8,128)S(1)} %get-tuple-element.89), channel_id=1, source_target_pairs={{0,4},{4,8},{8,12},{12,16},{16,20},{20,24},{24,28},{28,0},{1,5},{5... | collective-permute-start | bytes 147464 | tf_op jit(solution)/shard_map/ppermute | solution.py:48
  34.1 7.6 %collective-permute-start.10 = (f32[3,8,512]{2,1,0:T(8,128)S(1)}, f32[3,8,512]{2,1,0:T(8,128)S(1)}, u32[]{:S(2)}, u32[]{:S(2)}) collective-permute-start(f32[3,8,512]{2,1,0:T(8,128)S(1)} %get-tuple-element.88), channel_id=1, source_target_pairs={{0,28},{4,0},{8,4},{12,8},{16,12},{20,16},{24,20},{28,24},{1,29},{... | collective-permute-start | bytes 147464 | tf_op jit(solution)/shard_map/ppermute | solution.py:48
  41.8 6.7 %collective-permute-start.13 = (f32[3,8,512]{2,1,0:T(8,128)S(1)}, f32[3,8,512]{2,1,0:T(8,128)S(1)}, u32[]{:S(2)}, u32[]{:S(2)}) collective-permute-start(f32[3,8,512]{2,1,0:T(8,128)S(1)} %fusion.1.push), channel_id=1, source_target_pairs={{0,28},{4,0},{8,4},{12,8},{16,12},{20,16},{24,20},{28,24},{1,29},{... | collective-permute-start | bytes 147464 | tf_op jit(solution)/shard_map/ppermute | solution.py:48
  46.8 6.8 %collective-permute-start.12 = (f32[3,8,512]{2,1,0:T(8,128)S(1)}, f32[3,8,512]{2,1,0:T(8,128)S(1)}, u32[]{:S(2)}, u32[]{:S(2)}) collective-permute-start(f32[3,8,512]{2,1,0:T(8,128)S(1)} %fusion.1.push), channel_id=1, source_target_pairs={{0,4},{4,8},{8,12},{12,16},{16,20},{20,24},{24,28},{28,0},{1,5},{5... | collective-permute-start | bytes 147464 | tf_op jit(solution)/shard_map/ppermute | solution.py:48
  53.6 5.4 %collective-permute-start.14 = (f32[3,24,512]{2,1,0:T(8,128)S(1)}, f32[3,24,512]{2,1,0:T(8,128)S(1)}, u32[]{:S(2)}, u32[]{:S(2)}) collective-permute-start(f32[3,24,512]{2,1,0:T(8,128)S(1)} %pad_maximum_fusion.push), channel_id=1, source_target_pairs={{0,1},{1,2},{2,3},{3,0},{4,5},{5,6},{6,7},{7,4},{8,9},{9,10},{10,1... | collective-permute-start | bytes 442376 | tf_op jit(solution)/shard_map/ppermute | solution.py:48
  53.6 5.4 %collective-permute-start.15 = (f32[3,24,512]{2,1,0:T(8,128)S(1)}, f32[3,24,512]{2,1,0:T(8,128)S(1)}, u32[]{:S(2)}, u32[]{:S(2)}) collective-permute-start(f32[3,24,512]{2,1,0:T(8,128)S(1)} %pad_maximum_fusion.push), channel_id=1, source_target_pairs={{0,3},{1,0},{2,1},{3,2},{4,7},{5,4},{6,5},{7,6},{8,11},{9,8},{10,9... | collective-permute-start | bytes 442376 | tf_op jit(solution)/shard_map/ppermute | solution.py:48
  59.0 19.6 %copy-start.3 = (bf16[256,128]{1,0:T(8,128)(2,1)S(1)}, bf16[256,128]{1,0:T(8,128)(2,1)}, u32[]{:S(2)}) copy-start(bf16[256,128]{1,0:T(8,128)(2,1)} %constant.8.clone.table_high) | copy-start | bytes 196612
  59.0 19.6 %copy-start.4 = (bf16[256,128]{1,0:T(8,128)(2,1)S(1)}, bf16[256,128]{1,0:T(8,128)(2,1)}, u32[]{:S(2)}) copy-start(bf16[256,128]{1,0:T(8,128)(2,1)} %constant.9.clone.table_low) | copy-start | bytes 196612
  59.0 34.5 %copy-start.1 = (bf16[256,256]{1,0:T(8,128)(2,1)S(1)}, bf16[256,256]{1,0:T(8,128)(2,1)}, u32[]{:S(2)}) copy-start(bf16[256,256]{1,0:T(8,128)(2,1)} %constant.10.clone.table_high) | copy-start | bytes 393220
  59.0 34.5 %copy-start.2 = (bf16[256,256]{1,0:T(8,128)(2,1)S(1)}, bf16[256,256]{1,0:T(8,128)(2,1)}, u32[]{:S(2)}) copy-start(bf16[256,256]{1,0:T(8,128)(2,1)} %constant.11.clone.table_low) | copy-start | bytes 393220
  65.5 7.8 %collective-permute-start.16 = (f32[32,128]{1,0:T(8,128)S(1)}, f32[32,128]{1,0:T(8,128)S(1)}, u32[]{:S(2)}, u32[]{:S(2)}) collective-permute-start(f32[32,128]{1,0:T(8,128)S(1)} %get-tuple-element.72), channel_id=1, source_target_pairs={{0,4},{4,8},{8,12},{12,16},{16,20},{20,24},{24,28},{28,0},{1,5},{5... | collective-permute-start | bytes 49160 | tf_op jit(solution)/shard_map/ppermute | solution.py:48
  65.5 7.8 %collective-permute-start.17 = (f32[32,128]{1,0:T(8,128)S(1)}, f32[32,128]{1,0:T(8,128)S(1)}, u32[]{:S(2)}, u32[]{:S(2)}) collective-permute-start(f32[32,128]{1,0:T(8,128)S(1)} %get-tuple-element.73), channel_id=1, source_target_pairs={{0,28},{4,0},{8,4},{12,8},{16,12},{20,16},{24,20},{28,24},{1,29},{... | collective-permute-start | bytes 49160 | tf_op jit(solution)/shard_map/ppermute | solution.py:48
  70.2 3.1 %collective-permute-start.18 = (f32[16,128]{1,0:T(8,128)S(1)}, f32[16,128]{1,0:T(8,128)S(1)}, u32[]{:S(2)}, u32[]{:S(2)}) collective-permute-start(f32[16,128]{1,0:T(8,128)S(1)} %get-tuple-element.74), channel_id=1, source_target_pairs={{0,1},{1,2},{2,3},{3,0},{4,5},{5,6},{6,7},{7,4},{8,9},{9,10},{10,1... | collective-permute-start | bytes 24584 | tf_op jit(solution)/shard_map/ppermute | solution.py:48
  70.2 3.1 %collective-permute-start.19 = (f32[16,128]{1,0:T(8,128)S(1)}, f32[16,128]{1,0:T(8,128)S(1)}, u32[]{:S(2)}, u32[]{:S(2)}) collective-permute-start(f32[16,128]{1,0:T(8,128)S(1)} %get-tuple-element.75), channel_id=1, source_target_pairs={{0,3},{1,0},{2,1},{3,2},{4,7},{5,4},{6,5},{7,6},{8,11},{9,8},{10,9... | collective-permute-start | bytes 24584 | tf_op jit(solution)/shard_map/ppermute | solution.py:48
  73.5 3.8 %collective-permute-start.20 = (f32[32,512]{1,0:T(8,128)S(1)}, f32[32,512]{1,0:T(8,128)S(1)}, u32[]{:S(2)}, u32[]{:S(2)}) collective-permute-start(f32[32,512]{1,0:T(8,128)S(1)} %get-tuple-element.77), channel_id=1, source_target_pairs={{0,1},{1,2},{2,3},{3,0},{4,5},{5,6},{6,7},{7,4},{8,9},{9,10},{10,1... | collective-permute-start | bytes 196616 | tf_op jit(solution)/shard_map/ppermute | solution.py:48
  73.6 5.0 %collective-permute-start.21 = (f32[32,512]{1,0:T(8,128)S(1)}, f32[32,512]{1,0:T(8,128)S(1)}, u32[]{:S(2)}, u32[]{:S(2)}) collective-permute-start(f32[32,512]{1,0:T(8,128)S(1)} %get-tuple-element.78), channel_id=1, source_target_pairs={{0,2},{1,3},{2,0},{3,1},{4,6},{5,7},{6,4},{7,5},{8,10},{9,11},{10,... | collective-permute-start | bytes 196616 | tf_op jit(solution)/shard_map/ppermute | solution.py:48
  75.7 2.9 %collective-permute-start.22 = (f32[32,512]{1,0:T(8,128)S(1)}, f32[32,512]{1,0:T(8,128)S(1)}, u32[]{:S(2)}, u32[]{:S(2)}) collective-permute-start(f32[32,512]{1,0:T(8,128)S(1)} %get-tuple-element.79), channel_id=1, source_target_pairs={{0,3},{1,0},{2,1},{3,2},{4,7},{5,4},{6,5},{7,6},{8,11},{9,8},{10,9... | collective-permute-start | bytes 196616 | tf_op jit(solution)/shard_map/ppermute | solution.py:48
  79.3 8.3 %collective-permute-start.23 = (f32[32,512]{1,0:T(8,128)S(1)}, f32[32,512]{1,0:T(8,128)S(1)}, u32[]{:S(2)}, u32[]{:S(2)}) collective-permute-start(f32[32,512]{1,0:T(8,128)S(1)} %get-tuple-element.81), channel_id=1, source_target_pairs={{0,4},{4,8},{8,12},{12,16},{16,20},{20,24},{24,28},{28,0},{1,5},{5... | collective-permute-start | bytes 196616 | tf_op jit(solution)/shard_map/ppermute | solution.py:48
  79.3 8.3 %collective-permute-start.24 = (f32[32,512]{1,0:T(8,128)S(1)}, f32[32,512]{1,0:T(8,128)S(1)}, u32[]{:S(2)}, u32[]{:S(2)}) collective-permute-start(f32[32,512]{1,0:T(8,128)S(1)} %get-tuple-element.82), channel_id=1, source_target_pairs={{0,8},{4,12},{8,16},{12,20},{16,24},{20,28},{24,0},{28,4},{1,9},{5... | collective-permute-start | bytes 196616 | tf_op jit(solution)/shard_map/ppermute | solution.py:48
  79.4 12.9 %collective-permute-start.25 = (f32[32,512]{1,0:T(8,128)S(1)}, f32[32,512]{1,0:T(8,128)S(1)}, u32[]{:S(2)}, u32[]{:S(2)}) collective-permute-start(f32[32,512]{1,0:T(8,128)S(1)} %get-tuple-element.83), channel_id=1, source_target_pairs={{0,12},{4,16},{8,20},{12,24},{16,28},{20,0},{24,4},{28,8},{1,13},{... | collective-permute-start | bytes 196616 | tf_op jit(solution)/shard_map/ppermute | solution.py:48
  80.5 11.8 %collective-permute-start.26 = (f32[32,512]{1,0:T(8,128)S(1)}, f32[32,512]{1,0:T(8,128)S(1)}, u32[]{:S(2)}, u32[]{:S(2)}) collective-permute-start(f32[32,512]{1,0:T(8,128)S(1)} %get-tuple-element.84), channel_id=1, source_target_pairs={{0,16},{4,20},{8,24},{12,28},{16,0},{20,4},{24,8},{28,12},{1,17},{... | collective-permute-start | bytes 196616 | tf_op jit(solution)/shard_map/ppermute | solution.py:48
  84.6 7.7 %collective-permute-start.27 = (f32[32,512]{1,0:T(8,128)S(1)}, f32[32,512]{1,0:T(8,128)S(1)}, u32[]{:S(2)}, u32[]{:S(2)}) collective-permute-start(f32[32,512]{1,0:T(8,128)S(1)} %get-tuple-element.85), channel_id=1, source_target_pairs={{0,20},{4,24},{8,28},{12,0},{16,4},{20,8},{24,12},{28,16},{1,21},{... | collective-permute-start | bytes 196616 | tf_op jit(solution)/shard_map/ppermute | solution.py:48
  87.6 5.9 %collective-permute-start.28 = (f32[32,512]{1,0:T(8,128)S(1)}, f32[32,512]{1,0:T(8,128)S(1)}, u32[]{:S(2)}, u32[]{:S(2)}) collective-permute-start(f32[32,512]{1,0:T(8,128)S(1)} %get-tuple-element.86), channel_id=1, source_target_pairs={{0,24},{4,28},{8,0},{12,4},{16,8},{20,12},{24,16},{28,20},{1,25},{... | collective-permute-start | bytes 196616 | tf_op jit(solution)/shard_map/ppermute | solution.py:48
  87.6 5.9 %collective-permute-start.29 = (f32[32,512]{1,0:T(8,128)S(1)}, f32[32,512]{1,0:T(8,128)S(1)}, u32[]{:S(2)}, u32[]{:S(2)}) collective-permute-start(f32[32,512]{1,0:T(8,128)S(1)} %get-tuple-element.87), channel_id=1, source_target_pairs={{0,28},{4,0},{8,4},{12,8},{16,12},{20,16},{24,20},{28,24},{1,29},{... | collective-permute-start | bytes 196616 | tf_op jit(solution)/shard_map/ppermute | solution.py:48
where the time goes:
time: 95.4 us; the launch traced here: 95.1 us
  starting transfers between devices  45.6 us (48%)
  Pallas kernels  25.1 us (26%)
  waiting for transfers between devices  21.4 us (22%)
  local copies, waits for them, and re-layouts  2.05 us (2%)
    ppermute x30, starting transfers between devices, shift(): lax.ppermute(array, axis, [(i, (i + step) % devices) for i in range(devic...  45.6 us
    pallas_call x13, Pallas kernels, call(): pl.pallas_call(kernel, out_shape=out_shape, in_specs=[IN_SMEM] * len(scal...  23 us
    ppermute x30, waiting for transfers between devices, shift(): lax.ppermute(array, axis, [(i, (i + step) % devices) for i in range(devic...  21.4 us
    unnamed x16, local copies, waits for them, and re-layouts  2.05 us
    pallas_call x1, Pallas kernels, pack(): pl.pallas_call(functools.partial(pack_kernel, layout), out_shape=[float32...  2.04 us
  transfers between devices with their start and end apart: 30, of which 15 were waited for; matrix products, arithmetic and copies ran while one was open for 0% of the time, Pallas kernels for 9%

commit v1 on v0

--- a/solution.py
+++ b/solution.py
@@ -43,9 +43,22 @@
     )(*scalars, *arrays)
 
 
-def shift(array, axis, step):
+def swap(array, axis, partner):
     devices = lax.axis_size(axis)
-    return lax.ppermute(array, axis, [(i, (i + step) % devices) for i in range(devices)])
+    pairs = [(i, (i + (1 if i % 2 == partner else -1)) % devices) for i in range(devices)]
+    return lax.ppermute(array, axis, pairs)
+
+
+def even(axis):
+    return lax.rem(lax.axis_index(axis), 2) == 0
+
+
+def in_order(axis, shape):
+    parity = jnp.full(shape, lax.rem(lax.axis_index(axis), 2), jnp.int32)
+    return lambda one, two: (
+        jnp.where(parity == 0, two, one),
+        jnp.where(parity == 0, one, two),
+    )
 
 
 def cosine_coefficients():
@@ -115,7 +128,7 @@
     return jnp.concatenate(rows, axis=1)
 
 
-def slot_visits(layout, facts, marks, saved, blocks, step_z, high, low, visit, skip):
+def slot_visits(layout, facts, marks, saved, blocks, step, high, low, visit, skip):
     size_x, size_z, size_y = layout.sizes
     half_x, half_z = size_x // 2, size_z // 2
     slots = layout.slots
@@ -123,9 +136,9 @@
     def body(index, carry):
         block, slot = index // slots, index % slots
         block = blocks[0] + block * (blocks[1] - blocks[0] if len(blocks) > 1 else 0)
-        fact = (step_z + 1) * 3 * slots + block * slots + slot
-        first_x = facts[0, fact] + (block - 1) * size_x
-        first_z = facts[1, fact] + step_z * size_z
+        fact = (step * 3 + block) * slots + slot
+        first_x = facts[0, fact]
+        first_z = facts[1, fact]
         first_y = facts[2, fact]
         meets_x = (first_x > -BOX) & (first_x < size_x)
         meets_z = (first_z > -BOX) & (first_z < size_z)
@@ -196,7 +209,7 @@
 
 
 def sample_slots(
-    layout, facts, marks, motion, field_high, field_low, out, saved, blocks, step_z, high, low
+    layout, facts, marks, motion, field_high, field_low, out, saved, blocks, step, high, low
 ):
     def visit(index, row, first, weight_y, pieces):
         rows = pl.ds(first, WINDOW)
@@ -226,7 +239,7 @@
         for c in range(3):
             out[c, pl.ds(index, 1), :] = jnp.zeros((1, layout.markers), jnp.float32)
 
-    slot_visits(layout, facts, marks, saved, blocks, step_z, high, low, visit, skip)
+    slot_visits(layout, facts, marks, saved, blocks, step, high, low, visit, skip)
 
 
 def sample_kernel(layout, groups, moved, facts, *refs):
@@ -236,7 +249,7 @@
     motion, refs = refs[:moved], refs[moved:]
     outs, refs = refs[:count], refs[count:]
     saved, (high, low) = refs[:count], refs[count:]
-    for i, (blocks, step_z) in enumerate(groups):
+    for i, (blocks, step) in enumerate(groups):
         sample_slots(
             layout,
             facts,
@@ -247,7 +260,7 @@
             outs[i],
             saved[i],
             blocks,
-            step_z,
+            step,
             high,
             low,
         )
@@ -277,7 +290,7 @@
     return results[: len(groups)], results[len(groups) :]
 
 
-def spread_slots(layout, blocks, step_z, facts, saved, push, own_rows, total, high, low):
+def spread_slots(layout, blocks, step, facts, saved, push, own_rows, total, high, low):
     def visit(index, row, first, weight_y, pieces):
         slot = index if own_rows else row
         count = sum(width for _, width in pieces)
@@ -300,12 +313,12 @@
                 total[c, pl.ds(first, WINDOW), pl.ds(lane, width)] += part
             column += width
 
-    slot_visits(layout, facts, None, saved, blocks, step_z, high, low, visit, None)
+    slot_visits(layout, facts, None, saved, blocks, step, high, low, visit, None)
 
 
 def spread_own_kernel(layout, facts, saved, push, total, high, low):
     total[...] = jnp.zeros(total.shape, jnp.float32)
-    spread_slots(layout, (1,), 0, facts, saved, push, True, total, high, low)
+    spread_slots(layout, (1,), 1, facts, saved, push, True, total, high, low)
 
 
 def spread_own(layout, facts, saved, push):
@@ -322,7 +335,7 @@
 
 def spread_side_kernel(layout, facts, saved, push, before, total, high, low):
     total[...] = before[...]
-    spread_slots(layout, (0, 2), 0, facts, saved, push, False, total, high, low)
+    spread_slots(layout, (0, 2), 1, facts, saved, push, False, total, high, low)
 
 
 def spread_side(layout, facts, saved, push, before):
@@ -340,17 +353,17 @@
 def spread_rest_kernel(
     layout,
     facts,
-    lower_saved,
-    upper_saved,
-    lower_push,
-    upper_push,
+    saved_0,
+    saved_1,
+    push_0,
+    push_1,
     before,
     predicted,
     velocity,
-    u_first,
-    u_last,
-    w_first,
-    w_last,
+    u_0,
+    u_1,
+    w_0,
+    w_1,
     inner,
     total,
     high,
@@ -359,18 +372,20 @@
     size_x, size_z, size_y = layout.sizes
     total[...] = before[...]
     row = (0, 1, 2)
-    spread_slots(layout, row, -1, facts, lower_saved, lower_push, False, total, high, low)
-    spread_slots(layout, row, 1, facts, upper_saved, upper_push, False, total, high, low)
+    spread_slots(layout, row, 0, facts, saved_0, push_0, False, total, high, low)
+    spread_slots(layout, row, 2, facts, saved_1, push_1, False, total, high, low)
     for c in range(3):
         for q, (xs, zs) in enumerate(quarters(layout.sizes)):
             part = jnp.transpose(total[c, :, q * LANES : (q + 1) * LANES])
             part = part.reshape(size_x // 2, size_z // 2, size_y)
             velocity[c, xs, zs] = predicted[c, xs, zs] + part
-    u_first[...] = velocity[0, 0]
-    u_last[...] = velocity[0, size_x - 1]
+    last = jnp.where(even("gx"), size_x - 1, 0)
+    u_0[...] = velocity[0, last]
+    u_1[...] = velocity[0, size_x - 1 - last]
+    choose = in_order("gz", (1, size_y))
     for x in range(size_x):
-        w_first[x : x + 1] = velocity[2, x, 0:1]
-        w_last[x : x + 1] = velocity[2, x, size_z - 1 : size_z]
+        first, last = velocity[2, x, 0:1], velocity[2, x, size_z - 1 : size_z]
+        w_0[x : x + 1], w_1[x : x + 1] = choose(first, last)
     row = lax.broadcasted_iota(jnp.int32, (size_z, size_y), 0)
     lane = lax.broadcasted_iota(jnp.int32, (size_z, size_y), 1)
     for x in range(size_x):
@@ -408,10 +423,10 @@
     cells_hbm,
     fraction_hbm,
     own,
-    x_last,
-    x_first,
-    z_last,
-    z_first,
+    x_0,
+    x_1,
+    z_0,
+    z_1,
     slot_ids,
     corners,
     cells,
@@ -419,7 +434,7 @@
     edges,
     done,
 ):
-    size_x, size_z, _ = layout.sizes
+    size_x, size_z, size_y = layout.sizes
     slots = layout.slots
     moves = [
         (slot_ids_hbm, slot_ids),
@@ -430,10 +445,11 @@
     for c in range(4):
         moves.append((flow.at[c, :, pl.ds(size_z - 8, 8)], edges.at[0, c]))
         moves.append((flow.at[c, :, pl.ds(0, 8)], edges.at[1, c]))
+    last = jnp.where(even("gx"), size_x - 1, 0)
     for c in range(4):
         rows = pl.ds(c * size_z, size_z)
-        moves.append((flow.at[c, size_x - 1], x_last.at[rows]))
-        moves.append((flow.at[c, 0], x_first.at[rows]))
+        moves.append((flow.at[c, last], x_0.at[rows]))
+        moves.append((flow.at[c, size_x - 1 - last], x_1.at[rows]))
     copies = [pltpu.make_async_copy(a, b, done.at[i]) for i, (a, b) in enumerate(moves)]
     for copy in copies:
         copy.start()
@@ -443,7 +459,7 @@
     length_z = size_z * lax.axis_size("gz")
     offset_x = length_x + HALF - lax.axis_index("gx") * size_x
     offset_z = length_z + HALF - lax.axis_index("gz") * size_z
-    targets = ((own, 0), (z_last, layout.ghost_z), (z_first, layout.ghost_z))
+    targets = ((own, 0), (z_0, layout.ghost_z), (z_1, layout.ghost_z))
     for a, direction in enumerate((0, 2, 1)):
         for t in range(layout.tiles):
             lanes = slice(t * LANES, (t + 1) * LANES)
@@ -463,11 +479,13 @@
             target[row : row + 1] = fact.astype(jnp.float32)
     for copy in copies[4:]:
         copy.wait()
+    choose = in_order("gz", (1, size_y))
     for c in range(4):
         for x in range(size_x):
             row = c * size_x + x
-            z_last[row : row + 1] = edges[0, c, x, 7:8]
-            z_first[row : row + 1] = edges[1, c, x, 0:1]
+            z_0[row : row + 1], z_1[row : row + 1] = choose(
+                edges[1, c, x, 0:1], edges[0, c, x, 7:8]
+            )
 
 
 def pack(layout, slot_ids, corners, flow, cells, fraction):
@@ -513,22 +531,32 @@
     )
 
 
-def collect_kernel(layout, own, left, right, below, above, corners_below, corners_above, *refs):
+def collect_kernel(layout, own, side_0, side_1, one, two, corners_0, corners_1, *refs):
     rows, (facts, table) = refs[:3], refs[3:]
-    count = layout.rows
+    count, slots = layout.rows, layout.slots
+    size_x, size_z, _ = layout.sizes
     for row, middle, base, sides in (
-        (rows[0], below, layout.ghost_z, corners_below),
+        (rows[0], one, layout.ghost_z, corners_0),
         (rows[1], own, 0, None),
-        (rows[2], above, layout.ghost_z, corners_above),
+        (rows[2], two, layout.ghost_z, corners_1),
     ):
-        row[:count] = left[...] if sides is None else sides[:count]
+        row[:count] = side_0[...] if sides is None else sides[:count]
         row[count : 2 * count] = middle[base : base + count]
-        row[2 * count :] = right[...] if sides is None else sides[count:]
+        row[2 * count :] = side_1[...] if sides is None else sides[count:]
     for block in range(9):
         first = (block % 3) * count + layout.fact_row
-        out = slice(block * layout.slots, (block + 1) * layout.slots)
-        table[out] = rows[block // 3][first : first + layout.slots]
-    facts[...] = jnp.transpose(table[...])[:8].astype(jnp.int32)
+        out = slice(block * slots, (block + 1) * slots)
+        table[out] = rows[block // 3][first : first + slots]
+    kind = lax.broadcasted_iota(jnp.int32, (8, LANES), 0)
+    slot = lax.broadcasted_iota(jnp.int32, (8, LANES), 1)
+    last = 2 * 3 * slots
+    move_x = jnp.where(even("gx"), size_x, -size_x)
+    move_z = jnp.where(even("gz"), size_z, -size_z)
+    place = slot - jnp.where(slot >= last, last, jnp.where(slot >= 3 * slots, 3 * slots, 0))
+    moved_x = jnp.where(place < slots, move_x, jnp.where(place >= 2 * slots, -move_x, 0))
+    moved_z = jnp.where(slot < 3 * slots, move_z, jnp.where(slot >= last, -move_z, 0))
+    moved = jnp.where(kind == 0, moved_x, jnp.where(kind == 1, moved_z, 0))
+    facts[...] = jnp.transpose(table[...])[:8].astype(jnp.int32) + moved
 
 
 def collect(layout, *tiles):
@@ -615,16 +643,20 @@
     u_last,
     w_first,
     w_last,
-    left,
-    right,
-    lower,
-    upper,
+    x_0,
+    x_1,
+    z_0,
+    z_1,
     predicted,
     field_high,
     field_low,
 ):
     size_x, size_z, size_y = layout.sizes
     row = lax.broadcasted_iota(jnp.int32, (8, size_y), 0)
+    lower, upper = in_order("gz", z_0[: layout.ghost_z].shape)(
+        z_0[: layout.ghost_z], z_1[: layout.ghost_z]
+    )
+    left, right = in_order("gx", x_0.shape)(x_0[...], x_1[...])
     for x in range(size_x):
         carried_low = w_first[x : x + 1]
         carried_high = w_last[x : x + 1]
@@ -657,32 +689,34 @@
             field_low[c, :, q * LANES : (q + 1) * LANES] = part - high
 
 
-def predict_outer(layout, inner, left, right, lower, upper):
+def predict_outer(layout, inner, *layers):
     _, _, size_y = layout.sizes
     return call(
         functools.partial(predict_outer_kernel, layout),
         [float32(3, *layout.sizes)] + [float32(3, size_y, layout.plane)] * 2,
         [],
-        [*inner, left, right, lower, upper],
+        [*inner, *layers],
         [],
         10 * inner[0].size,
         16 * inner[0].size,
     )
 
 
-def divergence_kernel(sizes, parts, inner, u_below, u_above, w_below, w_above, *rest):
+def divergence_kernel(sizes, parts, inner, u_0, u_1, w_0, w_1, *rest):
     outs, whole = rest[:parts], rest[parts]
     size_x, size_z, size_y = sizes
     row = lax.broadcasted_iota(jnp.int32, (size_z, size_y), 0)
     group = LANES // size_z
+    u_below, u_above = in_order("gx", u_0.shape)(u_0[...], u_1[...])
+    w_below, w_above = in_order("gz", w_0.shape)(w_0[...], w_1[...])
     for q in range(size_x // group):
         pieces = []
         for x in range(q * group, (q + 1) * group):
             piece = inner[x]
             if x == 0:
-                piece -= 0.5 * u_below[...]
+                piece -= 0.5 * u_below
             if x == size_x - 1:
-                piece += 0.5 * u_above[...]
+                piece += 0.5 * u_above
             piece -= jnp.where(row == 0, 0.5 * w_below[x : x + 1], 0.0)
             piece += jnp.where(row == size_z - 1, 0.5 * w_above[x : x + 1], 0.0)
             pieces.append(piece)
@@ -690,7 +724,7 @@
         whole[:, q * LANES : (q + 1) * LANES] = jnp.transpose(part)
     height = size_y // parts
     for step in range(parts):
-        first = pl.multiple_of(lax.rem(lax.axis_index("gz") + step, parts) * height, 8)
+        first = pl.multiple_of((lax.axis_index("gz") ^ step) * height, 8)
         outs[step][...] = whole[pl.ds(first, height), :]
 
 
@@ -733,7 +767,7 @@
     height = size_y // parts_z
     group = LANES // size_z
     for step in range(parts_z):
-        gathered[lax.rem(lax.axis_index("gz") + parts_z - step, parts_z)] = pieces[step][...]
+        gathered[lax.axis_index("gz") ^ step] = pieces[step][...]
     for block in range(parts_z // group):
         for q in range(size_x // group):
             lanes = slice(q * LANES, (q + 1) * LANES)
@@ -754,7 +788,7 @@
     whole[...] = result
     rows = whole.shape[0] // parts_x
     for step in range(parts_x):
-        first = pl.multiple_of(lax.rem(lax.axis_index("gx") + step, parts_x) * rows, 8)
+        first = pl.multiple_of((lax.axis_index("gx") ^ step) * rows, 8)
         outs[step][...] = whole[pl.ds(first, rows), :]
 
 
@@ -788,7 +822,7 @@
     height = size_y // parts_z
     group = LANES // size_x
     for step in range(parts_x):
-        gathered[lax.rem(lax.axis_index("gx") + parts_x - step, parts_x)] = pieces[step][...]
+        gathered[lax.axis_index("gx") ^ step] = pieces[step][...]
     for block in range(parts_x // group):
         for q in range(height // group):
             lanes = slice(q * LANES, (q + 1) * LANES)
@@ -853,7 +887,12 @@
 
 
 def exchange(pieces, axis):
-    return [pieces[0]] + [shift(pieces[d], axis, d) for d in range(1, len(pieces))]
+    devices = lax.axis_size(axis)
+    assert devices & (devices - 1) == 0
+    return [pieces[0]] + [
+        lax.ppermute(pieces[d], axis, [(i, i ^ d) for i in range(devices)])
+        for d in range(1, devices)
+    ]
 
 
 def on_device(
@@ -866,52 +905,40 @@
     slots, markers = marker_cells.shape[1:]
     layout = Layout(sizes, slots, markers)
 
-    own, x_last, x_first, z_last, z_first = pack(
+    own, x_0, x_1, z_0, z_1 = pack(
         layout, slot_ids, corners, flow_state, marker_cells, marker_frac
     )
-    left = shift(own, "gx", 1)
-    right = shift(own, "gx", -1)
-    below, above = shift(z_last, "gz", 1), shift(z_first, "gz", -1)
-    x_below, x_above = shift(x_last, "gx", 1), shift(x_first, "gx", -1)
+    marks_0 = swap(own, "gx", 0)
+    marks_1 = swap(own, "gx", 1)
+    z_0, z_1 = swap(z_0, "gz", 0), swap(z_1, "gz", 1)
+    x_0, x_1 = swap(x_0, "gx", 0), swap(x_1, "gx", 1)
     inner = predict_inner(sizes, flow_state)
-    sides = join(left, right)
-    corners_below, corners_above = shift(sides, "gz", 1), shift(sides, "gz", -1)
-    predicted, *fields = predict_outer(layout, inner, x_below, x_above, below, above)
-    lower, row, upper, facts = collect(
-        layout, own, left, right, below, above, corners_below, corners_above
+    sides = join(marks_0, marks_1)
+    corners_0, corners_1 = swap(sides, "gz", 0), swap(sides, "gz", 1)
+    predicted, *fields = predict_outer(layout, inner, x_0, x_1, z_0, z_1)
+    row_0, row, row_1, facts = collect(
+        layout, own, marks_0, marks_1, z_0, z_1, corners_0, corners_1
     )
 
     tiles = (0, 1, 2)
-    parts, (lower_saved, upper_saved) = sample(
-        layout, ((tiles, -1), (tiles, 1)), facts, (lower, upper), fields, ()
-    )
-    from_upper = shift(parts[0], "gz", -1)
-    from_lower = shift(parts[1], "gz", 1)
-    (side_part,), (side_saved,) = sample(layout, (((0, 2), 0),), facts, (row,), fields, ())
-    from_z = from_upper + from_lower
-    from_right = shift(side_part[:, :slots] + from_z[:, :slots], "gx", -1)
-    from_left = shift(side_part[:, slots:] + from_z[:, 2 * slots :], "gx", 1)
+    parts, rows_saved = sample(layout, ((tiles, 0), (tiles, 2)), facts, (row_0, row_1), fields, ())
+    from_z = swap(parts[0], "gz", 0) + swap(parts[1], "gz", 1)
+    (side_part,), (side_saved,) = sample(layout, (((0, 2), 1),), facts, (row,), fields, ())
+    from_0 = swap(side_part[:, :slots] + from_z[:, :slots], "gx", 0)
+    from_1 = swap(side_part[:, slots:] + from_z[:, 2 * slots :], "gx", 1)
     motion = (particle_velocity, particle_spin)
-    (own_part,), (own_saved,) = sample(layout, (((1,), 0),), facts, (row,), fields, motion)
-    push = own_part - (from_z[:, slots : 2 * slots] + from_right + from_left)
-
-    left_push = shift(push, "gx", 1)
-    right_push = shift(push, "gx", -1)
-    row_push = jnp.concatenate([left_push, push, right_push], axis=1)
-    lower_push = shift(row_push, "gz", 1)
-    upper_push = shift(row_push, "gz", -1)
+    (own_part,), (own_saved,) = sample(layout, (((1,), 1),), facts, (row,), fields, motion)
+    push = own_part - (from_z[:, slots : 2 * slots] + from_0 + from_1)
+
+    row_push = jnp.concatenate([swap(push, "gx", 0), push, swap(push, "gx", 1)], axis=1)
+    rows_push = swap(row_push, "gz", 0), swap(row_push, "gz", 1)
     forcing = spread_own(layout, facts, own_saved, push)
     forcing = spread_side(layout, facts, side_saved, row_push, forcing)
-    velocity, u_first, u_last, w_first, w_last, change = spread_rest(
-        layout, facts, (lower_saved, upper_saved), (lower_push, upper_push), forcing, predicted
-    )
-
-    ghosts = (
-        shift(u_last, "gx", 1),
-        shift(u_first, "gx", -1),
-        shift(w_last, "gz", 1),
-        shift(w_first, "gz", -1),
-    )
+    velocity, u_0, u_1, w_0, w_1, change = spread_rest(
+        layout, facts, rows_saved, rows_push, forcing, predicted
+    )
+
+    ghosts = (swap(u_0, "gx", 0), swap(u_1, "gx", 1), swap(w_0, "gz", 0), swap(w_1, "gz", 1))
     pieces = divergence(sizes, counts[1], change, ghosts)
     pieces = exchange(pieces, "gz")
     pieces = transform_z(sizes, counts, table_z(length_z, counts[0]), pieces)

time: 95.4 us -> 95.3 us (level)
  starting transfers between devices: 45.6 us -> 38.4 us
  waiting for transfers between devices: 21.4 us -> 28.6 us
    ppermute x30, starting transfers between devices: 45.6 us -> 38.4 us  [the longest x20 25.2 us: swap(): return lax.ppermute(array, axis, pairs)]
    ppermute x30, waiting for transfers between devices: 21.4 us -> 28.6 us  [the longest x20 19.5 us: swap(): return lax.ppermute(array, axis, pairs)]
  transfers between devices with their start and end apart: 30 -> 30, of which waited for: 15 -> 14; matrix products, arithmetic and copies ran while one was open for 0% -> 0% of each run, Pallas kernels for 9% -> 9%
where the time goes in v1:
time: 95.3 us; the launch traced here: 95.1 us
  starting transfers between devices  38.4 us (40%)
  waiting for transfers between devices  28.6 us (30%)
  Pallas kernels  25.1 us (26%)
  local copies, waits for them, and re-layouts  2.05 us (2%)
    ppermute x20, starting transfers between devices, swap(): return lax.ppermute(array, axis, pairs)  25.2 us
    pallas_call x13, Pallas kernels, call(): pl.pallas_call(kernel, out_shape=out_shape, in_specs=[IN_SMEM] * len(scal...  23 us
    ppermute x20, waiting for transfers between devices, swap(): return lax.ppermute(array, axis, pairs)  19.5 us
    ppermute x10, starting transfers between devices, exchange(): lax.ppermute(pieces[d], axis, [(i, i ^ d) for i in range(devices)])  13.2 us
    ppermute x10, waiting for transfers between devices, exchange(): lax.ppermute(pieces[d], axis, [(i, i ^ d) for i in range(devices)])  9.12 us
    pallas_call x1, Pallas kernels, pack(): pl.pallas_call(functools.partial(pack_kernel, layout), out_shape=[float32...  2.06 us
    unnamed x16, local copies, waits for them, and re-layouts  2.05 us
  transfers between devices with their start and end apart: 30, of which 14 were waited for; matrix products, arithmetic and copies ran while one was open for 0% of the time, Pallas kernels for 9%

profile of v1, /device:TPU:0, one launch (start us, length us, event | category | flops | bytes accessed | tf_op | source)
XLA Modules:
  0.0 95.1 jit_solution(17940238907212194429)
XLA Ops:
  0.6 2.1 %pack.1 = (f32[104,128]{1,0:T(8,128)}, f32[128,128]{1,0:T(8,128)}, f32[128,128]{1,0:T(8,128)}, f32[168,128]{1,0:T(8,128)}, f32[168,128]{1,0:T(8,128)}) custom-call(s32[8]{0:T(128)} %slot_ids_hbm.1, s32[3,8]{1,0:T(4,128)} %corners_hbm.1, f32[4,16,32,128]{3,2,1,0:T(8,128)} %flow.3, s32[3,8,512]{2,1,0:T(8,128)} %cells_hbm.1, f32[3,8,512]{2,1,0:T(8,128)} %fraction_hbm.1), custom_call_target="tpu_custom_call" | custom-call | flops 262144 | bytes 262144 | tf_op jit(solution)/shard_map/pack/pallas_call | solution.py:494
  2.7 3.1 %collective-permute-start = (f32[104,128]{1,0:T(8,128)}, f32[104,128]{1,0:T(8,128)S(1)}, u32[]{:S(2)}, u32[]{:S(2)}) collective-permute-start(f32[104,128]{1,0:T(8,128)} %get-tuple-element.45.own), channel_id=1, source_target_pairs={{0,4},{4,0},{8,12},{12,8},{16,20},{20,16},{24,28},{28,24},{1,5},{5... | collective-permute-start | bytes 159752 | tf_op jit(solution)/shard_map/ppermute | solution.py:49
  5.8 3.5 %collective-permute-start.1 = (f32[104,128]{1,0:T(8,128)}, f32[104,128]{1,0:T(8,128)S(1)}, u32[]{:S(2)}, u32[]{:S(2)}) collective-permute-start(f32[104,128]{1,0:T(8,128)} %get-tuple-element.45.own), channel_id=1, source_target_pairs={{0,28},{4,8},{8,4},{12,16},{16,12},{20,24},{24,20},{28,0},{1,29},{... | collective-permute-start | bytes 159752 | tf_op jit(solution)/shard_map/ppermute | solution.py:49
  9.3 3.5 %collective-permute-done.1.right.side_1 = f32[104,128]{1,0:T(8,128)S(1)} collective-permute-done((f32[104,128]{1,0:T(8,128)}, f32[104,128]{1,0:T(8,128)S(1)}, u32[]{:S(2)}, u32[]{:S(2)}) %collective-permute-start.1) | collective-permute-done | bytes 53280 | tf_op jit(solution)/shard_map/ppermute | solution.py:49
  12.9 1.6 %collective-permute-start.5 = (f32[208,128]{1,0:T(8,128)S(1)}, f32[208,128]{1,0:T(8,128)S(1)}, u32[]{:S(2)}, u32[]{:S(2)}) collective-permute-start(f32[208,128]{1,0:T(8,128)S(1)} %shard_map.122), channel_id=1, source_target_pairs={{0,3},{1,2},{2,1},{3,0},{4,7},{5,6},{6,5},{7,4},{8,11},{9,10},{10,... | collective-permute-start | bytes 319496 | tf_op jit(solution)/shard_map/ppermute | solution.py:49
  14.6 0.6 collective-permute-start.3
  15.1 3.5 %collective-permute-start.7 = (f32[128,128]{1,0:T(8,128)}, f32[128,128]{1,0:T(8,128)S(1)}, u32[]{:S(2)}, u32[]{:S(2)}) collective-permute-start(f32[128,128]{1,0:T(8,128)} %get-tuple-element.57), channel_id=1, source_target_pairs={{0,28},{4,8},{8,4},{12,16},{16,12},{20,24},{24,20},{28,0},{1,29},{... | collective-permute-start | bytes 196616 | tf_op jit(solution)/shard_map/ppermute | solution.py:49
  18.7 1.2 %copy-done = f32[4,16,32,128]{3,2,1,0:T(8,128)S(1)} copy-done((f32[4,16,32,128]{3,2,1,0:T(8,128)S(1)}, f32[4,16,32,128]{3,2,1,0:T(8,128)}, u32[]{:S(2)}) %copy-start) | copy-done | bytes 1048600
  19.9 0.9 shard_map.124
  20.8 1.5 %collective-permute-done.7.x_1 = f32[128,128]{1,0:T(8,128)S(1)} collective-permute-done((f32[128,128]{1,0:T(8,128)}, f32[128,128]{1,0:T(8,128)S(1)}, u32[]{:S(2)}, u32[]{:S(2)}) %collective-permute-start.7) | collective-permute-done | bytes 65568 | tf_op jit(solution)/shard_map/ppermute | solution.py:49
  22.3 0.3 shard_map.125
  22.7 0.8 copy-done.5
  23.5 0.1 shard_map.123
  23.6 5.3 %shard_map.126 = (f32[3,24,512]{2,1,0:T(8,128)S(1)}, f32[3,24,512]{2,1,0:T(8,128)S(1)}, f32[24,80,512]{2,1,0:T(8,128)S(1)}, f32[24,80,512]{2,1,0:T(8,128)S(1)}) custom-call(s32[8,128]{1,0:T(8,128)S(1)} %get-tuple-element.48.facts, f32[312,128]{1,0:T(8,128)S(1)} %get-tuple-element.49.refs_0_, f32[312,128]{1,0:T(8,128)S(1)} %get-tuple-element.50.refs_1_, ...), custom_call_target="tpu_custom_call" | custom-call | flops 7247757312 | bytes 1572864 | tf_op jit(solution)/shard_map/pallas_call | solution.py:35
  29.0 0.1 collective-permute-start.9
  29.1 2.8 %shard_map.128 = (f32[3,16,512]{2,1,0:T(8,128)S(1)}, f32[16,80,512]{2,1,0:T(8,128)S(1)}) custom-call(s32[8,128]{1,0:T(8,128)S(1)} %get-tuple-element.48.facts, f32[312,128]{1,0:T(8,128)S(1)} %get-tuple-element.62.refs_0_, f32[3,128,512]{2,1,0:T(8,128)S(1)} %get-tuple-element.58.refs_2_.refs_1_, f32[3,128,512]{2,1,0:T(8,128)S(1)} %get-tuple-element.59.refs_3_.refs_2_), custom_call_target="tpu_custom_call" | custom-call | flops 2415919104 | bytes 1572864 | tf_op jit(solution)/shard_map/pallas_call | solution.py:35
  31.9 2.6 %collective-permute-done.9 = f32[3,24,512]{2,1,0:T(8,128)S(1)} collective-permute-done((f32[3,24,512]{2,1,0:T(8,128)S(1)}, f32[3,24,512]{2,1,0:T(8,128)S(1)}, u32[]{:S(2)}, u32[]{:S(2)}) %collective-permute-start.9) | collective-permute-done | bytes 147488 | tf_op jit(solution)/shard_map/ppermute | solution.py:49
  34.6 3.8 %collective-permute-start.11 = (f32[3,8,512]{2,1,0:T(8,128)S(1)}, f32[3,8,512]{2,1,0:T(8,128)S(1)}, u32[]{:S(2)}, u32[]{:S(2)}) collective-permute-start(f32[3,8,512]{2,1,0:T(8,128)S(1)} %get-tuple-element.89), channel_id=1, source_target_pairs={{0,28},{4,8},{8,4},{12,16},{16,12},{20,24},{24,20},{28,0},{1,29},{... | collective-permute-start | bytes 147464 | tf_op jit(solution)/shard_map/ppermute | solution.py:49
  38.4 1.0 %shard_map.127 = (f32[3,8,512]{2,1,0:T(8,128)S(1)}, f32[8,80,512]{2,1,0:T(8,128)S(1)}) custom-call(s32[8,128]{1,0:T(8,128)S(1)} %get-tuple-element.48.facts, f32[312,128]{1,0:T(8,128)S(1)} %get-tuple-element.62.refs_0_, f32[3,128,512]{2,1,0:T(8,128)S(1)} %get-tuple-element.58.refs_2_.refs_1_, f32[3,128,512]{2,1,0:T(8,128)S(1)} %get-tuple-element.59.refs_3_.refs_2_, ...), custom_call_target="tpu_custom_call" | custom-call | flops 1207959552 | bytes 1572864 | tf_op jit(solution)/shard_map/pallas_call | solution.py:35
  39.3 2.6 %collective-permute-done.11 = f32[3,8,512]{2,1,0:T(8,128)S(1)} collective-permute-done((f32[3,8,512]{2,1,0:T(8,128)S(1)}, f32[3,8,512]{2,1,0:T(8,128)S(1)}, u32[]{:S(2)}, u32[]{:S(2)}) %collective-permute-start.11) | collective-permute-done | bytes 49184 | tf_op jit(solution)/shard_map/ppermute | solution.py:49
  41.9 0.6 collective-permute-done.10
  42.6 2.7 %collective-permute-start.13 = (f32[3,8,512]{2,1,0:T(8,128)S(1)}, f32[3,8,512]{2,1,0:T(8,128)S(1)}, u32[]{:S(2)}, u32[]{:S(2)}) collective-permute-start(f32[3,8,512]{2,1,0:T(8,128)S(1)} %fusion.1.push), channel_id=1, source_target_pairs={{0,28},{4,8},{8,4},{12,16},{16,12},{20,24},{24,20},{28,0},{1,29},{... | collective-permute-start | bytes 147464 | tf_op jit(solution)/shard_map/ppermute | solution.py:49
  45.2 1.0 %shard_map.129.before = f32[3,128,512]{2,1,0:T(8,128)S(1)} custom-call(s32[8,128]{1,0:T(8,128)S(1)} %get-tuple-element.48.facts, f32[8,80,512]{2,1,0:T(8,128)S(1)} %get-tuple-element.68.saved, f32[3,8,512]{2,1,0:T(8,128)S(1)} %fusion.1.push), custom_call_target="tpu_custom_call" | custom-call | flops 1207959552 | bytes 786432 | tf_op jit(solution)/shard_map/pallas_call | solution.py:35
  46.2 3.3 %collective-permute-done.13 = f32[3,8,512]{2,1,0:T(8,128)S(1)} collective-permute-done((f32[3,8,512]{2,1,0:T(8,128)S(1)}, f32[3,8,512]{2,1,0:T(8,128)S(1)}, u32[]{:S(2)}, u32[]{:S(2)}) %collective-permute-start.13) | collective-permute-done | bytes 49184 | tf_op jit(solution)/shard_map/ppermute | solution.py:49
  49.5 0.9 collective-permute-done.12
  50.5 1.1 %collective-permute-start.15 = (f32[3,24,512]{2,1,0:T(8,128)S(1)}, f32[3,24,512]{2,1,0:T(8,128)S(1)}, u32[]{:S(2)}, u32[]{:S(2)}) collective-permute-start(f32[3,24,512]{2,1,0:T(8,128)S(1)} %pad_maximum_fusion.push), channel_id=1, source_target_pairs={{0,3},{1,2},{2,1},{3,0},{4,7},{5,6},{6,5},{7,4},{8,11},{9,10},{10,... | collective-permute-start | bytes 442376 | tf_op jit(solution)/shard_map/ppermute | solution.py:49
  51.6 2.8 %shard_map.130.before = f32[3,128,512]{2,1,0:T(8,128)S(1)} custom-call(s32[8,128]{1,0:T(8,128)S(1)} %get-tuple-element.48.facts, f32[16,80,512]{2,1,0:T(8,128)S(1)} %get-tuple-element.67.saved, f32[3,24,512]{2,1,0:T(8,128)S(1)} %pad_maximum_fusion.push, f32[3,128,512]{2,1,0:T(8,128)S(1)} %shard_map.129.before), custom_call_target="tpu_custom_call" | custom-call | flops 2415919104 | bytes 1572864 | tf_op jit(solution)/shard_map/pallas_call | solution.py:35
  54.5 1.6 %collective-permute-done.15.push_1 = f32[3,24,512]{2,1,0:T(8,128)S(1)} collective-permute-done((f32[3,24,512]{2,1,0:T(8,128)S(1)}, f32[3,24,512]{2,1,0:T(8,128)S(1)}, u32[]{:S(2)}, u32[]{:S(2)}) %collective-permute-start.15) | collective-permute-done | bytes 147488 | tf_op jit(solution)/shard_map/ppermute | solution.py:49
  56.1 6.4 %shard_map.131 = (f32[3,16,32,128]{3,2,1,0:T(8,128)}, f32[32,128]{1,0:T(8,128)S(1)}, f32[32,128]{1,0:T(8,128)S(1)}, f32[16,128]{1,0:T(8,128)S(1)}, f32[16,128]{1,0:T(8,128)S(1)}, /*index=5*/f32[16,32,128]{2,1,0:T(8,128)S(1)}) custom-call(s32[8,128]{1,0:T(8,128)S(1)} %get-tuple-element.48.facts, f32[24,80,512]{2,1,0:T(8,128)S(1)} %get-tuple-element.60.saved_0, ...), custom_call_target="tpu_custom_call" | custom-call | flops 7247757312 | bytes 2359296 | tf_op jit(solution)/shard_map/pallas_call | solution.py:35
  62.5 4.7 %collective-permute-start.17 = (f32[32,128]{1,0:T(8,128)S(1)}, f32[32,128]{1,0:T(8,128)S(1)}, u32[]{:S(2)}, u32[]{:S(2)}) collective-permute-start(f32[32,128]{1,0:T(8,128)S(1)} %get-tuple-element.73), channel_id=1, source_target_pairs={{0,28},{4,8},{8,4},{12,16},{16,12},{20,24},{24,20},{28,0},{1,29},{... | collective-permute-start | bytes 49160 | tf_op jit(solution)/shard_map/ppermute | solution.py:49
  67.2 0.2 collective-permute-start.19
  67.4 0.9 collective-permute-done.18.w_0
  68.4 1.9 %collective-permute-done.19.w_1 = f32[16,128]{1,0:T(8,128)S(1)} collective-permute-done((f32[16,128]{1,0:T(8,128)S(1)}, f32[16,128]{1,0:T(8,128)S(1)}, u32[]{:S(2)}, u32[]{:S(2)}) %collective-permute-start.19) | collective-permute-done | bytes 8224 | tf_op jit(solution)/shard_map/ppermute | solution.py:49
  70.3 0.2 shard_map.132
  70.5 0.6 collective-permute-start.20
  71.1 0.1 collective-permute-start.21
  71.2 1.3 %collective-permute-start.22 = (f32[32,512]{1,0:T(8,128)S(1)}, f32[32,512]{1,0:T(8,128)S(1)}, u32[]{:S(2)}, u32[]{:S(2)}) collective-permute-start(f32[32,512]{1,0:T(8,128)S(1)} %get-tuple-element.79), channel_id=1, source_target_pairs={{0,3},{1,2},{2,1},{3,0},{4,7},{5,6},{6,5},{7,4},{8,11},{9,10},{10,... | collective-permute-start | bytes 196616 | tf_op jit(solution)/shard_map/ppermute | solution.py:893
  72.5 3.3 %collective-permute-done.21.refs_2_ = f32[32,512]{1,0:T(8,128)S(1)} collective-permute-done((f32[32,512]{1,0:T(8,128)S(1)}, f32[32,512]{1,0:T(8,128)S(1)}, u32[]{:S(2)}, u32[]{:S(2)}) %collective-permute-start.21) | collective-permute-done | bytes 65568 | tf_op jit(solution)/shard_map/ppermute | solution.py:893
  75.9 0.7 shard_map.133
  76.7 3.4 %collective-permute-start.25 = (f32[32,512]{1,0:T(8,128)S(1)}, f32[32,512]{1,0:T(8,128)S(1)}, u32[]{:S(2)}, u32[]{:S(2)}) collective-permute-start(f32[32,512]{1,0:T(8,128)S(1)} %get-tuple-element.83), channel_id=1, source_target_pairs={{0,12},{4,8},{8,4},{12,0},{16,28},{20,24},{24,20},{28,16},{1,13},{... | collective-permute-start | bytes 196616 | tf_op jit(solution)/shard_map/ppermute | solution.py:893
  80.1 1.1 %collective-permute-start.26 = (f32[32,512]{1,0:T(8,128)S(1)}, f32[32,512]{1,0:T(8,128)S(1)}, u32[]{:S(2)}, u32[]{:S(2)}) collective-permute-start(f32[32,512]{1,0:T(8,128)S(1)} %get-tuple-element.84), channel_id=1, source_target_pairs={{0,16},{4,20},{8,24},{12,28},{16,0},{20,4},{24,8},{28,12},{1,17},{... | collective-permute-start | bytes 196616 | tf_op jit(solution)/shard_map/ppermute | solution.py:893
  81.1 1.4 %collective-permute-start.27 = (f32[32,512]{1,0:T(8,128)S(1)}, f32[32,512]{1,0:T(8,128)S(1)}, u32[]{:S(2)}, u32[]{:S(2)}) collective-permute-start(f32[32,512]{1,0:T(8,128)S(1)} %get-tuple-element.85), channel_id=1, source_target_pairs={{0,20},{4,16},{8,28},{12,24},{16,4},{20,0},{24,12},{28,8},{1,21},{... | collective-permute-start | bytes 196616 | tf_op jit(solution)/shard_map/ppermute | solution.py:893
  82.5 3.9 %collective-permute-start.28 = (f32[32,512]{1,0:T(8,128)S(1)}, f32[32,512]{1,0:T(8,128)S(1)}, u32[]{:S(2)}, u32[]{:S(2)}) collective-permute-start(f32[32,512]{1,0:T(8,128)S(1)} %get-tuple-element.86), channel_id=1, source_target_pairs={{0,24},{4,28},{8,16},{12,20},{16,8},{20,12},{24,0},{28,4},{1,25},{... | collective-permute-start | bytes 196616 | tf_op jit(solution)/shard_map/ppermute | solution.py:893
  86.4 1.3 %collective-permute-start.29 = (f32[32,512]{1,0:T(8,128)S(1)}, f32[32,512]{1,0:T(8,128)S(1)}, u32[]{:S(2)}, u32[]{:S(2)}) collective-permute-start(f32[32,512]{1,0:T(8,128)S(1)} %get-tuple-element.87), channel_id=1, source_target_pairs={{0,28},{4,24},{8,20},{12,16},{16,12},{20,8},{24,4},{28,0},{1,29},{... | collective-permute-start | bytes 196616 | tf_op jit(solution)/shard_map/ppermute | solution.py:893
  87.7 2.4 %collective-permute-done.26.refs_4_ = f32[32,512]{1,0:T(8,128)S(1)} collective-permute-done((f32[32,512]{1,0:T(8,128)S(1)}, f32[32,512]{1,0:T(8,128)S(1)}, u32[]{:S(2)}, u32[]{:S(2)}) %collective-permute-start.26) | collective-permute-done | bytes 65568 | tf_op jit(solution)/shard_map/ppermute | solution.py:893
  90.1 1.6 %collective-permute-done.27.refs_5_ = f32[32,512]{1,0:T(8,128)S(1)} collective-permute-done((f32[32,512]{1,0:T(8,128)S(1)}, f32[32,512]{1,0:T(8,128)S(1)}, u32[]{:S(2)}, u32[]{:S(2)}) %collective-permute-start.27) | collective-permute-done | bytes 65568 | tf_op jit(solution)/shard_map/ppermute | solution.py:893
  91.7 1.8 %collective-permute-done.29.refs_7_ = f32[32,512]{1,0:T(8,128)S(1)} collective-permute-done((f32[32,512]{1,0:T(8,128)S(1)}, f32[32,512]{1,0:T(8,128)S(1)}, u32[]{:S(2)}, u32[]{:S(2)}) %collective-permute-start.29) | collective-permute-done | bytes 65568 | tf_op jit(solution)/shard_map/ppermute | solution.py:893
  93.5 1.6 %shard_map.134 = f32[2,32,16,128]{3,2,1,0:T(8,128)} custom-call(bf16[256,256]{1,0:T(8,128)(2,1)S(1)} %copy-done.1, bf16[256,256]{1,0:T(8,128)(2,1)S(1)} %copy-done.2, f32[32,512]{1,0:T(8,128)S(1)} %get-tuple-element.80.refs_0_, f32[32,512]{1,0:T(8,128)S(1)} %collective-permute-done.23.refs_1_, f32[32,512]{1,0:T(8,128)S(1)} %collective-permute-done.24.refs_2_, ...), custom_call_target="tpu_custom_call" | custom-call | flops 201326592 | bytes 1572864 | tf_op jit(solution)/shard_map/pallas_call | solution.py:35
  (46 shorter events, 0.6 us)
Async XLA Ops:
  2.7 6.6 %collective-permute-start = (f32[104,128]{1,0:T(8,128)}, f32[104,128]{1,0:T(8,128)S(1)}, u32[]{:S(2)}, u32[]{:S(2)}) collective-permute-start(f32[104,128]{1,0:T(8,128)} %get-tuple-element.45.own), channel_id=1, source_target_pairs={{0,4},{4,0},{8,12},{12,8},{16,20},{20,16},{24,28},{28,24},{1,5},{5... | collective-permute-start | bytes 159752 | tf_op jit(solution)/shard_map/ppermute | solution.py:49
  5.8 7.0 %collective-permute-start.1 = (f32[104,128]{1,0:T(8,128)}, f32[104,128]{1,0:T(8,128)S(1)}, u32[]{:S(2)}, u32[]{:S(2)}) collective-permute-start(f32[104,128]{1,0:T(8,128)} %get-tuple-element.45.own), channel_id=1, source_target_pairs={{0,28},{4,8},{8,4},{12,16},{16,12},{20,24},{24,20},{28,0},{1,29},{... | collective-permute-start | bytes 159752 | tf_op jit(solution)/shard_map/ppermute | solution.py:49
  9.3 5.8 %collective-permute-start.6 = (f32[128,128]{1,0:T(8,128)}, f32[128,128]{1,0:T(8,128)S(1)}, u32[]{:S(2)}, u32[]{:S(2)}) collective-permute-start(f32[128,128]{1,0:T(8,128)} %get-tuple-element.56), channel_id=1, source_target_pairs={{0,4},{4,0},{8,12},{12,8},{16,20},{20,16},{24,28},{28,24},{1,5},{5... | collective-permute-start | bytes 196616 | tf_op jit(solution)/shard_map/ppermute | solution.py:49
  12.8 9.8 %collective-permute-start.4 = (f32[208,128]{1,0:T(8,128)S(1)}, f32[208,128]{1,0:T(8,128)S(1)}, u32[]{:S(2)}, u32[]{:S(2)}) collective-permute-start(f32[208,128]{1,0:T(8,128)S(1)} %shard_map.122), channel_id=1, source_target_pairs={{0,1},{1,0},{2,3},{3,2},{4,5},{5,4},{6,7},{7,6},{8,9},{9,8},{10,11... | collective-permute-start | bytes 319496 | tf_op jit(solution)/shard_map/ppermute | solution.py:49
  12.9 9.8 %collective-permute-start.5 = (f32[208,128]{1,0:T(8,128)S(1)}, f32[208,128]{1,0:T(8,128)S(1)}, u32[]{:S(2)}, u32[]{:S(2)}) collective-permute-start(f32[208,128]{1,0:T(8,128)S(1)} %shard_map.122), channel_id=1, source_target_pairs={{0,3},{1,2},{2,1},{3,0},{4,7},{5,6},{6,5},{7,4},{8,11},{9,10},{10,... | collective-permute-start | bytes 319496 | tf_op jit(solution)/shard_map/ppermute | solution.py:49
  14.5 7.8 %collective-permute-start.2 = (f32[168,128]{1,0:T(8,128)}, f32[168,128]{1,0:T(8,128)S(1)}, u32[]{:S(2)}, u32[]{:S(2)}) collective-permute-start(f32[168,128]{1,0:T(8,128)} %get-tuple-element.46), channel_id=1, source_target_pairs={{0,1},{1,0},{2,3},{3,2},{4,5},{5,4},{6,7},{7,6},{8,9},{9,8},{10,11... | collective-permute-start | bytes 258056 | tf_op jit(solution)/shard_map/ppermute | solution.py:49
  14.6 7.8 %collective-permute-start.3 = (f32[168,128]{1,0:T(8,128)}, f32[168,128]{1,0:T(8,128)S(1)}, u32[]{:S(2)}, u32[]{:S(2)}) collective-permute-start(f32[168,128]{1,0:T(8,128)} %get-tuple-element.47), channel_id=1, source_target_pairs={{0,3},{1,2},{2,1},{3,0},{4,7},{5,6},{6,5},{7,4},{8,11},{9,10},{10,... | collective-permute-start | bytes 258056 | tf_op jit(solution)/shard_map/ppermute | solution.py:49
  15.1 7.2 %collective-permute-start.7 = (f32[128,128]{1,0:T(8,128)}, f32[128,128]{1,0:T(8,128)S(1)}, u32[]{:S(2)}, u32[]{:S(2)}) collective-permute-start(f32[128,128]{1,0:T(8,128)} %get-tuple-element.57), channel_id=1, source_target_pairs={{0,28},{4,8},{8,4},{12,16},{16,12},{20,24},{24,20},{28,0},{1,29},{... | collective-permute-start | bytes 196616 | tf_op jit(solution)/shard_map/ppermute | solution.py:49
  18.7 1.2 %copy-start = (f32[4,16,32,128]{3,2,1,0:T(8,128)S(1)}, f32[4,16,32,128]{3,2,1,0:T(8,128)}, u32[]{:S(2)}) copy-start(f32[4,16,32,128]{3,2,1,0:T(8,128)} %flow.3) | copy-start | bytes 3145732
  22.7 0.8 copy-start.5
  28.9 3.0 %collective-permute-start.8 = (f32[3,24,512]{2,1,0:T(8,128)S(1)}, f32[3,24,512]{2,1,0:T(8,128)S(1)}, u32[]{:S(2)}, u32[]{:S(2)}) collective-permute-start(f32[3,24,512]{2,1,0:T(8,128)S(1)} %get-tuple-element.64), channel_id=1, source_target_pairs={{0,1},{1,0},{2,3},{3,2},{4,5},{5,4},{6,7},{7,6},{8,9},{9,8},{10,11... | collective-permute-start | bytes 442376 | tf_op jit(solution)/shard_map/ppermute | solution.py:49
  29.0 5.6 %collective-permute-start.9 = (f32[3,24,512]{2,1,0:T(8,128)S(1)}, f32[3,24,512]{2,1,0:T(8,128)S(1)}, u32[]{:S(2)}, u32[]{:S(2)}) collective-permute-start(f32[3,24,512]{2,1,0:T(8,128)S(1)} %get-tuple-element.65), channel_id=1, source_target_pairs={{0,3},{1,2},{2,1},{3,0},{4,7},{5,6},{6,5},{7,4},{8,11},{9,10},{10,... | collective-permute-start | bytes 442376 | tf_op jit(solution)/shard_map/ppermute | solution.py:49
  29.0 9.3 %copy-start.6 = (f32[3,128]{1,0:T(4,128)S(1)}, f32[3,128]{1,0:T(4,128)}, u32[]{:S(2)}) copy-start(f32[3,128]{1,0:T(4,128)} %refs_3_.1) | copy-start | bytes 4612
  29.0 9.3 %copy-start.7 = (f32[3,128]{1,0:T(4,128)S(1)}, f32[3,128]{1,0:T(4,128)}, u32[]{:S(2)}) copy-start(f32[3,128]{1,0:T(4,128)} %refs_4_.1) | copy-start | bytes 4612
  34.6 7.3 %collective-permute-start.11 = (f32[3,8,512]{2,1,0:T(8,128)S(1)}, f32[3,8,512]{2,1,0:T(8,128)S(1)}, u32[]{:S(2)}, u32[]{:S(2)}) collective-permute-start(f32[3,8,512]{2,1,0:T(8,128)S(1)} %get-tuple-element.89), channel_id=1, source_target_pairs={{0,28},{4,8},{8,4},{12,16},{16,12},{20,24},{24,20},{28,0},{1,29},{... | collective-permute-start | bytes 147464 | tf_op jit(solution)/shard_map/ppermute | solution.py:49
  38.4 4.2 %collective-permute-start.10 = (f32[3,8,512]{2,1,0:T(8,128)S(1)}, f32[3,8,512]{2,1,0:T(8,128)S(1)}, u32[]{:S(2)}, u32[]{:S(2)}) collective-permute-start(f32[3,8,512]{2,1,0:T(8,128)S(1)} %get-tuple-element.88), channel_id=1, source_target_pairs={{0,4},{4,0},{8,12},{12,8},{16,20},{20,16},{24,28},{28,24},{1,5},{5... | collective-permute-start | bytes 147464 | tf_op jit(solution)/shard_map/ppermute | solution.py:49
  42.6 7.0 %collective-permute-start.13 = (f32[3,8,512]{2,1,0:T(8,128)S(1)}, f32[3,8,512]{2,1,0:T(8,128)S(1)}, u32[]{:S(2)}, u32[]{:S(2)}) collective-permute-start(f32[3,8,512]{2,1,0:T(8,128)S(1)} %fusion.1.push), channel_id=1, source_target_pairs={{0,28},{4,8},{8,4},{12,16},{16,12},{20,24},{24,20},{28,0},{1,29},{... | collective-permute-start | bytes 147464 | tf_op jit(solution)/shard_map/ppermute | solution.py:49
  45.2 5.1 %collective-permute-start.12 = (f32[3,8,512]{2,1,0:T(8,128)S(1)}, f32[3,8,512]{2,1,0:T(8,128)S(1)}, u32[]{:S(2)}, u32[]{:S(2)}) collective-permute-start(f32[3,8,512]{2,1,0:T(8,128)S(1)} %fusion.1.push), channel_id=1, source_target_pairs={{0,4},{4,0},{8,12},{12,8},{16,20},{20,16},{24,28},{28,24},{1,5},{5... | collective-permute-start | bytes 147464 | tf_op jit(solution)/shard_map/ppermute | solution.py:49
  50.4 4.1 %collective-permute-start.14 = (f32[3,24,512]{2,1,0:T(8,128)S(1)}, f32[3,24,512]{2,1,0:T(8,128)S(1)}, u32[]{:S(2)}, u32[]{:S(2)}) collective-permute-start(f32[3,24,512]{2,1,0:T(8,128)S(1)} %pad_maximum_fusion.push), channel_id=1, source_target_pairs={{0,1},{1,0},{2,3},{3,2},{4,5},{5,4},{6,7},{7,6},{8,9},{9,8},{10,11... | collective-permute-start | bytes 442376 | tf_op jit(solution)/shard_map/ppermute | solution.py:49
  50.5 5.6 %collective-permute-start.15 = (f32[3,24,512]{2,1,0:T(8,128)S(1)}, f32[3,24,512]{2,1,0:T(8,128)S(1)}, u32[]{:S(2)}, u32[]{:S(2)}) collective-permute-start(f32[3,24,512]{2,1,0:T(8,128)S(1)} %pad_maximum_fusion.push), channel_id=1, source_target_pairs={{0,3},{1,2},{2,1},{3,0},{4,7},{5,6},{6,5},{7,4},{8,11},{9,10},{10,... | collective-permute-start | bytes 442376 | tf_op jit(solution)/shard_map/ppermute | solution.py:49
  56.1 19.8 %copy-start.3 = (bf16[256,128]{1,0:T(8,128)(2,1)S(1)}, bf16[256,128]{1,0:T(8,128)(2,1)}, u32[]{:S(2)}) copy-start(bf16[256,128]{1,0:T(8,128)(2,1)} %constant.8.clone.table_high) | copy-start | bytes 196612
  56.1 19.8 %copy-start.4 = (bf16[256,128]{1,0:T(8,128)(2,1)S(1)}, bf16[256,128]{1,0:T(8,128)(2,1)}, u32[]{:S(2)}) copy-start(bf16[256,128]{1,0:T(8,128)(2,1)} %constant.9.clone.table_low) | copy-start | bytes 196612
  56.1 37.4 %copy-start.1 = (bf16[256,256]{1,0:T(8,128)(2,1)S(1)}, bf16[256,256]{1,0:T(8,128)(2,1)}, u32[]{:S(2)}) copy-start(bf16[256,256]{1,0:T(8,128)(2,1)} %constant.10.clone.table_high) | copy-start | bytes 393220
  56.1 37.4 %copy-start.2 = (bf16[256,256]{1,0:T(8,128)(2,1)S(1)}, bf16[256,256]{1,0:T(8,128)(2,1)}, u32[]{:S(2)}) copy-start(bf16[256,256]{1,0:T(8,128)(2,1)} %constant.11.clone.table_low) | copy-start | bytes 393220
  62.5 7.8 %collective-permute-start.16 = (f32[32,128]{1,0:T(8,128)S(1)}, f32[32,128]{1,0:T(8,128)S(1)}, u32[]{:S(2)}, u32[]{:S(2)}) collective-permute-start(f32[32,128]{1,0:T(8,128)S(1)} %get-tuple-element.72), channel_id=1, source_target_pairs={{0,4},{4,0},{8,12},{12,8},{16,20},{20,16},{24,28},{28,24},{1,5},{5... | collective-permute-start | bytes 49160 | tf_op jit(solution)/shard_map/ppermute | solution.py:49
  62.5 7.8 %collective-permute-start.17 = (f32[32,128]{1,0:T(8,128)S(1)}, f32[32,128]{1,0:T(8,128)S(1)}, u32[]{:S(2)}, u32[]{:S(2)}) collective-permute-start(f32[32,128]{1,0:T(8,128)S(1)} %get-tuple-element.73), channel_id=1, source_target_pairs={{0,28},{4,8},{8,4},{12,16},{16,12},{20,24},{24,20},{28,0},{1,29},{... | collective-permute-start | bytes 49160 | tf_op jit(solution)/shard_map/ppermute | solution.py:49
  67.2 1.2 %collective-permute-start.18 = (f32[16,128]{1,0:T(8,128)S(1)}, f32[16,128]{1,0:T(8,128)S(1)}, u32[]{:S(2)}, u32[]{:S(2)}) collective-permute-start(f32[16,128]{1,0:T(8,128)S(1)} %get-tuple-element.74), channel_id=1, source_target_pairs={{0,1},{1,0},{2,3},{3,2},{4,5},{5,4},{6,7},{7,6},{8,9},{9,8},{10,11... | collective-permute-start | bytes 24584 | tf_op jit(solution)/shard_map/ppermute | solution.py:49
  67.2 3.1 %collective-permute-start.19 = (f32[16,128]{1,0:T(8,128)S(1)}, f32[16,128]{1,0:T(8,128)S(1)}, u32[]{:S(2)}, u32[]{:S(2)}) collective-permute-start(f32[16,128]{1,0:T(8,128)S(1)} %get-tuple-element.75), channel_id=1, source_target_pairs={{0,3},{1,2},{2,1},{3,0},{4,7},{5,6},{6,5},{7,4},{8,11},{9,10},{10,... | collective-permute-start | bytes 24584 | tf_op jit(solution)/shard_map/ppermute | solution.py:49
  70.5 2.0 %collective-permute-start.20 = (f32[32,512]{1,0:T(8,128)S(1)}, f32[32,512]{1,0:T(8,128)S(1)}, u32[]{:S(2)}, u32[]{:S(2)}) collective-permute-start(f32[32,512]{1,0:T(8,128)S(1)} %get-tuple-element.77), channel_id=1, source_target_pairs={{0,1},{1,0},{2,3},{3,2},{4,5},{5,4},{6,7},{7,6},{8,9},{9,8},{10,11... | collective-permute-start | bytes 196616 | tf_op jit(solution)/shard_map/ppermute | solution.py:893
  71.1 4.8 %collective-permute-start.21 = (f32[32,512]{1,0:T(8,128)S(1)}, f32[32,512]{1,0:T(8,128)S(1)}, u32[]{:S(2)}, u32[]{:S(2)}) collective-permute-start(f32[32,512]{1,0:T(8,128)S(1)} %get-tuple-element.78), channel_id=1, source_target_pairs={{0,2},{1,3},{2,0},{3,1},{4,6},{5,7},{6,4},{7,5},{8,10},{9,11},{10,... | collective-permute-start | bytes 196616 | tf_op jit(solution)/shard_map/ppermute | solution.py:893
  71.2 4.7 %collective-permute-start.22 = (f32[32,512]{1,0:T(8,128)S(1)}, f32[32,512]{1,0:T(8,128)S(1)}, u32[]{:S(2)}, u32[]{:S(2)}) collective-permute-start(f32[32,512]{1,0:T(8,128)S(1)} %get-tuple-element.79), channel_id=1, source_target_pairs={{0,3},{1,2},{2,1},{3,0},{4,7},{5,6},{6,5},{7,4},{8,11},{9,10},{10,... | collective-permute-start | bytes 196616 | tf_op jit(solution)/shard_map/ppermute | solution.py:893
  76.5 6.0 %collective-permute-start.23 = (f32[32,512]{1,0:T(8,128)S(1)}, f32[32,512]{1,0:T(8,128)S(1)}, u32[]{:S(2)}, u32[]{:S(2)}) collective-permute-start(f32[32,512]{1,0:T(8,128)S(1)} %get-tuple-element.81), channel_id=1, source_target_pairs={{0,4},{4,0},{8,12},{12,8},{16,20},{20,16},{24,28},{28,24},{1,5},{5... | collective-permute-start | bytes 196616 | tf_op jit(solution)/shard_map/ppermute | solution.py:893
  76.6 9.8 %collective-permute-start.24 = (f32[32,512]{1,0:T(8,128)S(1)}, f32[32,512]{1,0:T(8,128)S(1)}, u32[]{:S(2)}, u32[]{:S(2)}) collective-permute-start(f32[32,512]{1,0:T(8,128)S(1)} %get-tuple-element.82), channel_id=1, source_target_pairs={{0,8},{4,12},{8,0},{12,4},{16,24},{20,28},{24,16},{28,20},{1,9},{5... | collective-permute-start | bytes 196616 | tf_op jit(solution)/shard_map/ppermute | solution.py:893
  76.7 11.1 %collective-permute-start.25 = (f32[32,512]{1,0:T(8,128)S(1)}, f32[32,512]{1,0:T(8,128)S(1)}, u32[]{:S(2)}, u32[]{:S(2)}) collective-permute-start(f32[32,512]{1,0:T(8,128)S(1)} %get-tuple-element.83), channel_id=1, source_target_pairs={{0,12},{4,8},{8,4},{12,0},{16,28},{20,24},{24,20},{28,16},{1,13},{... | collective-permute-start | bytes 196616 | tf_op jit(solution)/shard_map/ppermute | solution.py:893
  80.1 10.0 %collective-permute-start.26 = (f32[32,512]{1,0:T(8,128)S(1)}, f32[32,512]{1,0:T(8,128)S(1)}, u32[]{:S(2)}, u32[]{:S(2)}) collective-permute-start(f32[32,512]{1,0:T(8,128)S(1)} %get-tuple-element.84), channel_id=1, source_target_pairs={{0,16},{4,20},{8,24},{12,28},{16,0},{20,4},{24,8},{28,12},{1,17},{... | collective-permute-start | bytes 196616 | tf_op jit(solution)/shard_map/ppermute | solution.py:893
  81.1 10.5 %collective-permute-start.27 = (f32[32,512]{1,0:T(8,128)S(1)}, f32[32,512]{1,0:T(8,128)S(1)}, u32[]{:S(2)}, u32[]{:S(2)}) collective-permute-start(f32[32,512]{1,0:T(8,128)S(1)} %get-tuple-element.85), channel_id=1, source_target_pairs={{0,20},{4,16},{8,28},{12,24},{16,4},{20,0},{24,12},{28,8},{1,21},{... | collective-permute-start | bytes 196616 | tf_op jit(solution)/shard_map/ppermute | solution.py:893
  82.5 9.2 %collective-permute-start.28 = (f32[32,512]{1,0:T(8,128)S(1)}, f32[32,512]{1,0:T(8,128)S(1)}, u32[]{:S(2)}, u32[]{:S(2)}) collective-permute-start(f32[32,512]{1,0:T(8,128)S(1)} %get-tuple-element.86), channel_id=1, source_target_pairs={{0,24},{4,28},{8,16},{12,20},{16,8},{20,12},{24,0},{28,4},{1,25},{... | collective-permute-start | bytes 196616 | tf_op jit(solution)/shard_map/ppermute | solution.py:893
  86.4 7.1 %collective-permute-start.29 = (f32[32,512]{1,0:T(8,128)S(1)}, f32[32,512]{1,0:T(8,128)S(1)}, u32[]{:S(2)}, u32[]{:S(2)}) collective-permute-start(f32[32,512]{1,0:T(8,128)S(1)} %get-tuple-element.87), channel_id=1, source_target_pairs={{0,28},{4,24},{8,20},{12,16},{16,12},{20,8},{24,4},{28,0},{1,29},{... | collective-permute-start | bytes 196616 | tf_op jit(solution)/shard_map/ppermute | solution.py:893

commit v2 on v1

--- a/solution.py
+++ b/solution.py
@@ -51,6 +51,10 @@
 
 def even(axis):
     return lax.rem(lax.axis_index(axis), 2) == 0
+
+
+def steps(devices):
+    return [0, *range(devices - 1, 0, -1)]
 
 
 def in_order(axis, shape):
@@ -585,7 +589,7 @@
     return minus, plus
 
 
-def predict_inner_kernel(sizes, flow, inner, u_first, u_last, w_first, w_last):
+def predict_inner_kernel(sizes, flow, own, inner, u_first, u_last, w_first, w_last, kept):
     size_x, size_z, size_y = sizes
     row = lax.broadcasted_iota(jnp.int32, (size_z, size_y), 0)
     lane = lax.broadcasted_iota(jnp.int32, (size_z, size_y), 1)
@@ -619,17 +623,21 @@
             inner[c, x] = value + time_step * (viscosity * laplace - advect - gradient[c])
         w_first[x : x + 1] = flow[2, x, 0:1]
         w_last[x : x + 1] = flow[2, x, size_z - 1 : size_z]
+    kept[...] = own[...]
     u_first[...] = flow[0, 0]
     u_last[...] = flow[0, size_x - 1]
 
 
-def predict_inner(sizes, flow):
+def predict_inner(sizes, flow, own):
     size_x, size_z, size_y = sizes
     return call(
         functools.partial(predict_inner_kernel, sizes),
-        [float32(3, *sizes)] + [float32(size_z, size_y)] * 2 + [float32(size_x, size_y)] * 2,
+        [float32(3, *sizes)]
+        + [float32(size_z, size_y)] * 2
+        + [float32(size_x, size_y)] * 2
+        + [float32(*own.shape)],
         [],
-        [flow],
+        [flow, own],
         [],
         200 * flow.size,
         8 * flow.size,
@@ -723,9 +731,9 @@
         part = jnp.concatenate(pieces, axis=0)
         whole[:, q * LANES : (q + 1) * LANES] = jnp.transpose(part)
     height = size_y // parts
-    for step in range(parts):
+    for out, step in zip(outs, steps(parts)):
         first = pl.multiple_of((lax.axis_index("gz") ^ step) * height, 8)
-        outs[step][...] = whole[pl.ds(first, height), :]
+        out[...] = whole[pl.ds(first, height), :]
 
 
 def divergence(sizes, parts, inner, ghosts):
@@ -766,8 +774,8 @@
     outs, (gathered, turned, whole) = refs[:parts_x], refs[parts_x:]
     height = size_y // parts_z
     group = LANES // size_z
-    for step in range(parts_z):
-        gathered[lax.axis_index("gz") ^ step] = pieces[step][...]
+    for piece, step in zip(pieces, steps(parts_z)):
+        gathered[lax.axis_index("gz") ^ step] = piece[...]
     for block in range(parts_z // group):
         for q in range(size_x // group):
             lanes = slice(q * LANES, (q + 1) * LANES)
@@ -787,9 +795,9 @@
     )
     whole[...] = result
     rows = whole.shape[0] // parts_x
-    for step in range(parts_x):
+    for out, step in zip(outs, steps(parts_x)):
         first = pl.multiple_of((lax.axis_index("gx") ^ step) * rows, 8)
-        outs[step][...] = whole[pl.ds(first, rows), :]
+        out[...] = whole[pl.ds(first, rows), :]
 
 
 def transform_z(sizes, counts, table, pieces):
@@ -821,8 +829,8 @@
     modes = size_z * parts_z // parts_x
     height = size_y // parts_z
     group = LANES // size_x
-    for step in range(parts_x):
-        gathered[lax.axis_index("gx") ^ step] = pieces[step][...]
+    for piece, step in zip(pieces, steps(parts_x)):
+        gathered[lax.axis_index("gx") ^ step] = piece[...]
     for block in range(parts_x // group):
         for q in range(height // group):
             lanes = slice(q * LANES, (q + 1) * LANES)
@@ -890,8 +898,8 @@
     devices = lax.axis_size(axis)
     assert devices & (devices - 1) == 0
     return [pieces[0]] + [
-        lax.ppermute(pieces[d], axis, [(i, i ^ d) for i in range(devices)])
-        for d in range(1, devices)
+        lax.ppermute(piece, axis, [(i, i ^ step) for i in range(devices)])
+        for piece, step in zip(pieces[1:], steps(devices)[1:])
     ]
 
 
@@ -912,7 +920,7 @@
     marks_1 = swap(own, "gx", 1)
     z_0, z_1 = swap(z_0, "gz", 0), swap(z_1, "gz", 1)
     x_0, x_1 = swap(x_0, "gx", 0), swap(x_1, "gx", 1)
-    inner = predict_inner(sizes, flow_state)
+    *inner, own = predict_inner(sizes, flow_state, own)
     sides = join(marks_0, marks_1)
     corners_0, corners_1 = swap(sides, "gz", 0), swap(sides, "gz", 1)
     predicted, *fields = predict_outer(layout, inner, x_0, x_1, z_0, z_1)

time: 95.3 us -> 92.5 us (0.971)
  waiting for transfers between devices: 28.6 us -> 26.6 us
    ppermute x10, waiting for transfers between devices: 9.12 us -> 7.92 us  [exchange(): lax.ppermute(piece, axis, [(i, i ^ step) for i in range(devices)])]
  transfers between devices with their start and end apart: 30 -> 30, of which waited for: 14 -> 16; matrix products, arithmetic and copies ran while one was open for 0% -> 0% of each run, Pallas kernels for 9% -> 10%
where the time goes in v2:
time: 92.5 us; the launch traced here: 92.3 us
  starting transfers between devices  37.6 us (41%)
  waiting for transfers between devices  26.6 us (29%)
  Pallas kernels  25.1 us (27%)
  local copies, waits for them, and re-layouts  2.05 us (2%)
    ppermute x20, starting transfers between devices, swap(): return lax.ppermute(array, axis, pairs)  25.2 us
    pallas_call x13, Pallas kernels, call(): pl.pallas_call(kernel, out_shape=out_shape, in_specs=[IN_SMEM] * len(scal...  23 us
    ppermute x20, waiting for transfers between devices, swap(): return lax.ppermute(array, axis, pairs)  18.7 us
    ppermute x10, starting transfers between devices, exchange(): lax.ppermute(piece, axis, [(i, i ^ step) for i in range(devices)])  12.4 us
    ppermute x10, waiting for transfers between devices, exchange(): lax.ppermute(piece, axis, [(i, i ^ step) for i in range(devices)])  7.92 us
    pallas_call x1, Pallas kernels, pack(): pl.pallas_call(functools.partial(pack_kernel, layout), out_shape=[float32...  2.06 us
    unnamed x16, local copies, waits for them, and re-layouts  2.05 us
  transfers between devices with their start and end apart: 30, of which 16 were waited for; matrix products, arithmetic and copies ran while one was open for 0% of the time, Pallas kernels for 10%

profile of v2, /device:TPU:0, one launch (start us, length us, event | category | flops | bytes accessed | tf_op | source)
XLA Modules:
  0.0 92.3 jit_solution(18028621082303422343)
XLA Ops:
  0.6 2.1 %pack.1 = (f32[104,128]{1,0:T(8,128)}, f32[128,128]{1,0:T(8,128)}, f32[128,128]{1,0:T(8,128)}, f32[168,128]{1,0:T(8,128)}, f32[168,128]{1,0:T(8,128)}) custom-call(s32[8]{0:T(128)} %slot_ids_hbm.1, s32[3,8]{1,0:T(4,128)} %corners_hbm.1, f32[4,16,32,128]{3,2,1,0:T(8,128)} %flow.3, s32[3,8,512]{2,1,0:T(8,128)} %cells_hbm.1, f32[3,8,512]{2,1,0:T(8,128)} %fraction_hbm.1), custom_call_target="tpu_custom_call" | custom-call | flops 262144 | bytes 262144 | tf_op jit(solution)/shard_map/pack/pallas_call | solution.py:498
  2.7 3.1 %collective-permute-start = (f32[104,128]{1,0:T(8,128)}, f32[104,128]{1,0:T(8,128)S(1)}, u32[]{:S(2)}, u32[]{:S(2)}) collective-permute-start(f32[104,128]{1,0:T(8,128)} %get-tuple-element.46.own), channel_id=1, source_target_pairs={{0,4},{4,0},{8,12},{12,8},{16,20},{20,16},{24,28},{28,24},{1,5},{5... | collective-permute-start | bytes 159752 | tf_op jit(solution)/shard_map/ppermute | solution.py:49
  5.8 3.5 %collective-permute-start.1 = (f32[104,128]{1,0:T(8,128)}, f32[104,128]{1,0:T(8,128)S(1)}, u32[]{:S(2)}, u32[]{:S(2)}) collective-permute-start(f32[104,128]{1,0:T(8,128)} %get-tuple-element.46.own), channel_id=1, source_target_pairs={{0,28},{4,8},{8,4},{12,16},{16,12},{20,24},{24,20},{28,0},{1,29},{... | collective-permute-start | bytes 159752 | tf_op jit(solution)/shard_map/ppermute | solution.py:49
  9.3 3.5 %collective-permute-done.1.right.side_1 = f32[104,128]{1,0:T(8,128)S(1)} collective-permute-done((f32[104,128]{1,0:T(8,128)}, f32[104,128]{1,0:T(8,128)S(1)}, u32[]{:S(2)}, u32[]{:S(2)}) %collective-permute-start.1) | collective-permute-done | bytes 53280 | tf_op jit(solution)/shard_map/ppermute | solution.py:49
  12.9 1.6 %collective-permute-start.5 = (f32[208,128]{1,0:T(8,128)S(1)}, f32[208,128]{1,0:T(8,128)S(1)}, u32[]{:S(2)}, u32[]{:S(2)}) collective-permute-start(f32[208,128]{1,0:T(8,128)S(1)} %shard_map.123), channel_id=1, source_target_pairs={{0,3},{1,2},{2,1},{3,0},{4,7},{5,6},{6,5},{7,4},{8,11},{9,10},{10,... | collective-permute-start | bytes 319496 | tf_op jit(solution)/shard_map/ppermute | solution.py:49
  14.6 0.6 collective-permute-start.3
  15.1 3.5 %collective-permute-start.7 = (f32[128,128]{1,0:T(8,128)}, f32[128,128]{1,0:T(8,128)S(1)}, u32[]{:S(2)}, u32[]{:S(2)}) collective-permute-start(f32[128,128]{1,0:T(8,128)} %get-tuple-element.59), channel_id=1, source_target_pairs={{0,28},{4,8},{8,4},{12,16},{16,12},{20,24},{24,20},{28,0},{1,29},{... | collective-permute-start | bytes 196616 | tf_op jit(solution)/shard_map/ppermute | solution.py:49
  18.7 1.2 %copy-done = f32[4,16,32,128]{3,2,1,0:T(8,128)S(1)} copy-done((f32[4,16,32,128]{3,2,1,0:T(8,128)S(1)}, f32[4,16,32,128]{3,2,1,0:T(8,128)}, u32[]{:S(2)}) %copy-start) | copy-done | bytes 1048600
  19.9 0.8 copy-done.5
  20.7 0.9 shard_map.122
  21.6 0.7 collective-permute-done.7.x_1
  22.3 0.3 shard_map.125
  22.7 0.1 shard_map.124
  22.8 5.3 %shard_map.126 = (f32[3,24,512]{2,1,0:T(8,128)S(1)}, f32[3,24,512]{2,1,0:T(8,128)S(1)}, f32[24,80,512]{2,1,0:T(8,128)S(1)}, f32[24,80,512]{2,1,0:T(8,128)S(1)}) custom-call(s32[8,128]{1,0:T(8,128)S(1)} %get-tuple-element.50.facts, f32[312,128]{1,0:T(8,128)S(1)} %get-tuple-element.51.refs_0_, f32[312,128]{1,0:T(8,128)S(1)} %get-tuple-element.52.refs_1_, ...), custom_call_target="tpu_custom_call" | custom-call | flops 7247757312 | bytes 1572864 | tf_op jit(solution)/shard_map/pallas_call | solution.py:35
  28.1 0.1 collective-permute-start.9
  28.2 2.8 %shard_map.128 = (f32[3,16,512]{2,1,0:T(8,128)S(1)}, f32[16,80,512]{2,1,0:T(8,128)S(1)}) custom-call(s32[8,128]{1,0:T(8,128)S(1)} %get-tuple-element.50.facts, f32[312,128]{1,0:T(8,128)S(1)} %get-tuple-element.64.refs_0_, f32[3,128,512]{2,1,0:T(8,128)S(1)} %get-tuple-element.60.refs_2_.refs_1_, f32[3,128,512]{2,1,0:T(8,128)S(1)} %get-tuple-element.61.refs_3_.refs_2_), custom_call_target="tpu_custom_call" | custom-call | flops 2415919104 | bytes 1572864 | tf_op jit(solution)/shard_map/pallas_call | solution.py:35
  31.1 2.6 %collective-permute-done.9 = f32[3,24,512]{2,1,0:T(8,128)S(1)} collective-permute-done((f32[3,24,512]{2,1,0:T(8,128)S(1)}, f32[3,24,512]{2,1,0:T(8,128)S(1)}, u32[]{:S(2)}, u32[]{:S(2)}) %collective-permute-start.9) | collective-permute-done | bytes 147488 | tf_op jit(solution)/shard_map/ppermute | solution.py:49
  33.8 3.8 %collective-permute-start.11 = (f32[3,8,512]{2,1,0:T(8,128)S(1)}, f32[3,8,512]{2,1,0:T(8,128)S(1)}, u32[]{:S(2)}, u32[]{:S(2)}) collective-permute-start(f32[3,8,512]{2,1,0:T(8,128)S(1)} %get-tuple-element.91), channel_id=1, source_target_pairs={{0,28},{4,8},{8,4},{12,16},{16,12},{20,24},{24,20},{28,0},{1,29},{... | collective-permute-start | bytes 147464 | tf_op jit(solution)/shard_map/ppermute | solution.py:49
  37.6 1.0 %shard_map.127 = (f32[3,8,512]{2,1,0:T(8,128)S(1)}, f32[8,80,512]{2,1,0:T(8,128)S(1)}) custom-call(s32[8,128]{1,0:T(8,128)S(1)} %get-tuple-element.50.facts, f32[312,128]{1,0:T(8,128)S(1)} %get-tuple-element.64.refs_0_, f32[3,128,512]{2,1,0:T(8,128)S(1)} %get-tuple-element.60.refs_2_.refs_1_, f32[3,128,512]{2,1,0:T(8,128)S(1)} %get-tuple-element.61.refs_3_.refs_2_, ...), custom_call_target="tpu_custom_call" | custom-call | flops 1207959552 | bytes 1572864 | tf_op jit(solution)/shard_map/pallas_call | solution.py:35
  38.5 2.5 %collective-permute-done.11 = f32[3,8,512]{2,1,0:T(8,128)S(1)} collective-permute-done((f32[3,8,512]{2,1,0:T(8,128)S(1)}, f32[3,8,512]{2,1,0:T(8,128)S(1)}, u32[]{:S(2)}, u32[]{:S(2)}) %collective-permute-start.11) | collective-permute-done | bytes 49184 | tf_op jit(solution)/shard_map/ppermute | solution.py:49
  41.1 0.6 collective-permute-done.10
  41.8 2.7 %collective-permute-start.13 = (f32[3,8,512]{2,1,0:T(8,128)S(1)}, f32[3,8,512]{2,1,0:T(8,128)S(1)}, u32[]{:S(2)}, u32[]{:S(2)}) collective-permute-start(f32[3,8,512]{2,1,0:T(8,128)S(1)} %fusion.1.push), channel_id=1, source_target_pairs={{0,28},{4,8},{8,4},{12,16},{16,12},{20,24},{24,20},{28,0},{1,29},{... | collective-permute-start | bytes 147464 | tf_op jit(solution)/shard_map/ppermute | solution.py:49
  44.4 1.0 %shard_map.129.before = f32[3,128,512]{2,1,0:T(8,128)S(1)} custom-call(s32[8,128]{1,0:T(8,128)S(1)} %get-tuple-element.50.facts, f32[8,80,512]{2,1,0:T(8,128)S(1)} %get-tuple-element.70.saved, f32[3,8,512]{2,1,0:T(8,128)S(1)} %fusion.1.push), custom_call_target="tpu_custom_call" | custom-call | flops 1207959552 | bytes 786432 | tf_op jit(solution)/shard_map/pallas_call | solution.py:35
  45.4 3.3 %collective-permute-done.13 = f32[3,8,512]{2,1,0:T(8,128)S(1)} collective-permute-done((f32[3,8,512]{2,1,0:T(8,128)S(1)}, f32[3,8,512]{2,1,0:T(8,128)S(1)}, u32[]{:S(2)}, u32[]{:S(2)}) %collective-permute-start.13) | collective-permute-done | bytes 49184 | tf_op jit(solution)/shard_map/ppermute | solution.py:49
  48.7 0.9 collective-permute-done.12
  49.7 1.1 %collective-permute-start.15 = (f32[3,24,512]{2,1,0:T(8,128)S(1)}, f32[3,24,512]{2,1,0:T(8,128)S(1)}, u32[]{:S(2)}, u32[]{:S(2)}) collective-permute-start(f32[3,24,512]{2,1,0:T(8,128)S(1)} %pad_maximum_fusion.push), channel_id=1, source_target_pairs={{0,3},{1,2},{2,1},{3,0},{4,7},{5,6},{6,5},{7,4},{8,11},{9,10},{10,... | collective-permute-start | bytes 442376 | tf_op jit(solution)/shard_map/ppermute | solution.py:49
  50.8 2.8 %shard_map.130.before = f32[3,128,512]{2,1,0:T(8,128)S(1)} custom-call(s32[8,128]{1,0:T(8,128)S(1)} %get-tuple-element.50.facts, f32[16,80,512]{2,1,0:T(8,128)S(1)} %get-tuple-element.69.saved, f32[3,24,512]{2,1,0:T(8,128)S(1)} %pad_maximum_fusion.push, f32[3,128,512]{2,1,0:T(8,128)S(1)} %shard_map.129.before), custom_call_target="tpu_custom_call" | custom-call | flops 2415919104 | bytes 1572864 | tf_op jit(solution)/shard_map/pallas_call | solution.py:35
  53.7 1.6 %collective-permute-done.15.push_1 = f32[3,24,512]{2,1,0:T(8,128)S(1)} collective-permute-done((f32[3,24,512]{2,1,0:T(8,128)S(1)}, f32[3,24,512]{2,1,0:T(8,128)S(1)}, u32[]{:S(2)}, u32[]{:S(2)}) %collective-permute-start.15) | collective-permute-done | bytes 147488 | tf_op jit(solution)/shard_map/ppermute | solution.py:49
  55.3 6.4 %shard_map.131 = (f32[3,16,32,128]{3,2,1,0:T(8,128)}, f32[32,128]{1,0:T(8,128)S(1)}, f32[32,128]{1,0:T(8,128)S(1)}, f32[16,128]{1,0:T(8,128)S(1)}, f32[16,128]{1,0:T(8,128)S(1)}, /*index=5*/f32[16,32,128]{2,1,0:T(8,128)S(1)}) custom-call(s32[8,128]{1,0:T(8,128)S(1)} %get-tuple-element.50.facts, f32[24,80,512]{2,1,0:T(8,128)S(1)} %get-tuple-element.62.saved_0, ...), custom_call_target="tpu_custom_call" | custom-call | flops 7247757312 | bytes 2359296 | tf_op jit(solution)/shard_map/pallas_call | solution.py:35
  61.7 4.7 %collective-permute-start.17 = (f32[32,128]{1,0:T(8,128)S(1)}, f32[32,128]{1,0:T(8,128)S(1)}, u32[]{:S(2)}, u32[]{:S(2)}) collective-permute-start(f32[32,128]{1,0:T(8,128)S(1)} %get-tuple-element.75), channel_id=1, source_target_pairs={{0,28},{4,8},{8,4},{12,16},{16,12},{20,24},{24,20},{28,0},{1,29},{... | collective-permute-start | bytes 49160 | tf_op jit(solution)/shard_map/ppermute | solution.py:49
  66.4 0.2 collective-permute-start.19
  66.6 0.9 %collective-permute-done.18.w_0 = f32[16,128]{1,0:T(8,128)S(1)} collective-permute-done((f32[16,128]{1,0:T(8,128)S(1)}, f32[16,128]{1,0:T(8,128)S(1)}, u32[]{:S(2)}, u32[]{:S(2)}) %collective-permute-start.18) | collective-permute-done | bytes 8224 | tf_op jit(solution)/shard_map/ppermute | solution.py:49
  67.6 1.9 %collective-permute-done.19.w_1 = f32[16,128]{1,0:T(8,128)S(1)} collective-permute-done((f32[16,128]{1,0:T(8,128)S(1)}, f32[16,128]{1,0:T(8,128)S(1)}, u32[]{:S(2)}, u32[]{:S(2)}) %collective-permute-start.19) | collective-permute-done | bytes 8224 | tf_op jit(solution)/shard_map/ppermute | solution.py:49
  69.5 0.2 shard_map.132
  69.7 0.3 collective-permute-start.20
  70.0 1.9 %collective-permute-start.21 = (f32[32,512]{1,0:T(8,128)S(1)}, f32[32,512]{1,0:T(8,128)S(1)}, u32[]{:S(2)}, u32[]{:S(2)}) collective-permute-start(f32[32,512]{1,0:T(8,128)S(1)} %get-tuple-element.80), channel_id=1, source_target_pairs={{0,2},{1,3},{2,0},{3,1},{4,6},{5,7},{6,4},{7,5},{8,10},{9,11},{10,... | collective-permute-start | bytes 196616 | tf_op jit(solution)/shard_map/ppermute | solution.py:901
  71.9 1.6 %collective-permute-done.20.refs_1_ = f32[32,512]{1,0:T(8,128)S(1)} collective-permute-done((f32[32,512]{1,0:T(8,128)S(1)}, f32[32,512]{1,0:T(8,128)S(1)}, u32[]{:S(2)}, u32[]{:S(2)}) %collective-permute-start.20) | collective-permute-done | bytes 65568 | tf_op jit(solution)/shard_map/ppermute | solution.py:901
  73.5 2.1 %collective-permute-done.21.refs_2_ = f32[32,512]{1,0:T(8,128)S(1)} collective-permute-done((f32[32,512]{1,0:T(8,128)S(1)}, f32[32,512]{1,0:T(8,128)S(1)}, u32[]{:S(2)}, u32[]{:S(2)}) %collective-permute-start.21) | collective-permute-done | bytes 65568 | tf_op jit(solution)/shard_map/ppermute | solution.py:901
  75.6 0.7 shard_map.133
  76.2 2.7 %collective-permute-start.23 = (f32[32,512]{1,0:T(8,128)S(1)}, f32[32,512]{1,0:T(8,128)S(1)}, u32[]{:S(2)}, u32[]{:S(2)}) collective-permute-start(f32[32,512]{1,0:T(8,128)S(1)} %get-tuple-element.83), channel_id=1, source_target_pairs={{0,28},{4,24},{8,20},{12,16},{16,12},{20,8},{24,4},{28,0},{1,29},{... | collective-permute-start | bytes 196616 | tf_op jit(solution)/shard_map/ppermute | solution.py:901
  78.9 5.0 %collective-permute-start.26 = (f32[32,512]{1,0:T(8,128)S(1)}, f32[32,512]{1,0:T(8,128)S(1)}, u32[]{:S(2)}, u32[]{:S(2)}) collective-permute-start(f32[32,512]{1,0:T(8,128)S(1)} %get-tuple-element.86), channel_id=1, source_target_pairs={{0,16},{4,20},{8,24},{12,28},{16,0},{20,4},{24,8},{28,12},{1,17},{... | collective-permute-start | bytes 196616 | tf_op jit(solution)/shard_map/ppermute | solution.py:901
  83.9 0.2 collective-permute-start.27
  84.2 0.6 collective-permute-start.28
  84.7 1.0 %collective-permute-done.24.refs_2_ = f32[32,512]{1,0:T(8,128)S(1)} collective-permute-done((f32[32,512]{1,0:T(8,128)S(1)}, f32[32,512]{1,0:T(8,128)S(1)}, u32[]{:S(2)}, u32[]{:S(2)}) %collective-permute-start.24) | collective-permute-done | bytes 65568 | tf_op jit(solution)/shard_map/ppermute | solution.py:901
  85.8 1.7 %collective-permute-start.29 = (f32[32,512]{1,0:T(8,128)S(1)}, f32[32,512]{1,0:T(8,128)S(1)}, u32[]{:S(2)}, u32[]{:S(2)}) collective-permute-start(f32[32,512]{1,0:T(8,128)S(1)} %get-tuple-element.89), channel_id=1, source_target_pairs={{0,4},{4,0},{8,12},{12,8},{16,20},{20,16},{24,28},{28,24},{1,5},{5... | collective-permute-start | bytes 196616 | tf_op jit(solution)/shard_map/ppermute | solution.py:901
  87.5 2.7 %collective-permute-done.26.refs_4_ = f32[32,512]{1,0:T(8,128)S(1)} collective-permute-done((f32[32,512]{1,0:T(8,128)S(1)}, f32[32,512]{1,0:T(8,128)S(1)}, u32[]{:S(2)}, u32[]{:S(2)}) %collective-permute-start.26) | collective-permute-done | bytes 65568 | tf_op jit(solution)/shard_map/ppermute | solution.py:901
  90.2 0.4 collective-permute-done.28.refs_6_
  90.7 1.6 %shard_map.134 = f32[2,32,16,128]{3,2,1,0:T(8,128)} custom-call(bf16[256,256]{1,0:T(8,128)(2,1)S(1)} %copy-done.1, bf16[256,256]{1,0:T(8,128)(2,1)S(1)} %copy-done.2, f32[32,512]{1,0:T(8,128)S(1)} %get-tuple-element.82.refs_0_, f32[32,512]{1,0:T(8,128)S(1)} %collective-permute-done.23.refs_1_, f32[32,512]{1,0:T(8,128)S(1)} %collective-permute-done.24.refs_2_, ...), custom_call_target="tpu_custom_call" | custom-call | flops 201326592 | bytes 1572864 | tf_op jit(solution)/shard_map/pallas_call | solution.py:35
  (46 shorter events, 0.5 us)
Async XLA Ops:
  2.7 6.6 %collective-permute-start = (f32[104,128]{1,0:T(8,128)}, f32[104,128]{1,0:T(8,128)S(1)}, u32[]{:S(2)}, u32[]{:S(2)}) collective-permute-start(f32[104,128]{1,0:T(8,128)} %get-tuple-element.46.own), channel_id=1, source_target_pairs={{0,4},{4,0},{8,12},{12,8},{16,20},{20,16},{24,28},{28,24},{1,5},{5... | collective-permute-start | bytes 159752 | tf_op jit(solution)/shard_map/ppermute | solution.py:49
  5.8 7.0 %collective-permute-start.1 = (f32[104,128]{1,0:T(8,128)}, f32[104,128]{1,0:T(8,128)S(1)}, u32[]{:S(2)}, u32[]{:S(2)}) collective-permute-start(f32[104,128]{1,0:T(8,128)} %get-tuple-element.46.own), channel_id=1, source_target_pairs={{0,28},{4,8},{8,4},{12,16},{16,12},{20,24},{24,20},{28,0},{1,29},{... | collective-permute-start | bytes 159752 | tf_op jit(solution)/shard_map/ppermute | solution.py:49
  9.3 5.8 %collective-permute-start.6 = (f32[128,128]{1,0:T(8,128)}, f32[128,128]{1,0:T(8,128)S(1)}, u32[]{:S(2)}, u32[]{:S(2)}) collective-permute-start(f32[128,128]{1,0:T(8,128)} %get-tuple-element.58), channel_id=1, source_target_pairs={{0,4},{4,0},{8,12},{12,8},{16,20},{20,16},{24,28},{28,24},{1,5},{5... | collective-permute-start | bytes 196616 | tf_op jit(solution)/shard_map/ppermute | solution.py:49
  12.8 9.8 %collective-permute-start.4 = (f32[208,128]{1,0:T(8,128)S(1)}, f32[208,128]{1,0:T(8,128)S(1)}, u32[]{:S(2)}, u32[]{:S(2)}) collective-permute-start(f32[208,128]{1,0:T(8,128)S(1)} %shard_map.123), channel_id=1, source_target_pairs={{0,1},{1,0},{2,3},{3,2},{4,5},{5,4},{6,7},{7,6},{8,9},{9,8},{10,11... | collective-permute-start | bytes 319496 | tf_op jit(solution)/shard_map/ppermute | solution.py:49
  12.9 9.8 %collective-permute-start.5 = (f32[208,128]{1,0:T(8,128)S(1)}, f32[208,128]{1,0:T(8,128)S(1)}, u32[]{:S(2)}, u32[]{:S(2)}) collective-permute-start(f32[208,128]{1,0:T(8,128)S(1)} %shard_map.123), channel_id=1, source_target_pairs={{0,3},{1,2},{2,1},{3,0},{4,7},{5,6},{6,5},{7,4},{8,11},{9,10},{10,... | collective-permute-start | bytes 319496 | tf_op jit(solution)/shard_map/ppermute | solution.py:49
  14.5 7.8 %collective-permute-start.2 = (f32[168,128]{1,0:T(8,128)}, f32[168,128]{1,0:T(8,128)S(1)}, u32[]{:S(2)}, u32[]{:S(2)}) collective-permute-start(f32[168,128]{1,0:T(8,128)} %get-tuple-element.48), channel_id=1, source_target_pairs={{0,1},{1,0},{2,3},{3,2},{4,5},{5,4},{6,7},{7,6},{8,9},{9,8},{10,11... | collective-permute-start | bytes 258056 | tf_op jit(solution)/shard_map/ppermute | solution.py:49
  14.6 7.8 %collective-permute-start.3 = (f32[168,128]{1,0:T(8,128)}, f32[168,128]{1,0:T(8,128)S(1)}, u32[]{:S(2)}, u32[]{:S(2)}) collective-permute-start(f32[168,128]{1,0:T(8,128)} %get-tuple-element.49), channel_id=1, source_target_pairs={{0,3},{1,2},{2,1},{3,0},{4,7},{5,6},{6,5},{7,4},{8,11},{9,10},{10,... | collective-permute-start | bytes 258056 | tf_op jit(solution)/shard_map/ppermute | solution.py:49
  15.1 7.2 %collective-permute-start.7 = (f32[128,128]{1,0:T(8,128)}, f32[128,128]{1,0:T(8,128)S(1)}, u32[]{:S(2)}, u32[]{:S(2)}) collective-permute-start(f32[128,128]{1,0:T(8,128)} %get-tuple-element.59), channel_id=1, source_target_pairs={{0,28},{4,8},{8,4},{12,16},{16,12},{20,24},{24,20},{28,0},{1,29},{... | collective-permute-start | bytes 196616 | tf_op jit(solution)/shard_map/ppermute | solution.py:49
  18.7 1.2 %copy-start = (f32[4,16,32,128]{3,2,1,0:T(8,128)S(1)}, f32[4,16,32,128]{3,2,1,0:T(8,128)}, u32[]{:S(2)}) copy-start(f32[4,16,32,128]{3,2,1,0:T(8,128)} %flow.3) | copy-start | bytes 3145732
  19.9 0.8 copy-start.5
  28.1 3.0 %collective-permute-start.8 = (f32[3,24,512]{2,1,0:T(8,128)S(1)}, f32[3,24,512]{2,1,0:T(8,128)S(1)}, u32[]{:S(2)}, u32[]{:S(2)}) collective-permute-start(f32[3,24,512]{2,1,0:T(8,128)S(1)} %get-tuple-element.66), channel_id=1, source_target_pairs={{0,1},{1,0},{2,3},{3,2},{4,5},{5,4},{6,7},{7,6},{8,9},{9,8},{10,11... | collective-permute-start | bytes 442376 | tf_op jit(solution)/shard_map/ppermute | solution.py:49
  28.1 5.6 %collective-permute-start.9 = (f32[3,24,512]{2,1,0:T(8,128)S(1)}, f32[3,24,512]{2,1,0:T(8,128)S(1)}, u32[]{:S(2)}, u32[]{:S(2)}) collective-permute-start(f32[3,24,512]{2,1,0:T(8,128)S(1)} %get-tuple-element.67), channel_id=1, source_target_pairs={{0,3},{1,2},{2,1},{3,0},{4,7},{5,6},{6,5},{7,4},{8,11},{9,10},{10,... | collective-permute-start | bytes 442376 | tf_op jit(solution)/shard_map/ppermute | solution.py:49
  28.2 9.3 %copy-start.6 = (f32[3,128]{1,0:T(4,128)S(1)}, f32[3,128]{1,0:T(4,128)}, u32[]{:S(2)}) copy-start(f32[3,128]{1,0:T(4,128)} %refs_3_.1) | copy-start | bytes 4612
  28.2 9.3 %copy-start.7 = (f32[3,128]{1,0:T(4,128)S(1)}, f32[3,128]{1,0:T(4,128)}, u32[]{:S(2)}) copy-start(f32[3,128]{1,0:T(4,128)} %refs_4_.1) | copy-start | bytes 4612
  33.8 7.3 %collective-permute-start.11 = (f32[3,8,512]{2,1,0:T(8,128)S(1)}, f32[3,8,512]{2,1,0:T(8,128)S(1)}, u32[]{:S(2)}, u32[]{:S(2)}) collective-permute-start(f32[3,8,512]{2,1,0:T(8,128)S(1)} %get-tuple-element.91), channel_id=1, source_target_pairs={{0,28},{4,8},{8,4},{12,16},{16,12},{20,24},{24,20},{28,0},{1,29},{... | collective-permute-start | bytes 147464 | tf_op jit(solution)/shard_map/ppermute | solution.py:49
  37.6 4.2 %collective-permute-start.10 = (f32[3,8,512]{2,1,0:T(8,128)S(1)}, f32[3,8,512]{2,1,0:T(8,128)S(1)}, u32[]{:S(2)}, u32[]{:S(2)}) collective-permute-start(f32[3,8,512]{2,1,0:T(8,128)S(1)} %get-tuple-element.90), channel_id=1, source_target_pairs={{0,4},{4,0},{8,12},{12,8},{16,20},{20,16},{24,28},{28,24},{1,5},{5... | collective-permute-start | bytes 147464 | tf_op jit(solution)/shard_map/ppermute | solution.py:49
  41.8 7.0 %collective-permute-start.13 = (f32[3,8,512]{2,1,0:T(8,128)S(1)}, f32[3,8,512]{2,1,0:T(8,128)S(1)}, u32[]{:S(2)}, u32[]{:S(2)}) collective-permute-start(f32[3,8,512]{2,1,0:T(8,128)S(1)} %fusion.1.push), channel_id=1, source_target_pairs={{0,28},{4,8},{8,4},{12,16},{16,12},{20,24},{24,20},{28,0},{1,29},{... | collective-permute-start | bytes 147464 | tf_op jit(solution)/shard_map/ppermute | solution.py:49
  44.4 5.1 %collective-permute-start.12 = (f32[3,8,512]{2,1,0:T(8,128)S(1)}, f32[3,8,512]{2,1,0:T(8,128)S(1)}, u32[]{:S(2)}, u32[]{:S(2)}) collective-permute-start(f32[3,8,512]{2,1,0:T(8,128)S(1)} %fusion.1.push), channel_id=1, source_target_pairs={{0,4},{4,0},{8,12},{12,8},{16,20},{20,16},{24,28},{28,24},{1,5},{5... | collective-permute-start | bytes 147464 | tf_op jit(solution)/shard_map/ppermute | solution.py:49
  49.6 4.1 %collective-permute-start.14 = (f32[3,24,512]{2,1,0:T(8,128)S(1)}, f32[3,24,512]{2,1,0:T(8,128)S(1)}, u32[]{:S(2)}, u32[]{:S(2)}) collective-permute-start(f32[3,24,512]{2,1,0:T(8,128)S(1)} %pad_maximum_fusion.push), channel_id=1, source_target_pairs={{0,1},{1,0},{2,3},{3,2},{4,5},{5,4},{6,7},{7,6},{8,9},{9,8},{10,11... | collective-permute-start | bytes 442376 | tf_op jit(solution)/shard_map/ppermute | solution.py:49
  49.7 5.6 %collective-permute-start.15 = (f32[3,24,512]{2,1,0:T(8,128)S(1)}, f32[3,24,512]{2,1,0:T(8,128)S(1)}, u32[]{:S(2)}, u32[]{:S(2)}) collective-permute-start(f32[3,24,512]{2,1,0:T(8,128)S(1)} %pad_maximum_fusion.push), channel_id=1, source_target_pairs={{0,3},{1,2},{2,1},{3,0},{4,7},{5,6},{6,5},{7,4},{8,11},{9,10},{10,... | collective-permute-start | bytes 442376 | tf_op jit(solution)/shard_map/ppermute | solution.py:49
  55.3 20.3 %copy-start.3 = (bf16[256,128]{1,0:T(8,128)(2,1)S(1)}, bf16[256,128]{1,0:T(8,128)(2,1)}, u32[]{:S(2)}) copy-start(bf16[256,128]{1,0:T(8,128)(2,1)} %constant.8.clone.table_high) | copy-start | bytes 196612
  55.3 20.3 %copy-start.4 = (bf16[256,128]{1,0:T(8,128)(2,1)S(1)}, bf16[256,128]{1,0:T(8,128)(2,1)}, u32[]{:S(2)}) copy-start(bf16[256,128]{1,0:T(8,128)(2,1)} %constant.9.clone.table_low) | copy-start | bytes 196612
  55.3 35.4 %copy-start.1 = (bf16[256,256]{1,0:T(8,128)(2,1)S(1)}, bf16[256,256]{1,0:T(8,128)(2,1)}, u32[]{:S(2)}) copy-start(bf16[256,256]{1,0:T(8,128)(2,1)} %constant.10.clone.table_high) | copy-start | bytes 393220
  55.3 35.4 %copy-start.2 = (bf16[256,256]{1,0:T(8,128)(2,1)S(1)}, bf16[256,256]{1,0:T(8,128)(2,1)}, u32[]{:S(2)}) copy-start(bf16[256,256]{1,0:T(8,128)(2,1)} %constant.11.clone.table_low) | copy-start | bytes 393220
  61.7 7.8 %collective-permute-start.16 = (f32[32,128]{1,0:T(8,128)S(1)}, f32[32,128]{1,0:T(8,128)S(1)}, u32[]{:S(2)}, u32[]{:S(2)}) collective-permute-start(f32[32,128]{1,0:T(8,128)S(1)} %get-tuple-element.74), channel_id=1, source_target_pairs={{0,4},{4,0},{8,12},{12,8},{16,20},{20,16},{24,28},{28,24},{1,5},{5... | collective-permute-start | bytes 49160 | tf_op jit(solution)/shard_map/ppermute | solution.py:49
  61.7 7.8 %collective-permute-start.17 = (f32[32,128]{1,0:T(8,128)S(1)}, f32[32,128]{1,0:T(8,128)S(1)}, u32[]{:S(2)}, u32[]{:S(2)}) collective-permute-start(f32[32,128]{1,0:T(8,128)S(1)} %get-tuple-element.75), channel_id=1, source_target_pairs={{0,28},{4,8},{8,4},{12,16},{16,12},{20,24},{24,20},{28,0},{1,29},{... | collective-permute-start | bytes 49160 | tf_op jit(solution)/shard_map/ppermute | solution.py:49
  66.4 1.2 %collective-permute-start.18 = (f32[16,128]{1,0:T(8,128)S(1)}, f32[16,128]{1,0:T(8,128)S(1)}, u32[]{:S(2)}, u32[]{:S(2)}) collective-permute-start(f32[16,128]{1,0:T(8,128)S(1)} %get-tuple-element.76), channel_id=1, source_target_pairs={{0,1},{1,0},{2,3},{3,2},{4,5},{5,4},{6,7},{7,6},{8,9},{9,8},{10,11... | collective-permute-start | bytes 24584 | tf_op jit(solution)/shard_map/ppermute | solution.py:49
  66.4 3.1 %collective-permute-start.19 = (f32[16,128]{1,0:T(8,128)S(1)}, f32[16,128]{1,0:T(8,128)S(1)}, u32[]{:S(2)}, u32[]{:S(2)}) collective-permute-start(f32[16,128]{1,0:T(8,128)S(1)} %get-tuple-element.77), channel_id=1, source_target_pairs={{0,3},{1,2},{2,1},{3,0},{4,7},{5,6},{6,5},{7,4},{8,11},{9,10},{10,... | collective-permute-start | bytes 24584 | tf_op jit(solution)/shard_map/ppermute | solution.py:49
  69.7 3.8 %collective-permute-start.20 = (f32[32,512]{1,0:T(8,128)S(1)}, f32[32,512]{1,0:T(8,128)S(1)}, u32[]{:S(2)}, u32[]{:S(2)}) collective-permute-start(f32[32,512]{1,0:T(8,128)S(1)} %get-tuple-element.79), channel_id=1, source_target_pairs={{0,3},{1,2},{2,1},{3,0},{4,7},{5,6},{6,5},{7,4},{8,11},{9,10},{10,... | collective-permute-start | bytes 196616 | tf_op jit(solution)/shard_map/ppermute | solution.py:901
  70.0 5.6 %collective-permute-start.21 = (f32[32,512]{1,0:T(8,128)S(1)}, f32[32,512]{1,0:T(8,128)S(1)}, u32[]{:S(2)}, u32[]{:S(2)}) collective-permute-start(f32[32,512]{1,0:T(8,128)S(1)} %get-tuple-element.80), channel_id=1, source_target_pairs={{0,2},{1,3},{2,0},{3,1},{4,6},{5,7},{6,4},{7,5},{8,10},{9,11},{10,... | collective-permute-start | bytes 196616 | tf_op jit(solution)/shard_map/ppermute | solution.py:901
  71.9 3.7 %collective-permute-start.22 = (f32[32,512]{1,0:T(8,128)S(1)}, f32[32,512]{1,0:T(8,128)S(1)}, u32[]{:S(2)}, u32[]{:S(2)}) collective-permute-start(f32[32,512]{1,0:T(8,128)S(1)} %get-tuple-element.81), channel_id=1, source_target_pairs={{0,1},{1,0},{2,3},{3,2},{4,5},{5,4},{6,7},{7,6},{8,9},{9,8},{10,11... | collective-permute-start | bytes 196616 | tf_op jit(solution)/shard_map/ppermute | solution.py:901
  76.2 8.0 %collective-permute-start.23 = (f32[32,512]{1,0:T(8,128)S(1)}, f32[32,512]{1,0:T(8,128)S(1)}, u32[]{:S(2)}, u32[]{:S(2)}) collective-permute-start(f32[32,512]{1,0:T(8,128)S(1)} %get-tuple-element.83), channel_id=1, source_target_pairs={{0,28},{4,24},{8,20},{12,16},{16,12},{20,8},{24,4},{28,0},{1,29},{... | collective-permute-start | bytes 196616 | tf_op jit(solution)/shard_map/ppermute | solution.py:901
  78.9 6.9 %collective-permute-start.24 = (f32[32,512]{1,0:T(8,128)S(1)}, f32[32,512]{1,0:T(8,128)S(1)}, u32[]{:S(2)}, u32[]{:S(2)}) collective-permute-start(f32[32,512]{1,0:T(8,128)S(1)} %get-tuple-element.84), channel_id=1, source_target_pairs={{0,24},{4,28},{8,16},{12,20},{16,8},{20,12},{24,0},{28,4},{1,25},{... | collective-permute-start | bytes 196616 | tf_op jit(solution)/shard_map/ppermute | solution.py:901
  78.9 8.6 %collective-permute-start.25 = (f32[32,512]{1,0:T(8,128)S(1)}, f32[32,512]{1,0:T(8,128)S(1)}, u32[]{:S(2)}, u32[]{:S(2)}) collective-permute-start(f32[32,512]{1,0:T(8,128)S(1)} %get-tuple-element.85), channel_id=1, source_target_pairs={{0,20},{4,16},{8,28},{12,24},{16,4},{20,0},{24,12},{28,8},{1,21},{... | collective-permute-start | bytes 196616 | tf_op jit(solution)/shard_map/ppermute | solution.py:901
  78.9 11.3 %collective-permute-start.26 = (f32[32,512]{1,0:T(8,128)S(1)}, f32[32,512]{1,0:T(8,128)S(1)}, u32[]{:S(2)}, u32[]{:S(2)}) collective-permute-start(f32[32,512]{1,0:T(8,128)S(1)} %get-tuple-element.86), channel_id=1, source_target_pairs={{0,16},{4,20},{8,24},{12,28},{16,0},{20,4},{24,8},{28,12},{1,17},{... | collective-permute-start | bytes 196616 | tf_op jit(solution)/shard_map/ppermute | solution.py:901
  83.9 6.3 %collective-permute-start.27 = (f32[32,512]{1,0:T(8,128)S(1)}, f32[32,512]{1,0:T(8,128)S(1)}, u32[]{:S(2)}, u32[]{:S(2)}) collective-permute-start(f32[32,512]{1,0:T(8,128)S(1)} %get-tuple-element.87), channel_id=1, source_target_pairs={{0,12},{4,8},{8,4},{12,0},{16,28},{20,24},{24,20},{28,16},{1,13},{... | collective-permute-start | bytes 196616 | tf_op jit(solution)/shard_map/ppermute | solution.py:901
  84.2 6.5 %collective-permute-start.28 = (f32[32,512]{1,0:T(8,128)S(1)}, f32[32,512]{1,0:T(8,128)S(1)}, u32[]{:S(2)}, u32[]{:S(2)}) collective-permute-start(f32[32,512]{1,0:T(8,128)S(1)} %get-tuple-element.88), channel_id=1, source_target_pairs={{0,8},{4,12},{8,0},{12,4},{16,24},{20,28},{24,16},{28,20},{1,9},{5... | collective-permute-start | bytes 196616 | tf_op jit(solution)/shard_map/ppermute | solution.py:901
  85.8 4.9 %collective-permute-start.29 = (f32[32,512]{1,0:T(8,128)S(1)}, f32[32,512]{1,0:T(8,128)S(1)}, u32[]{:S(2)}, u32[]{:S(2)}) collective-permute-start(f32[32,512]{1,0:T(8,128)S(1)} %get-tuple-element.89), channel_id=1, source_target_pairs={{0,4},{4,0},{8,12},{12,8},{16,20},{20,16},{24,28},{28,24},{1,5},{5... | collective-permute-start | bytes 196616 | tf_op jit(solution)/shard_map/ppermute | solution.py:901

commit v3 on v2

--- a/solution.py
+++ b/solution.py
@@ -355,24 +355,9 @@
 
 
 def spread_rest_kernel(
-    layout,
-    facts,
-    saved_0,
-    saved_1,
-    push_0,
-    push_1,
-    before,
-    predicted,
-    velocity,
-    u_0,
-    u_1,
-    w_0,
-    w_1,
-    inner,
-    total,
-    high,
-    low,
+    layout, parts, facts, saved_0, saved_1, push_0, push_1, before, predicted, velocity, *refs
 ):
+    outs, (total, high, low, edges, whole) = refs[:parts], refs[parts:]
     size_x, size_z, size_y = layout.sizes
     total[...] = before[...]
     row = (0, 1, 2)
@@ -383,40 +368,52 @@
             part = jnp.transpose(total[c, :, q * LANES : (q + 1) * LANES])
             part = part.reshape(size_x // 2, size_z // 2, size_y)
             velocity[c, xs, zs] = predicted[c, xs, zs] + part
-    last = jnp.where(even("gx"), size_x - 1, 0)
-    u_0[...] = velocity[0, last]
-    u_1[...] = velocity[0, size_x - 1 - last]
-    choose = in_order("gz", (1, size_y))
-    for x in range(size_x):
-        first, last = velocity[2, x, 0:1], velocity[2, x, size_z - 1 : size_z]
-        w_0[x : x + 1], w_1[x : x + 1] = choose(first, last)
     row = lax.broadcasted_iota(jnp.int32, (size_z, size_y), 0)
     lane = lax.broadcasted_iota(jnp.int32, (size_z, size_y), 1)
+    group = LANES // size_z
+    for q in range(size_x // group):
+        pieces = []
+        for x in range(q * group, (q + 1) * group):
+            y_minus, y_plus = y_neighbours(velocity[1, x], lane, 0.0, 0.0)
+            z_minus, z_plus = z_neighbours(velocity[2, x], row, 0.0, 0.0)
+            change = y_plus - y_minus + z_plus - z_minus
+            if x > 0:
+                change -= velocity[0, x - 1]
+            if x < size_x - 1:
+                change += velocity[0, x + 1]
+            pieces.append(change * 0.5)
+        part = jnp.concatenate(pieces, axis=0)
+        whole[:, q * LANES : (q + 1) * LANES] = jnp.transpose(part)
+    edges[...] = jnp.zeros(edges.shape, jnp.float32)
+    edges[:size_z] = velocity[0, 0]
+    edges[size_z : 2 * size_z] = velocity[0, size_x - 1]
     for x in range(size_x):
-        y_minus, y_plus = y_neighbours(velocity[1, x], lane, 0.0, 0.0)
-        z_minus, z_plus = z_neighbours(velocity[2, x], row, 0.0, 0.0)
-        change = y_plus - y_minus + z_plus - z_minus
-        if x > 0:
-            change -= velocity[0, x - 1]
-        if x < size_x - 1:
-            change += velocity[0, x + 1]
-        inner[x] = change * 0.5
-
-
-def spread_rest(layout, facts, saved, pushes, before, predicted):
+        first = 2 * size_z + 2 * x
+        edges[first : first + 1] = velocity[2, x, 0:1]
+        edges[first + 1 : first + 2] = velocity[2, x, size_z - 1 : size_z]
+    whole[:, layout.plane :] = jnp.transpose(edges[...])
+    height = size_y // parts
+    for out, step in zip(outs, steps(parts)):
+        first = pl.multiple_of((lax.axis_index("gz") ^ step) * height, 8)
+        out[...] = whole[pl.ds(first, height), :]
+
+
+def spread_rest(layout, parts, facts, saved, pushes, before, predicted):
     size_x, size_z, size_y = layout.sizes
-    return call(
-        functools.partial(spread_rest_kernel, layout),
-        [float32(3, size_x, size_z, size_y)]
-        + [float32(size_z, size_y)] * 2
-        + [float32(size_x, size_y)] * 2
-        + [float32(size_x, size_z, size_y)],
+    assert 2 * size_z + 2 * size_x <= LANES
+    width = layout.plane + LANES
+    velocity, *pieces = call(
+        functools.partial(spread_rest_kernel, layout, parts),
+        [float32(3, size_x, size_z, size_y)] + [float32(size_y // parts, width)] * parts,
         [facts],
         [*saved, *pushes, before, predicted],
-        [pltpu.VMEM(before.shape, jnp.float32)] + weight_scratch(layout),
+        [pltpu.VMEM(before.shape, jnp.float32)]
+        + weight_scratch(layout)
+        + [pltpu.VMEM((LANES, size_y), jnp.float32), pltpu.VMEM((size_y, width), jnp.float32)],
         2 * visit_cost(layout, (0, 1, 2)),
         12 * before.size,
     )
+    return velocity, pieces
 
 
 def pack_kernel(
@@ -710,48 +707,8 @@
     )
 
 
-def divergence_kernel(sizes, parts, inner, u_0, u_1, w_0, w_1, *rest):
-    outs, whole = rest[:parts], rest[parts]
-    size_x, size_z, size_y = sizes
-    row = lax.broadcasted_iota(jnp.int32, (size_z, size_y), 0)
-    group = LANES // size_z
-    u_below, u_above = in_order("gx", u_0.shape)(u_0[...], u_1[...])
-    w_below, w_above = in_order("gz", w_0.shape)(w_0[...], w_1[...])
-    for q in range(size_x // group):
-        pieces = []
-        for x in range(q * group, (q + 1) * group):
-            piece = inner[x]
-            if x == 0:
-                piece -= 0.5 * u_below
-            if x == size_x - 1:
-                piece += 0.5 * u_above
-            piece -= jnp.where(row == 0, 0.5 * w_below[x : x + 1], 0.0)
-            piece += jnp.where(row == size_z - 1, 0.5 * w_above[x : x + 1], 0.0)
-            pieces.append(piece)
-        part = jnp.concatenate(pieces, axis=0)
-        whole[:, q * LANES : (q + 1) * LANES] = jnp.transpose(part)
-    height = size_y // parts
-    for out, step in zip(outs, steps(parts)):
-        first = pl.multiple_of((lax.axis_index("gz") ^ step) * height, 8)
-        out[...] = whole[pl.ds(first, height), :]
-
-
-def divergence(sizes, parts, inner, ghosts):
-    size_x, size_z, size_y = sizes
-    plane = size_x * size_z
-    return call(
-        functools.partial(divergence_kernel, sizes, parts),
-        [float32(size_y // parts, plane)] * parts,
-        [],
-        [inner, *ghosts],
-        [pltpu.VMEM((size_y, plane), jnp.float32)],
-        10 * inner.size,
-        8 * inner.size,
-    )
-
-
 def swap_groups(values, width):
-    count = LANES // width
+    count = len(values)
     lane = lax.broadcasted_iota(jnp.int32, values[0].shape, 1)
     values = list(values)
     step = count // 2
@@ -773,16 +730,35 @@
     pieces, refs = refs[:parts_z], refs[parts_z:]
     outs, (gathered, turned, whole) = refs[:parts_x], refs[parts_x:]
     height = size_y // parts_z
+    columns = height * size_x
     group = LANES // size_z
     for piece, step in zip(pieces, steps(parts_z)):
         gathered[lax.axis_index("gz") ^ step] = piece[...]
-    for block in range(parts_z // group):
+    lane = lax.broadcasted_iota(jnp.int32, (height, LANES), 1)
+    edges = [gathered[i, :, size_x * size_z :] for i in range(parts_z)]
+    blocks = parts_z // group
+    for block in range(blocks):
         for q in range(size_x // group):
             lanes = slice(q * LANES, (q + 1) * LANES)
             values = [gathered[block * group + i, :, lanes] for i in range(group)]
             for j, value in enumerate(swap_groups(values, size_z)):
                 turned[block, pl.ds(q * group + j, height, stride=size_x), :] = value
-    lines = jnp.concatenate([turned[b] for b in range(turned.shape[0])], axis=1)
+        for end in range(2):
+            layer = edges[block * group]
+            for i in range(group):
+                moved = (i - end) * size_z % LANES
+                part = edges[block * group + i]
+                part = pltpu.roll(part, moved, 1) if moved else part
+                layer = part if i == 0 else jnp.where(lane < i * size_z, layer, part)
+            turned[block, pl.ds(columns + end, height, stride=2), :] = layer
+    for x in range(size_x):
+        ends = jnp.zeros((height, LANES), jnp.float32)
+        for i in range(parts_z):
+            part = pltpu.roll(edges[i], (2 * i - 2 * size_z - 2 * x) % LANES, 1)
+            ends = jnp.where((lane >= 2 * i) & (lane < 2 * i + 2), part, ends)
+        turned[blocks, pl.ds(x, height, stride=size_x), :] = ends
+    turned[blocks, columns:] = jnp.zeros((2 * height, LANES), jnp.float32)
+    lines = jnp.concatenate([turned[b] for b in range(blocks + 1)], axis=1)
     high, low = split(lines)
     result = lax.dot_general(
         table_high[...], high, TRANSPOSED, preferred_element_type=jnp.float32
@@ -793,11 +769,21 @@
     result += lax.dot_general(
         table_high[...], low, TRANSPOSED, preferred_element_type=jnp.float32
     )
-    whole[...] = result
+    whole[:, columns:] = jnp.zeros((whole.shape[0], LANES), jnp.float32)
+    whole[:, : columns + 2 * height] = result
     rows = whole.shape[0] // parts_x
+    modes = rows // 2
+    lane = lax.broadcasted_iota(jnp.int32, (modes, LANES), 1)
     for out, step in zip(outs, steps(parts_x)):
         first = pl.multiple_of((lax.axis_index("gx") ^ step) * rows, 8)
-        out[...] = whole[pl.ds(first, rows), :]
+        for t in range(columns // LANES):
+            out[t * rows : (t + 1) * rows] = whole[
+                pl.ds(first, rows), t * LANES : (t + 1) * LANES
+            ]
+        real = whole[pl.ds(first, modes), columns : columns + LANES]
+        imag = whole[pl.ds(first + modes, modes), columns : columns + LANES]
+        imag = pltpu.roll(imag, 2 * height, 1)
+        out[columns // LANES * rows :] = jnp.where(lane < 2 * height, real, imag)
 
 
 def transform_z(sizes, counts, table, pieces):
@@ -806,17 +792,19 @@
     length_z = size_z * parts_z
     height = size_y // parts_z
     columns = height * size_x
+    assert 2 * parts_z <= LANES and 4 * height <= LANES
+    rows = 2 * length_z // parts_x
     return call(
         functools.partial(transform_z_kernel, sizes, counts),
-        [float32(2 * length_z // parts_x, columns)] * parts_x,
+        [float32(columns // LANES * rows + rows // 2, LANES)] * parts_x,
         [],
         [*table, *pieces],
         [
-            pltpu.VMEM((parts_z, height, size_x * size_z), jnp.float32),
-            pltpu.VMEM((length_z // LANES, columns, LANES), jnp.float32),
-            pltpu.VMEM((2 * length_z, columns), jnp.float32),
+            pltpu.VMEM((parts_z, *pieces[0].shape), jnp.float32),
+            pltpu.VMEM((length_z // LANES + 1, columns + 2 * height, LANES), jnp.float32),
+            pltpu.VMEM((2 * length_z, columns + LANES), jnp.float32),
         ],
-        12 * length_z * length_z * columns,
+        24 * length_z * length_z * columns,
         12 * length_z * columns,
     )
 
@@ -829,12 +817,15 @@
     modes = size_z * parts_z // parts_x
     height = size_y // parts_z
     group = LANES // size_x
+    rows = 2 * modes
+    main = height // group * rows
     for piece, step in zip(pieces, steps(parts_x)):
         gathered[lax.axis_index("gx") ^ step] = piece[...]
     for block in range(parts_x // group):
         for q in range(height // group):
-            lanes = slice(q * LANES, (q + 1) * LANES)
-            values = [gathered[block * group + i, :, lanes] for i in range(group)]
+            values = [
+                gathered[block * group + i, q * rows : (q + 1) * rows] for i in range(group)
+            ]
             for j, value in enumerate(swap_groups(values, size_x)):
                 first = (q * group + j) * modes
                 for c in range(2):
@@ -842,6 +833,15 @@
                     turned[first : first + modes, column : column + LANES] = value[
                         c * modes : (c + 1) * modes
                     ]
+        ends = [gathered[block * group + i, main:] for i in range(group)]
+        column = 2 * length_x + block * LANES
+        for j, value in enumerate(swap_groups(ends, 2)):
+            for q in range(height // group):
+                first = (q * group + j) * modes
+                moved = -2 * group * q % LANES
+                turned[first : first + modes, column : column + LANES] = (
+                    pltpu.roll(value, moved, 1) if moved else value
+                )
     high, low = split(turned[...])
     result = jnp.dot(high, table_high[...], preferred_element_type=jnp.float32)
     result += jnp.dot(low, table_high[...], preferred_element_type=jnp.float32)
@@ -863,7 +863,7 @@
         [*table, *pieces],
         [
             pltpu.VMEM((parts_x, *pieces[0].shape), jnp.float32),
-            pltpu.VMEM((height * modes, 2 * length_x), jnp.float32),
+            pltpu.VMEM((height * modes, table[0].shape[0]), jnp.float32),
         ],
         24 * length_x * length_x * height * modes,
         24 * length_x * height * modes,
@@ -882,16 +882,30 @@
     return np.cos(turn), np.sin(turn)
 
 
-def table_z(length, blocks):
+def table_z(length, blocks, parts):
     cosine, sine = angles(length)
-    modes = length // blocks
+    modes, size = length // blocks, length // parts
     table = np.stack([cosine, -sine]).reshape(2, blocks, modes, length)
-    return split_table(table.transpose(1, 0, 2, 3).reshape(2 * length, length))
-
-
-def table_x(length, scale):
+    table = table.transpose(1, 0, 2, 3).reshape(2 * length, length)
+    ends = np.zeros((2 * length, LANES))
+    for part in range(parts):
+        ends[:, 2 * part] = 0.5 * table[:, (part * size - 1) % length]
+        ends[:, 2 * part + 1] = -0.5 * table[:, (part + 1) * size % length]
+    return split_table(np.concatenate([table, ends], axis=1))
+
+
+def table_x(length, parts, height, scale):
     cosine, sine = angles(length)
-    return split_table(np.block([[cosine, -sine], [sine, cosine]]) * scale)
+    size = length // parts
+    group = LANES // size
+    table = np.block([[cosine, -sine], [sine, cosine]]) * scale
+    ends = np.zeros((parts // group * LANES, 2 * length))
+    for part in range(parts):
+        for c in range(2):
+            row = part // group * LANES + c * 2 * height + 2 * (part % group)
+            ends[row] = 0.5 * table[c * length + (part * size - 1) % length]
+            ends[row + 1] = -0.5 * table[c * length + (part + 1) * size % length]
+    return split_table(np.concatenate([table, ends], axis=0))
 
 
 def exchange(pieces, axis):
@@ -907,7 +921,7 @@
     flow_state, slot_ids, corners, marker_cells, marker_frac, particle_velocity, particle_spin
 ):
     sizes = flow_state.shape[1:]
-    size_x, size_z, _ = sizes
+    size_x, size_z, size_y = sizes
     counts = (lax.axis_size("gx"), lax.axis_size("gz"))
     length_x, length_z = (size_x * counts[0], size_z * counts[1])
     slots, markers = marker_cells.shape[1:]
@@ -942,17 +956,16 @@
     rows_push = swap(row_push, "gz", 0), swap(row_push, "gz", 1)
     forcing = spread_own(layout, facts, own_saved, push)
     forcing = spread_side(layout, facts, side_saved, row_push, forcing)
-    velocity, u_0, u_1, w_0, w_1, change = spread_rest(
-        layout, facts, rows_saved, rows_push, forcing, predicted
-    )
-
-    ghosts = (swap(u_0, "gx", 0), swap(u_1, "gx", 1), swap(w_0, "gz", 0), swap(w_1, "gz", 1))
-    pieces = divergence(sizes, counts[1], change, ghosts)
+    velocity, pieces = spread_rest(
+        layout, counts[1], facts, rows_saved, rows_push, forcing, predicted
+    )
+
     pieces = exchange(pieces, "gz")
-    pieces = transform_z(sizes, counts, table_z(length_z, counts[0]), pieces)
+    pieces = transform_z(sizes, counts, table_z(length_z, *counts), pieces)
     pieces = exchange(pieces, "gx")
     scale = 1.0 / math.sqrt(length_x * length_z)
-    source = transform_x(sizes, counts, table_x(length_x, scale), pieces)
+    table = table_x(length_x, counts[0], size_y // counts[1], scale)
+    source = transform_x(sizes, counts, table, pieces)
     return velocity, source
 
 

time: 92.5 us -> 86.9 us (0.939)
  starting transfers between devices: 37.6 us -> 33.4 us
  waiting for transfers between devices: 26.6 us -> 24.6 us
    ppermute x20 -> x16, starting transfers between devices: 25.2 us -> 20.3 us  [swap(): return lax.ppermute(array, axis, pairs)]
    ppermute x20 -> x16, waiting for transfers between devices: 18.7 us -> 15.8 us  [swap(): return lax.ppermute(array, axis, pairs)]
    pallas_call x13 -> x12, Pallas kernels: 23 us -> 23.8 us  [call(): pl.pallas_call(kernel, out_shape=out_shape, in_specs=[IN_SMEM] * len(scal...]
  transfers between devices with their start and end apart: 30 -> 26, of which waited for: 16 -> 14; matrix products, arithmetic and copies ran while one was open for 0% -> 0% of each run, Pallas kernels for 10% -> 10%
where the time goes in v3:
time: 86.9 us; the launch traced here: 86.7 us
  starting transfers between devices  33.4 us (38%)
  Pallas kernels  25.8 us (30%)
  waiting for transfers between devices  24.6 us (28%)
  local copies, waits for them, and re-layouts  2.05 us (2%)
    pallas_call x12, Pallas kernels, call(): pl.pallas_call(kernel, out_shape=out_shape, in_specs=[IN_SMEM] * len(scal...  23.8 us
    ppermute x16, starting transfers between devices, swap(): return lax.ppermute(array, axis, pairs)  20.3 us
    ppermute x16, waiting for transfers between devices, swap(): return lax.ppermute(array, axis, pairs)  15.8 us
    ppermute x10, starting transfers between devices, exchange(): lax.ppermute(piece, axis, [(i, i ^ step) for i in range(devices)])  13.1 us
    ppermute x10, waiting for transfers between devices, exchange(): lax.ppermute(piece, axis, [(i, i ^ step) for i in range(devices)])  8.76 us
    pallas_call x1, Pallas kernels, pack(): pl.pallas_call(functools.partial(pack_kernel, layout), out_shape=[float32...  2.06 us
    unnamed x16, local copies, waits for them, and re-layouts  2.05 us
  transfers between devices with their start and end apart: 26, of which 14 were waited for; matrix products, arithmetic and copies ran while one was open for 0% of the time, Pallas kernels for 10%

profile of v3, /device:TPU:0, one launch (start us, length us, event | category | flops | bytes accessed | tf_op | source)
XLA Modules:
  0.0 86.7 jit_solution(13036161124360063156)
XLA Ops:
  0.6 2.1 %pack.1 = (f32[104,128]{1,0:T(8,128)}, f32[128,128]{1,0:T(8,128)}, f32[128,128]{1,0:T(8,128)}, f32[168,128]{1,0:T(8,128)}, f32[168,128]{1,0:T(8,128)}) custom-call(s32[8]{0:T(128)} %slot_ids_hbm.1, s32[3,8]{1,0:T(4,128)} %corners_hbm.1, f32[4,16,32,128]{3,2,1,0:T(8,128)} %flow.3, s32[3,8,512]{2,1,0:T(8,128)} %cells_hbm.1, f32[3,8,512]{2,1,0:T(8,128)} %fraction_hbm.1), custom_call_target="tpu_custom_call" | custom-call | flops 262144 | bytes 262144 | tf_op jit(solution)/shard_map/pack/pallas_call | solution.py:495
  2.7 3.1 %collective-permute-start = (f32[104,128]{1,0:T(8,128)}, f32[104,128]{1,0:T(8,128)S(1)}, u32[]{:S(2)}, u32[]{:S(2)}) collective-permute-start(f32[104,128]{1,0:T(8,128)} %get-tuple-element.41.own), channel_id=1, source_target_pairs={{0,4},{4,0},{8,12},{12,8},{16,20},{20,16},{24,28},{28,24},{1,5},{5... | collective-permute-start | bytes 159752 | tf_op jit(solution)/shard_map/ppermute | solution.py:49
  5.8 3.5 %collective-permute-start.1 = (f32[104,128]{1,0:T(8,128)}, f32[104,128]{1,0:T(8,128)S(1)}, u32[]{:S(2)}, u32[]{:S(2)}) collective-permute-start(f32[104,128]{1,0:T(8,128)} %get-tuple-element.41.own), channel_id=1, source_target_pairs={{0,28},{4,8},{8,4},{12,16},{16,12},{20,24},{24,20},{28,0},{1,29},{... | collective-permute-start | bytes 159752 | tf_op jit(solution)/shard_map/ppermute | solution.py:49
  9.3 3.5 %collective-permute-done.1.right.side_1 = f32[104,128]{1,0:T(8,128)S(1)} collective-permute-done((f32[104,128]{1,0:T(8,128)}, f32[104,128]{1,0:T(8,128)S(1)}, u32[]{:S(2)}, u32[]{:S(2)}) %collective-permute-start.1) | collective-permute-done | bytes 53280 | tf_op jit(solution)/shard_map/ppermute | solution.py:49
  12.8 0.1 collective-permute-start.4
  12.9 1.6 %collective-permute-start.5 = (f32[208,128]{1,0:T(8,128)S(1)}, f32[208,128]{1,0:T(8,128)S(1)}, u32[]{:S(2)}, u32[]{:S(2)}) collective-permute-start(f32[208,128]{1,0:T(8,128)S(1)} %shard_map.123), channel_id=1, source_target_pairs={{0,3},{1,2},{2,1},{3,0},{4,7},{5,6},{6,5},{7,4},{8,11},{9,10},{10,... | collective-permute-start | bytes 319496 | tf_op jit(solution)/shard_map/ppermute | solution.py:49
  14.5 0.1 collective-permute-start.2
  14.6 0.6 collective-permute-start.3
  15.1 3.5 %collective-permute-start.7 = (f32[128,128]{1,0:T(8,128)}, f32[128,128]{1,0:T(8,128)S(1)}, u32[]{:S(2)}, u32[]{:S(2)}) collective-permute-start(f32[128,128]{1,0:T(8,128)} %get-tuple-element.54), channel_id=1, source_target_pairs={{0,28},{4,8},{8,4},{12,16},{16,12},{20,24},{24,20},{28,0},{1,29},{... | collective-permute-start | bytes 196616 | tf_op jit(solution)/shard_map/ppermute | solution.py:49
  18.7 1.2 %copy-done = f32[4,16,32,128]{3,2,1,0:T(8,128)S(1)} copy-done((f32[4,16,32,128]{3,2,1,0:T(8,128)S(1)}, f32[4,16,32,128]{3,2,1,0:T(8,128)}, u32[]{:S(2)}) %copy-start) | copy-done | bytes 1048600
  19.9 0.8 copy-done.3
  20.7 0.9 %shard_map.122 = (f32[3,16,32,128]{3,2,1,0:T(8,128)S(1)}, f32[32,128]{1,0:T(8,128)S(1)}, f32[32,128]{1,0:T(8,128)S(1)}, f32[16,128]{1,0:T(8,128)S(1)}, f32[16,128]{1,0:T(8,128)S(1)}, /*index=5*/f32[104,128]{1,0:T(8,128)S(1)}) custom-call(f32[4,16,32,128]{3,2,1,0:T(8,128)S(1)} %copy-done, f32[104,128]{1,0:T(8,128)S(1)} %copy-done.3), custom_call_target="tpu_custom_call" | custom-call | flops 52428800 | bytes 2097152 | tf_op jit(solution)/shard_map/pallas_call | solution.py:35
  21.6 0.7 collective-permute-done.7.x_1
  22.3 0.3 shard_map.125
  22.7 0.1 shard_map.124
  22.8 5.3 %shard_map.126 = (f32[3,24,512]{2,1,0:T(8,128)S(1)}, f32[3,24,512]{2,1,0:T(8,128)S(1)}, f32[24,80,512]{2,1,0:T(8,128)S(1)}, f32[24,80,512]{2,1,0:T(8,128)S(1)}) custom-call(s32[8,128]{1,0:T(8,128)S(1)} %get-tuple-element.45.facts, f32[312,128]{1,0:T(8,128)S(1)} %get-tuple-element.46.refs_0_, f32[312,128]{1,0:T(8,128)S(1)} %get-tuple-element.47.refs_1_, ...), custom_call_target="tpu_custom_call" | custom-call | flops 7247757312 | bytes 1572864 | tf_op jit(solution)/shard_map/pallas_call | solution.py:35
  28.1 0.1 collective-permute-start.8
  28.1 0.1 collective-permute-start.9
  28.2 2.8 %shard_map.128 = (f32[3,16,512]{2,1,0:T(8,128)S(1)}, f32[16,80,512]{2,1,0:T(8,128)S(1)}) custom-call(s32[8,128]{1,0:T(8,128)S(1)} %get-tuple-element.45.facts, f32[312,128]{1,0:T(8,128)S(1)} %get-tuple-element.59.refs_0_, f32[3,128,512]{2,1,0:T(8,128)S(1)} %get-tuple-element.55.refs_2_.refs_1_, f32[3,128,512]{2,1,0:T(8,128)S(1)} %get-tuple-element.56.refs_3_.refs_2_), custom_call_target="tpu_custom_call" | custom-call | flops 2415919104 | bytes 1572864 | tf_op jit(solution)/shard_map/pallas_call | solution.py:35
  31.1 2.6 %collective-permute-done.9 = f32[3,24,512]{2,1,0:T(8,128)S(1)} collective-permute-done((f32[3,24,512]{2,1,0:T(8,128)S(1)}, f32[3,24,512]{2,1,0:T(8,128)S(1)}, u32[]{:S(2)}, u32[]{:S(2)}) %collective-permute-start.9) | collective-permute-done | bytes 147488 | tf_op jit(solution)/shard_map/ppermute | solution.py:49
  33.8 3.8 %collective-permute-start.11 = (f32[3,8,512]{2,1,0:T(8,128)S(1)}, f32[3,8,512]{2,1,0:T(8,128)S(1)}, u32[]{:S(2)}, u32[]{:S(2)}) collective-permute-start(f32[3,8,512]{2,1,0:T(8,128)S(1)} %get-tuple-element.81), channel_id=1, source_target_pairs={{0,28},{4,8},{8,4},{12,16},{16,12},{20,24},{24,20},{28,0},{1,29},{... | collective-permute-start | bytes 147464 | tf_op jit(solution)/shard_map/ppermute | solution.py:49
  37.6 1.0 %shard_map.127 = (f32[3,8,512]{2,1,0:T(8,128)S(1)}, f32[8,80,512]{2,1,0:T(8,128)S(1)}) custom-call(s32[8,128]{1,0:T(8,128)S(1)} %get-tuple-element.45.facts, f32[312,128]{1,0:T(8,128)S(1)} %get-tuple-element.59.refs_0_, f32[3,128,512]{2,1,0:T(8,128)S(1)} %get-tuple-element.55.refs_2_.refs_1_, f32[3,128,512]{2,1,0:T(8,128)S(1)} %get-tuple-element.56.refs_3_.refs_2_, ...), custom_call_target="tpu_custom_call" | custom-call | flops 1207959552 | bytes 1572864 | tf_op jit(solution)/shard_map/pallas_call | solution.py:35
  38.5 2.5 %collective-permute-done.11 = f32[3,8,512]{2,1,0:T(8,128)S(1)} collective-permute-done((f32[3,8,512]{2,1,0:T(8,128)S(1)}, f32[3,8,512]{2,1,0:T(8,128)S(1)}, u32[]{:S(2)}, u32[]{:S(2)}) %collective-permute-start.11) | collective-permute-done | bytes 49184 | tf_op jit(solution)/shard_map/ppermute | solution.py:49
  41.1 0.6 collective-permute-done.10
  41.7 2.7 %collective-permute-start.13 = (f32[3,8,512]{2,1,0:T(8,128)S(1)}, f32[3,8,512]{2,1,0:T(8,128)S(1)}, u32[]{:S(2)}, u32[]{:S(2)}) collective-permute-start(f32[3,8,512]{2,1,0:T(8,128)S(1)} %fusion.1.push), channel_id=1, source_target_pairs={{0,28},{4,8},{8,4},{12,16},{16,12},{20,24},{24,20},{28,0},{1,29},{... | collective-permute-start | bytes 147464 | tf_op jit(solution)/shard_map/ppermute | solution.py:49
  44.4 1.0 %shard_map.129.before = f32[3,128,512]{2,1,0:T(8,128)S(1)} custom-call(s32[8,128]{1,0:T(8,128)S(1)} %get-tuple-element.45.facts, f32[8,80,512]{2,1,0:T(8,128)S(1)} %get-tuple-element.65.saved, f32[3,8,512]{2,1,0:T(8,128)S(1)} %fusion.1.push), custom_call_target="tpu_custom_call" | custom-call | flops 1207959552 | bytes 786432 | tf_op jit(solution)/shard_map/pallas_call | solution.py:35
  45.4 3.3 %collective-permute-done.13 = f32[3,8,512]{2,1,0:T(8,128)S(1)} collective-permute-done((f32[3,8,512]{2,1,0:T(8,128)S(1)}, f32[3,8,512]{2,1,0:T(8,128)S(1)}, u32[]{:S(2)}, u32[]{:S(2)}) %collective-permute-start.13) | collective-permute-done | bytes 49184 | tf_op jit(solution)/shard_map/ppermute | solution.py:49
  48.7 0.9 %collective-permute-done.12 = f32[3,8,512]{2,1,0:T(8,128)S(1)} collective-permute-done((f32[3,8,512]{2,1,0:T(8,128)S(1)}, f32[3,8,512]{2,1,0:T(8,128)S(1)}, u32[]{:S(2)}, u32[]{:S(2)}) %collective-permute-start.12) | collective-permute-done | bytes 49184 | tf_op jit(solution)/shard_map/ppermute | solution.py:49
  49.7 1.1 %collective-permute-start.15 = (f32[3,24,512]{2,1,0:T(8,128)S(1)}, f32[3,24,512]{2,1,0:T(8,128)S(1)}, u32[]{:S(2)}, u32[]{:S(2)}) collective-permute-start(f32[3,24,512]{2,1,0:T(8,128)S(1)} %pad_maximum_fusion.push), channel_id=1, source_target_pairs={{0,3},{1,2},{2,1},{3,0},{4,7},{5,6},{6,5},{7,4},{8,11},{9,10},{10,... | collective-permute-start | bytes 442376 | tf_op jit(solution)/shard_map/ppermute | solution.py:49
  50.8 2.8 %shard_map.130.before = f32[3,128,512]{2,1,0:T(8,128)S(1)} custom-call(s32[8,128]{1,0:T(8,128)S(1)} %get-tuple-element.45.facts, f32[16,80,512]{2,1,0:T(8,128)S(1)} %get-tuple-element.64.saved, f32[3,24,512]{2,1,0:T(8,128)S(1)} %pad_maximum_fusion.push, f32[3,128,512]{2,1,0:T(8,128)S(1)} %shard_map.129.before), custom_call_target="tpu_custom_call" | custom-call | flops 2415919104 | bytes 1572864 | tf_op jit(solution)/shard_map/pallas_call | solution.py:35
  53.7 1.6 %collective-permute-done.15.push_1 = f32[3,24,512]{2,1,0:T(8,128)S(1)} collective-permute-done((f32[3,24,512]{2,1,0:T(8,128)S(1)}, f32[3,24,512]{2,1,0:T(8,128)S(1)}, u32[]{:S(2)}, u32[]{:S(2)}) %collective-permute-start.15) | collective-permute-done | bytes 147488 | tf_op jit(solution)/shard_map/ppermute | solution.py:49
  55.3 6.6 %shard_map.131 = (f32[3,16,32,128]{3,2,1,0:T(8,128)}, f32[32,640]{1,0:T(8,128)S(1)}, f32[32,640]{1,0:T(8,128)S(1)}, f32[32,640]{1,0:T(8,128)S(1)}, f32[32,640]{1,0:T(8,128)S(1)}) custom-call(s32[8,128]{1,0:T(8,128)S(1)} %get-tuple-element.45.facts, f32[24,80,512]{2,1,0:T(8,128)S(1)} %get-tuple-element.57.saved_0, ...), custom_call_target="tpu_custom_call" | custom-call | flops 7247757312 | bytes 2359296 | tf_op jit(solution)/shard_map/pallas_call | solution.py:35
  61.9 1.3 %collective-permute-start.17 = (f32[32,640]{1,0:T(8,128)S(1)}, f32[32,640]{1,0:T(8,128)S(1)}, u32[]{:S(2)}, u32[]{:S(2)}) collective-permute-start(f32[32,640]{1,0:T(8,128)S(1)} %get-tuple-element.70), channel_id=1, source_target_pairs={{0,2},{1,3},{2,0},{3,1},{4,6},{5,7},{6,4},{7,5},{8,10},{9,11},{10,... | collective-permute-start | bytes 245768 | tf_op jit(solution)/shard_map/ppermute | solution.py:915
  63.1 0.6 collective-permute-start.18
  63.8 2.9 %collective-permute-done.16.refs_1_ = f32[32,640]{1,0:T(8,128)S(1)} collective-permute-done((f32[32,640]{1,0:T(8,128)S(1)}, f32[32,640]{1,0:T(8,128)S(1)}, u32[]{:S(2)}, u32[]{:S(2)}) %collective-permute-start.16) | collective-permute-done | bytes 81952 | tf_op jit(solution)/shard_map/ppermute | solution.py:915
  66.6 1.4 %collective-permute-done.17.refs_2_ = f32[32,640]{1,0:T(8,128)S(1)} collective-permute-done((f32[32,640]{1,0:T(8,128)S(1)}, f32[32,640]{1,0:T(8,128)S(1)}, u32[]{:S(2)}, u32[]{:S(2)}) %collective-permute-start.17) | collective-permute-done | bytes 81952 | tf_op jit(solution)/shard_map/ppermute | solution.py:915
  68.0 1.1 %shard_map.132 = (f32[144,128]{1,0:T(8,128)S(1)}, f32[144,128]{1,0:T(8,128)S(1)}, f32[144,128]{1,0:T(8,128)S(1)}, f32[144,128]{1,0:T(8,128)S(1)}, f32[144,128]{1...) custom-call(bf16[256,256]{1,0:T(8,128)(2,1)S(1)} %copy-done.6, ...), custom_call_target="tpu_custom_call" | custom-call | flops 201326592 | bytes 786432 | tf_op jit(solution)/shard_map/pallas_call | solution.py:35
  69.1 2.9 %collective-permute-start.19 = (f32[144,128]{1,0:T(8,128)S(1)}, f32[144,128]{1,0:T(8,128)S(1)}, u32[]{:S(2)}, u32[]{:S(2)}) collective-permute-start(f32[144,128]{1,0:T(8,128)S(1)} %get-tuple-element.73), channel_id=1, source_target_pairs={{0,28},{4,24},{8,20},{12,16},{16,12},{20,8},{24,4},{28,0},{1,29},{... | collective-permute-start | bytes 221192 | tf_op jit(solution)/shard_map/ppermute | solution.py:915
  72.0 1.4 %collective-permute-start.20 = (f32[144,128]{1,0:T(8,128)S(1)}, f32[144,128]{1,0:T(8,128)S(1)}, u32[]{:S(2)}, u32[]{:S(2)}) collective-permute-start(f32[144,128]{1,0:T(8,128)S(1)} %get-tuple-element.74), channel_id=1, source_target_pairs={{0,24},{4,28},{8,16},{12,20},{16,8},{20,12},{24,0},{28,4},{1,25},{... | collective-permute-start | bytes 221192 | tf_op jit(solution)/shard_map/ppermute | solution.py:915
  73.5 3.3 %collective-permute-start.22 = (f32[144,128]{1,0:T(8,128)S(1)}, f32[144,128]{1,0:T(8,128)S(1)}, u32[]{:S(2)}, u32[]{:S(2)}) collective-permute-start(f32[144,128]{1,0:T(8,128)S(1)} %get-tuple-element.76), channel_id=1, source_target_pairs={{0,16},{4,20},{8,24},{12,28},{16,0},{20,4},{24,8},{28,12},{1,17},{... | collective-permute-start | bytes 221192 | tf_op jit(solution)/shard_map/ppermute | solution.py:915
  76.8 0.5 collective-permute-start.23
  77.3 2.0 %collective-permute-start.24 = (f32[144,128]{1,0:T(8,128)S(1)}, f32[144,128]{1,0:T(8,128)S(1)}, u32[]{:S(2)}, u32[]{:S(2)}) collective-permute-start(f32[144,128]{1,0:T(8,128)S(1)} %get-tuple-element.78), channel_id=1, source_target_pairs={{0,8},{4,12},{8,0},{12,4},{16,24},{20,28},{24,16},{28,20},{1,9},{5... | collective-permute-start | bytes 221192 | tf_op jit(solution)/shard_map/ppermute | solution.py:915
  79.3 1.0 %collective-permute-start.25 = (f32[144,128]{1,0:T(8,128)S(1)}, f32[144,128]{1,0:T(8,128)S(1)}, u32[]{:S(2)}, u32[]{:S(2)}) collective-permute-start(f32[144,128]{1,0:T(8,128)S(1)} %get-tuple-element.79), channel_id=1, source_target_pairs={{0,4},{4,0},{8,12},{12,8},{16,20},{20,16},{24,28},{28,24},{1,5},{5... | collective-permute-start | bytes 221192 | tf_op jit(solution)/shard_map/ppermute | solution.py:915
  80.3 2.9 %collective-permute-done.21.refs_3_ = f32[144,128]{1,0:T(8,128)S(1)} collective-permute-done((f32[144,128]{1,0:T(8,128)S(1)}, f32[144,128]{1,0:T(8,128)S(1)}, u32[]{:S(2)}, u32[]{:S(2)}) %collective-permute-start.21) | collective-permute-done | bytes 73760 | tf_op jit(solution)/shard_map/ppermute | solution.py:915
  83.2 0.8 collective-permute-done.22.refs_4_
  84.0 0.3 collective-permute-done.23.refs_5_
  84.3 0.5 collective-permute-done.24.refs_6_
  84.8 1.8 %shard_map.133 = f32[2,32,16,128]{3,2,1,0:T(8,128)} custom-call(bf16[384,256]{1,0:T(8,128)(2,1)S(1)} %copy-done.1, bf16[384,256]{1,0:T(8,128)(2,1)S(1)} %copy-done.2, f32[144,128]{1,0:T(8,128)S(1)} %get-tuple-element.72.refs_0_, f32[144,128]{1,0:T(8,128)S(1)} %collective-permute-done.19.refs_1_, f32[144,128]{1,0:T(8,128)S(1)} %collective-permute-done.20.refs_2_, ...), custom_call_target="tpu_custom_call" | custom-call | flops 201326592 | bytes 1572864 | tf_op jit(solution)/shard_map/pallas_call | solution.py:35
  (37 shorter events, 0.2 us)
Async XLA Ops:
  2.7 6.6 %collective-permute-start = (f32[104,128]{1,0:T(8,128)}, f32[104,128]{1,0:T(8,128)S(1)}, u32[]{:S(2)}, u32[]{:S(2)}) collective-permute-start(f32[104,128]{1,0:T(8,128)} %get-tuple-element.41.own), channel_id=1, source_target_pairs={{0,4},{4,0},{8,12},{12,8},{16,20},{20,16},{24,28},{28,24},{1,5},{5... | collective-permute-start | bytes 159752 | tf_op jit(solution)/shard_map/ppermute | solution.py:49
  5.8 7.0 %collective-permute-start.1 = (f32[104,128]{1,0:T(8,128)}, f32[104,128]{1,0:T(8,128)S(1)}, u32[]{:S(2)}, u32[]{:S(2)}) collective-permute-start(f32[104,128]{1,0:T(8,128)} %get-tuple-element.41.own), channel_id=1, source_target_pairs={{0,28},{4,8},{8,4},{12,16},{16,12},{20,24},{24,20},{28,0},{1,29},{... | collective-permute-start | bytes 159752 | tf_op jit(solution)/shard_map/ppermute | solution.py:49
  9.3 5.8 %collective-permute-start.6 = (f32[128,128]{1,0:T(8,128)}, f32[128,128]{1,0:T(8,128)S(1)}, u32[]{:S(2)}, u32[]{:S(2)}) collective-permute-start(f32[128,128]{1,0:T(8,128)} %get-tuple-element.53), channel_id=1, source_target_pairs={{0,4},{4,0},{8,12},{12,8},{16,20},{20,16},{24,28},{28,24},{1,5},{5... | collective-permute-start | bytes 196616 | tf_op jit(solution)/shard_map/ppermute | solution.py:49
  12.8 9.8 %collective-permute-start.4 = (f32[208,128]{1,0:T(8,128)S(1)}, f32[208,128]{1,0:T(8,128)S(1)}, u32[]{:S(2)}, u32[]{:S(2)}) collective-permute-start(f32[208,128]{1,0:T(8,128)S(1)} %shard_map.123), channel_id=1, source_target_pairs={{0,1},{1,0},{2,3},{3,2},{4,5},{5,4},{6,7},{7,6},{8,9},{9,8},{10,11... | collective-permute-start | bytes 319496 | tf_op jit(solution)/shard_map/ppermute | solution.py:49
  12.9 9.8 %collective-permute-start.5 = (f32[208,128]{1,0:T(8,128)S(1)}, f32[208,128]{1,0:T(8,128)S(1)}, u32[]{:S(2)}, u32[]{:S(2)}) collective-permute-start(f32[208,128]{1,0:T(8,128)S(1)} %shard_map.123), channel_id=1, source_target_pairs={{0,3},{1,2},{2,1},{3,0},{4,7},{5,6},{6,5},{7,4},{8,11},{9,10},{10,... | collective-permute-start | bytes 319496 | tf_op jit(solution)/shard_map/ppermute | solution.py:49
  14.5 7.8 %collective-permute-start.2 = (f32[168,128]{1,0:T(8,128)}, f32[168,128]{1,0:T(8,128)S(1)}, u32[]{:S(2)}, u32[]{:S(2)}) collective-permute-start(f32[168,128]{1,0:T(8,128)} %get-tuple-element.43), channel_id=1, source_target_pairs={{0,1},{1,0},{2,3},{3,2},{4,5},{5,4},{6,7},{7,6},{8,9},{9,8},{10,11... | collective-permute-start | bytes 258056 | tf_op jit(solution)/shard_map/ppermute | solution.py:49
  14.6 7.8 %collective-permute-start.3 = (f32[168,128]{1,0:T(8,128)}, f32[168,128]{1,0:T(8,128)S(1)}, u32[]{:S(2)}, u32[]{:S(2)}) collective-permute-start(f32[168,128]{1,0:T(8,128)} %get-tuple-element.44), channel_id=1, source_target_pairs={{0,3},{1,2},{2,1},{3,0},{4,7},{5,6},{6,5},{7,4},{8,11},{9,10},{10,... | collective-permute-start | bytes 258056 | tf_op jit(solution)/shard_map/ppermute | solution.py:49
  15.1 7.2 %collective-permute-start.7 = (f32[128,128]{1,0:T(8,128)}, f32[128,128]{1,0:T(8,128)S(1)}, u32[]{:S(2)}, u32[]{:S(2)}) collective-permute-start(f32[128,128]{1,0:T(8,128)} %get-tuple-element.54), channel_id=1, source_target_pairs={{0,28},{4,8},{8,4},{12,16},{16,12},{20,24},{24,20},{28,0},{1,29},{... | collective-permute-start | bytes 196616 | tf_op jit(solution)/shard_map/ppermute | solution.py:49
  18.7 1.2 %copy-start = (f32[4,16,32,128]{3,2,1,0:T(8,128)S(1)}, f32[4,16,32,128]{3,2,1,0:T(8,128)}, u32[]{:S(2)}) copy-start(f32[4,16,32,128]{3,2,1,0:T(8,128)} %flow.3) | copy-start | bytes 3145732
  19.9 0.8 copy-start.3
  28.1 3.0 %collective-permute-start.8 = (f32[3,24,512]{2,1,0:T(8,128)S(1)}, f32[3,24,512]{2,1,0:T(8,128)S(1)}, u32[]{:S(2)}, u32[]{:S(2)}) collective-permute-start(f32[3,24,512]{2,1,0:T(8,128)S(1)} %get-tuple-element.61), channel_id=1, source_target_pairs={{0,1},{1,0},{2,3},{3,2},{4,5},{5,4},{6,7},{7,6},{8,9},{9,8},{10,11... | collective-permute-start | bytes 442376 | tf_op jit(solution)/shard_map/ppermute | solution.py:49
  28.1 5.6 %collective-permute-start.9 = (f32[3,24,512]{2,1,0:T(8,128)S(1)}, f32[3,24,512]{2,1,0:T(8,128)S(1)}, u32[]{:S(2)}, u32[]{:S(2)}) collective-permute-start(f32[3,24,512]{2,1,0:T(8,128)S(1)} %get-tuple-element.62), channel_id=1, source_target_pairs={{0,3},{1,2},{2,1},{3,0},{4,7},{5,6},{6,5},{7,4},{8,11},{9,10},{10,... | collective-permute-start | bytes 442376 | tf_op jit(solution)/shard_map/ppermute | solution.py:49
  28.2 9.3 %copy-start.4 = (f32[3,128]{1,0:T(4,128)S(1)}, f32[3,128]{1,0:T(4,128)}, u32[]{:S(2)}) copy-start(f32[3,128]{1,0:T(4,128)} %refs_3_.1) | copy-start | bytes 4612
  28.2 9.3 %copy-start.5 = (f32[3,128]{1,0:T(4,128)S(1)}, f32[3,128]{1,0:T(4,128)}, u32[]{:S(2)}) copy-start(f32[3,128]{1,0:T(4,128)} %refs_4_.1) | copy-start | bytes 4612
  33.8 7.3 %collective-permute-start.11 = (f32[3,8,512]{2,1,0:T(8,128)S(1)}, f32[3,8,512]{2,1,0:T(8,128)S(1)}, u32[]{:S(2)}, u32[]{:S(2)}) collective-permute-start(f32[3,8,512]{2,1,0:T(8,128)S(1)} %get-tuple-element.81), channel_id=1, source_target_pairs={{0,28},{4,8},{8,4},{12,16},{16,12},{20,24},{24,20},{28,0},{1,29},{... | collective-permute-start | bytes 147464 | tf_op jit(solution)/shard_map/ppermute | solution.py:49
  37.6 4.2 %collective-permute-start.10 = (f32[3,8,512]{2,1,0:T(8,128)S(1)}, f32[3,8,512]{2,1,0:T(8,128)S(1)}, u32[]{:S(2)}, u32[]{:S(2)}) collective-permute-start(f32[3,8,512]{2,1,0:T(8,128)S(1)} %get-tuple-element.80), channel_id=1, source_target_pairs={{0,4},{4,0},{8,12},{12,8},{16,20},{20,16},{24,28},{28,24},{1,5},{5... | collective-permute-start | bytes 147464 | tf_op jit(solution)/shard_map/ppermute | solution.py:49
  41.7 7.0 %collective-permute-start.13 = (f32[3,8,512]{2,1,0:T(8,128)S(1)}, f32[3,8,512]{2,1,0:T(8,128)S(1)}, u32[]{:S(2)}, u32[]{:S(2)}) collective-permute-start(f32[3,8,512]{2,1,0:T(8,128)S(1)} %fusion.1.push), channel_id=1, source_target_pairs={{0,28},{4,8},{8,4},{12,16},{16,12},{20,24},{24,20},{28,0},{1,29},{... | collective-permute-start | bytes 147464 | tf_op jit(solution)/shard_map/ppermute | solution.py:49
  44.4 5.1 %collective-permute-start.12 = (f32[3,8,512]{2,1,0:T(8,128)S(1)}, f32[3,8,512]{2,1,0:T(8,128)S(1)}, u32[]{:S(2)}, u32[]{:S(2)}) collective-permute-start(f32[3,8,512]{2,1,0:T(8,128)S(1)} %fusion.1.push), channel_id=1, source_target_pairs={{0,4},{4,0},{8,12},{12,8},{16,20},{20,16},{24,28},{28,24},{1,5},{5... | collective-permute-start | bytes 147464 | tf_op jit(solution)/shard_map/ppermute | solution.py:49
  49.6 4.1 %collective-permute-start.14 = (f32[3,24,512]{2,1,0:T(8,128)S(1)}, f32[3,24,512]{2,1,0:T(8,128)S(1)}, u32[]{:S(2)}, u32[]{:S(2)}) collective-permute-start(f32[3,24,512]{2,1,0:T(8,128)S(1)} %pad_maximum_fusion.push), channel_id=1, source_target_pairs={{0,1},{1,0},{2,3},{3,2},{4,5},{5,4},{6,7},{7,6},{8,9},{9,8},{10,11... | collective-permute-start | bytes 442376 | tf_op jit(solution)/shard_map/ppermute | solution.py:49
  49.7 5.6 %collective-permute-start.15 = (f32[3,24,512]{2,1,0:T(8,128)S(1)}, f32[3,24,512]{2,1,0:T(8,128)S(1)}, u32[]{:S(2)}, u32[]{:S(2)}) collective-permute-start(f32[3,24,512]{2,1,0:T(8,128)S(1)} %pad_maximum_fusion.push), channel_id=1, source_target_pairs={{0,3},{1,2},{2,1},{3,0},{4,7},{5,6},{6,5},{7,4},{8,11},{9,10},{10,... | collective-permute-start | bytes 442376 | tf_op jit(solution)/shard_map/ppermute | solution.py:49
  55.3 12.7 %copy-start.6 = (bf16[256,256]{1,0:T(8,128)(2,1)S(1)}, bf16[256,256]{1,0:T(8,128)(2,1)}, u32[]{:S(2)}) copy-start(bf16[256,256]{1,0:T(8,128)(2,1)} %constant.8.clone.table_high) | copy-start | bytes 393220
  55.3 12.7 %copy-start.7 = (bf16[256,256]{1,0:T(8,128)(2,1)S(1)}, bf16[256,256]{1,0:T(8,128)(2,1)}, u32[]{:S(2)}) copy-start(bf16[256,256]{1,0:T(8,128)(2,1)} %constant.9.clone.table_low) | copy-start | bytes 393220
  55.3 29.6 %copy-start.1 = (bf16[384,256]{1,0:T(8,128)(2,1)S(1)}, bf16[384,256]{1,0:T(8,128)(2,1)}, u32[]{:S(2)}) copy-start(bf16[384,256]{1,0:T(8,128)(2,1)} %constant.10.clone.table_high) | copy-start | bytes 589828
  55.3 29.6 %copy-start.2 = (bf16[384,256]{1,0:T(8,128)(2,1)S(1)}, bf16[384,256]{1,0:T(8,128)(2,1)}, u32[]{:S(2)}) copy-start(bf16[384,256]{1,0:T(8,128)(2,1)} %constant.11.clone.table_low) | copy-start | bytes 589828
  61.9 4.7 %collective-permute-start.16 = (f32[32,640]{1,0:T(8,128)S(1)}, f32[32,640]{1,0:T(8,128)S(1)}, u32[]{:S(2)}, u32[]{:S(2)}) collective-permute-start(f32[32,640]{1,0:T(8,128)S(1)} %get-tuple-element.69), channel_id=1, source_target_pairs={{0,3},{1,2},{2,1},{3,0},{4,7},{5,6},{6,5},{7,4},{8,11},{9,10},{10,... | collective-permute-start | bytes 245768 | tf_op jit(solution)/shard_map/ppermute | solution.py:915
  61.9 6.1 %collective-permute-start.17 = (f32[32,640]{1,0:T(8,128)S(1)}, f32[32,640]{1,0:T(8,128)S(1)}, u32[]{:S(2)}, u32[]{:S(2)}) collective-permute-start(f32[32,640]{1,0:T(8,128)S(1)} %get-tuple-element.70), channel_id=1, source_target_pairs={{0,2},{1,3},{2,0},{3,1},{4,6},{5,7},{6,4},{7,5},{8,10},{9,11},{10,... | collective-permute-start | bytes 245768 | tf_op jit(solution)/shard_map/ppermute | solution.py:915
  63.1 4.9 %collective-permute-start.18 = (f32[32,640]{1,0:T(8,128)S(1)}, f32[32,640]{1,0:T(8,128)S(1)}, u32[]{:S(2)}, u32[]{:S(2)}) collective-permute-start(f32[32,640]{1,0:T(8,128)S(1)} %get-tuple-element.71), channel_id=1, source_target_pairs={{0,1},{1,0},{2,3},{3,2},{4,5},{5,4},{6,7},{7,6},{8,9},{9,8},{10,11... | collective-permute-start | bytes 245768 | tf_op jit(solution)/shard_map/ppermute | solution.py:915
  69.1 8.2 %collective-permute-start.19 = (f32[144,128]{1,0:T(8,128)S(1)}, f32[144,128]{1,0:T(8,128)S(1)}, u32[]{:S(2)}, u32[]{:S(2)}) collective-permute-start(f32[144,128]{1,0:T(8,128)S(1)} %get-tuple-element.73), channel_id=1, source_target_pairs={{0,28},{4,24},{8,20},{12,16},{16,12},{20,8},{24,4},{28,0},{1,29},{... | collective-permute-start | bytes 221192 | tf_op jit(solution)/shard_map/ppermute | solution.py:915
  72.0 7.3 %collective-permute-start.20 = (f32[144,128]{1,0:T(8,128)S(1)}, f32[144,128]{1,0:T(8,128)S(1)}, u32[]{:S(2)}, u32[]{:S(2)}) collective-permute-start(f32[144,128]{1,0:T(8,128)S(1)} %get-tuple-element.74), channel_id=1, source_target_pairs={{0,24},{4,28},{8,16},{12,20},{16,8},{20,12},{24,0},{28,4},{1,25},{... | collective-permute-start | bytes 221192 | tf_op jit(solution)/shard_map/ppermute | solution.py:915
  73.5 9.7 %collective-permute-start.21 = (f32[144,128]{1,0:T(8,128)S(1)}, f32[144,128]{1,0:T(8,128)S(1)}, u32[]{:S(2)}, u32[]{:S(2)}) collective-permute-start(f32[144,128]{1,0:T(8,128)S(1)} %get-tuple-element.75), channel_id=1, source_target_pairs={{0,20},{4,16},{8,28},{12,24},{16,4},{20,0},{24,12},{28,8},{1,21},{... | collective-permute-start | bytes 221192 | tf_op jit(solution)/shard_map/ppermute | solution.py:915
  73.5 10.5 %collective-permute-start.22 = (f32[144,128]{1,0:T(8,128)S(1)}, f32[144,128]{1,0:T(8,128)S(1)}, u32[]{:S(2)}, u32[]{:S(2)}) collective-permute-start(f32[144,128]{1,0:T(8,128)S(1)} %get-tuple-element.76), channel_id=1, source_target_pairs={{0,16},{4,20},{8,24},{12,28},{16,0},{20,4},{24,8},{28,12},{1,17},{... | collective-permute-start | bytes 221192 | tf_op jit(solution)/shard_map/ppermute | solution.py:915
  76.8 7.5 %collective-permute-start.23 = (f32[144,128]{1,0:T(8,128)S(1)}, f32[144,128]{1,0:T(8,128)S(1)}, u32[]{:S(2)}, u32[]{:S(2)}) collective-permute-start(f32[144,128]{1,0:T(8,128)S(1)} %get-tuple-element.77), channel_id=1, source_target_pairs={{0,12},{4,8},{8,4},{12,0},{16,28},{20,24},{24,20},{28,16},{1,13},{... | collective-permute-start | bytes 221192 | tf_op jit(solution)/shard_map/ppermute | solution.py:915
  77.3 7.5 %collective-permute-start.24 = (f32[144,128]{1,0:T(8,128)S(1)}, f32[144,128]{1,0:T(8,128)S(1)}, u32[]{:S(2)}, u32[]{:S(2)}) collective-permute-start(f32[144,128]{1,0:T(8,128)S(1)} %get-tuple-element.78), channel_id=1, source_target_pairs={{0,8},{4,12},{8,0},{12,4},{16,24},{20,28},{24,16},{28,20},{1,9},{5... | collective-permute-start | bytes 221192 | tf_op jit(solution)/shard_map/ppermute | solution.py:915
  79.3 5.5 %collective-permute-start.25 = (f32[144,128]{1,0:T(8,128)S(1)}, f32[144,128]{1,0:T(8,128)S(1)}, u32[]{:S(2)}, u32[]{:S(2)}) collective-permute-start(f32[144,128]{1,0:T(8,128)S(1)} %get-tuple-element.79), channel_id=1, source_target_pairs={{0,4},{4,0},{8,12},{12,8},{16,20},{20,16},{24,28},{28,24},{1,5},{5... | collective-permute-start | bytes 221192 | tf_op jit(solution)/shard_map/ppermute | solution.py:915

commit v4 on v3

--- a/solution.py
+++ b/solution.py
@@ -104,8 +104,7 @@
             count += 1
 
 
-def window_start(first_y, size_y):
-    return pl.multiple_of(jnp.minimum((first_y // 8) * 8, size_y - WINDOW), 8)
+BODIES = ((True, True), (True, False), (False, True), (False, False))
 
 
 def quarters(sizes):
@@ -132,8 +131,8 @@
     return jnp.concatenate(rows, axis=1)
 
 
-def slot_visits(layout, facts, marks, saved, blocks, step, high, low, visit, skip):
-    size_x, size_z, size_y = layout.sizes
+def slot_visits(layout, facts, marks, saved, blocks, step, high, low, visit):
+    size_x, size_z, _ = layout.sizes
     half_x, half_z = size_x // 2, size_z // 2
     slots = layout.slots
 
@@ -141,30 +140,20 @@
         block, slot = index // slots, index % slots
         block = blocks[0] + block * (blocks[1] - blocks[0] if len(blocks) > 1 else 0)
         fact = (step * 3 + block) * slots + slot
-        first_x = facts[0, fact]
-        first_z = facts[1, fact]
-        first_y = facts[2, fact]
-        meets_x = (first_x > -BOX) & (first_x < size_x)
-        meets_z = (first_z > -BOX) & (first_z < size_z)
-        active = (facts[3, fact] != 0) & meets_x & meets_z
-        whole_x = (first_x > half_x - BOX) & (first_x < half_x)
-        whole_z = (first_z > half_z - BOX) & (first_z < half_z)
-        upper_x = (first_x >= half_x).astype(jnp.int32)
-        upper_z = (first_z >= half_z).astype(jnp.int32)
+        kind = facts[4, fact]
 
         def part(all_x, all_z):
-            start_x = 0 if all_x else upper_x * half_x
-            start_z = 0 if all_z else upper_z * half_z
-            lanes = [
-                ((0 if all_z else upper_z) + z) * 2 * LANES + (0 if all_x else upper_x) * LANES
-                for z in range(2 if all_z else 1)
-            ]
-            width = (2 if all_x else 1) * LANES
+            first_x, first_z, first_y = facts[0, fact], facts[1, fact], facts[2, fact]
+            first = pl.multiple_of(facts[5, fact], 8)
+            upper_x = 0 if all_x else facts[6, fact]
+            upper_z = 0 if all_z else facts[7, fact]
+            start_x, start_z = upper_x * half_x, upper_z * half_z
+            lanes = [(upper_z + z) * 2 * LANES + upper_x * LANES for z in range(1 + all_z)]
+            width = (1 + all_x) * LANES
             if all_x and all_z:
                 pieces = [(0, 4 * LANES)]
             else:
                 pieces = [(pl.multiple_of(lane, LANES), width) for lane in lanes]
-            first = window_start(first_y, size_y)
             rows_x = slice(0, size_x if all_x else half_x)
             rows_z = slice(size_x, size_x + (size_z if all_z else half_z))
             rows_y = slice(size_x + size_z, size_x + size_z + WINDOW)
@@ -179,17 +168,10 @@
             weight_y = saved[index, rows_y, :]
             visit(index, block * slots + slot, first, weight_y, pieces)
 
-        for all_x in (True, False):
-            for all_z in (True, False):
-                one = whole_x if all_x else jnp.logical_not(whole_x)
-                two = whole_z if all_z else jnp.logical_not(whole_z)
-                pl.when(active & one & two)(functools.partial(part, all_x, all_z))
-
-        if skip is not None:
-
-            @pl.when(jnp.logical_not(active))
-            def _():
-                skip(index)
+        @pl.when(kind != 0)
+        def _():
+            for number, (all_x, all_z) in enumerate(BODIES):
+                pl.when(kind == number + 1)(functools.partial(part, all_x, all_z))
 
         return carry
 
@@ -239,11 +221,8 @@
             sampled = jnp.sum(part, axis=0, keepdims=True)
             out[c, pl.ds(index, 1), :] = sampled if target is None else target[c] - sampled
 
-    def skip(index):
-        for c in range(3):
-            out[c, pl.ds(index, 1), :] = jnp.zeros((1, layout.markers), jnp.float32)
-
-    slot_visits(layout, facts, marks, saved, blocks, step, high, low, visit, skip)
+    out[...] = jnp.zeros(out.shape, jnp.float32)
+    slot_visits(layout, facts, marks, saved, blocks, step, high, low, visit)
 
 
 def sample_kernel(layout, groups, moved, facts, *refs):
@@ -317,7 +296,7 @@
                 total[c, pl.ds(first, WINDOW), pl.ds(lane, width)] += part
             column += width
 
-    slot_visits(layout, facts, None, saved, blocks, step, high, low, visit, None)
+    slot_visits(layout, facts, None, saved, blocks, step, high, low, visit)
 
 
 def spread_own_kernel(layout, facts, saved, push, total, high, low):
@@ -535,7 +514,7 @@
 def collect_kernel(layout, own, side_0, side_1, one, two, corners_0, corners_1, *refs):
     rows, (facts, table) = refs[:3], refs[3:]
     count, slots = layout.rows, layout.slots
-    size_x, size_z, _ = layout.sizes
+    size_x, size_z, size_y = layout.sizes
     for row, middle, base, sides in (
         (rows[0], one, layout.ghost_z, corners_0),
         (rows[1], own, 0, None),
@@ -557,7 +536,21 @@
     moved_x = jnp.where(place < slots, move_x, jnp.where(place >= 2 * slots, -move_x, 0))
     moved_z = jnp.where(slot < 3 * slots, move_z, jnp.where(slot >= last, -move_z, 0))
     moved = jnp.where(kind == 0, moved_x, jnp.where(kind == 1, moved_z, 0))
-    facts[...] = jnp.transpose(table[...])[:8].astype(jnp.int32) + moved
+    known = jnp.transpose(table[...])[:8].astype(jnp.int32) + moved
+    first_x, first_z, first_y, particle = [known[i : i + 1] for i in range(4)]
+    half_x, half_z = size_x // 2, size_z // 2
+
+    def between(value, low, high):
+        return (value > low) & (value < high)
+
+    meets = between(first_x, -BOX, size_x) & between(first_z, -BOX, size_z) & (particle > 0)
+    part_x = jnp.where(between(first_x, half_x - BOX, half_x), 0, 2)
+    part_z = jnp.where(between(first_z, half_z - BOX, half_z), 0, 1)
+    facts[...] = known
+    facts[4:5] = jnp.where(meets, 1 + part_x + part_z, 0)
+    facts[5:6] = jnp.minimum(jnp.bitwise_and(first_y, -8), size_y - WINDOW)
+    facts[6:7] = jnp.where(first_x >= half_x, 1, 0)
+    facts[7:8] = jnp.where(first_z >= half_z, 1, 0)
 
 
 def collect(layout, *tiles):

time: 86.9 us -> 85 us (0.978)
  Pallas kernels: 25.8 us -> 22.9 us
  waiting for transfers between devices: 24.6 us -> 25.7 us
    pallas_call x12, Pallas kernels: 23.8 us -> 20.8 us  [call(): pl.pallas_call(kernel, out_shape=out_shape, in_specs=[IN_SMEM] * len(scal...]
    ppermute x16, waiting for transfers between devices: 15.8 us -> 16.9 us  [swap(): return lax.ppermute(array, axis, pairs)]
  transfers between devices with their start and end apart: 26 -> 26, of which waited for: 14 -> 14; matrix products, arithmetic and copies ran while one was open for 0% -> 0% of each run, Pallas kernels for 10% -> 9%
where the time goes in v4:
time: 85 us; the launch traced here: 84.7 us
  starting transfers between devices  33.2 us (39%)
  waiting for transfers between devices  25.7 us (30%)
  Pallas kernels  22.9 us (27%)
  local copies, waits for them, and re-layouts  2.06 us (2%)
    pallas_call x12, Pallas kernels, call(): pl.pallas_call(kernel, out_shape=out_shape, in_specs=[IN_SMEM] * len(scal...  20.8 us
    ppermute x16, starting transfers between devices, swap(): return lax.ppermute(array, axis, pairs)  20.2 us
    ppermute x16, waiting for transfers between devices, swap(): return lax.ppermute(array, axis, pairs)  16.9 us
    ppermute x10, starting transfers between devices, exchange(): lax.ppermute(piece, axis, [(i, i ^ step) for i in range(devices)])  13.1 us
    ppermute x10, waiting for transfers between devices, exchange(): lax.ppermute(piece, axis, [(i, i ^ step) for i in range(devices)])  8.76 us
    pallas_call x1, Pallas kernels, pack(): pl.pallas_call(functools.partial(pack_kernel, layout), out_shape=[float32...  2.06 us
    unnamed x16, local copies, waits for them, and re-layouts  2.06 us
  transfers between devices with their start and end apart: 26, of which 14 were waited for; matrix products, arithmetic and copies ran while one was open for 0% of the time, Pallas kernels for 9%

profile of v4, /device:TPU:0, one launch (start us, length us, event | category | flops | bytes accessed | tf_op | source)
XLA Modules:
  0.0 84.7 jit_solution(14140203493850913947)
XLA Ops:
  0.6 2.1 %pack.1 = (f32[104,128]{1,0:T(8,128)}, f32[128,128]{1,0:T(8,128)}, f32[128,128]{1,0:T(8,128)}, f32[168,128]{1,0:T(8,128)}, f32[168,128]{1,0:T(8,128)}) custom-call(s32[8]{0:T(128)} %slot_ids_hbm.1, s32[3,8]{1,0:T(4,128)} %corners_hbm.1, f32[4,16,32,128]{3,2,1,0:T(8,128)} %flow.3, s32[3,8,512]{2,1,0:T(8,128)} %cells_hbm.1, f32[3,8,512]{2,1,0:T(8,128)} %fraction_hbm.1), custom_call_target="tpu_custom_call" | custom-call | flops 262144 | bytes 262144 | tf_op jit(solution)/shard_map/pack/pallas_call | solution.py:474
  2.7 3.1 %collective-permute-start = (f32[104,128]{1,0:T(8,128)}, f32[104,128]{1,0:T(8,128)S(1)}, u32[]{:S(2)}, u32[]{:S(2)}) collective-permute-start(f32[104,128]{1,0:T(8,128)} %get-tuple-element.41.own), channel_id=1, source_target_pairs={{0,4},{4,0},{8,12},{12,8},{16,20},{20,16},{24,28},{28,24},{1,5},{5... | collective-permute-start | bytes 159752 | tf_op jit(solution)/shard_map/ppermute | solution.py:49
  5.8 3.5 %collective-permute-start.1 = (f32[104,128]{1,0:T(8,128)}, f32[104,128]{1,0:T(8,128)S(1)}, u32[]{:S(2)}, u32[]{:S(2)}) collective-permute-start(f32[104,128]{1,0:T(8,128)} %get-tuple-element.41.own), channel_id=1, source_target_pairs={{0,28},{4,8},{8,4},{12,16},{16,12},{20,24},{24,20},{28,0},{1,29},{... | collective-permute-start | bytes 159752 | tf_op jit(solution)/shard_map/ppermute | solution.py:49
  9.3 3.5 %collective-permute-done.1.right.side_1 = f32[104,128]{1,0:T(8,128)S(1)} collective-permute-done((f32[104,128]{1,0:T(8,128)}, f32[104,128]{1,0:T(8,128)S(1)}, u32[]{:S(2)}, u32[]{:S(2)}) %collective-permute-start.1) | collective-permute-done | bytes 53280 | tf_op jit(solution)/shard_map/ppermute | solution.py:49
  12.8 0.1 collective-permute-start.4
  12.9 1.6 %collective-permute-start.5 = (f32[208,128]{1,0:T(8,128)S(1)}, f32[208,128]{1,0:T(8,128)S(1)}, u32[]{:S(2)}, u32[]{:S(2)}) collective-permute-start(f32[208,128]{1,0:T(8,128)S(1)} %shard_map.123), channel_id=1, source_target_pairs={{0,3},{1,2},{2,1},{3,0},{4,7},{5,6},{6,5},{7,4},{8,11},{9,10},{10,... | collective-permute-start | bytes 319496 | tf_op jit(solution)/shard_map/ppermute | solution.py:49
  14.5 0.1 collective-permute-start.2
  14.6 0.6 collective-permute-start.3
  15.1 3.5 %collective-permute-start.7 = (f32[128,128]{1,0:T(8,128)}, f32[128,128]{1,0:T(8,128)S(1)}, u32[]{:S(2)}, u32[]{:S(2)}) collective-permute-start(f32[128,128]{1,0:T(8,128)} %get-tuple-element.54), channel_id=1, source_target_pairs={{0,28},{4,8},{8,4},{12,16},{16,12},{20,24},{24,20},{28,0},{1,29},{... | collective-permute-start | bytes 196616 | tf_op jit(solution)/shard_map/ppermute | solution.py:49
  18.7 1.2 %copy-done = f32[4,16,32,128]{3,2,1,0:T(8,128)S(1)} copy-done((f32[4,16,32,128]{3,2,1,0:T(8,128)S(1)}, f32[4,16,32,128]{3,2,1,0:T(8,128)}, u32[]{:S(2)}) %copy-start) | copy-done | bytes 1048600
  19.9 0.8 copy-done.3
  20.7 0.9 %shard_map.122 = (f32[3,16,32,128]{3,2,1,0:T(8,128)S(1)}, f32[32,128]{1,0:T(8,128)S(1)}, f32[32,128]{1,0:T(8,128)S(1)}, f32[16,128]{1,0:T(8,128)S(1)}, f32[16,128]{1,0:T(8,128)S(1)}, /*index=5*/f32[104,128]{1,0:T(8,128)S(1)}) custom-call(f32[4,16,32,128]{3,2,1,0:T(8,128)S(1)} %copy-done, f32[104,128]{1,0:T(8,128)S(1)} %copy-done.3), custom_call_target="tpu_custom_call" | custom-call | flops 52428800 | bytes 2097152 | tf_op jit(solution)/shard_map/pallas_call | solution.py:35
  21.6 0.7 collective-permute-done.7.x_1
  22.3 0.3 shard_map.125
  22.7 0.1 shard_map.124
  22.8 4.3 %shard_map.126 = (f32[3,24,512]{2,1,0:T(8,128)S(1)}, f32[3,24,512]{2,1,0:T(8,128)S(1)}, f32[24,80,512]{2,1,0:T(8,128)S(1)}, f32[24,80,512]{2,1,0:T(8,128)S(1)}) custom-call(s32[8,128]{1,0:T(8,128)S(1)} %get-tuple-element.45.facts, f32[312,128]{1,0:T(8,128)S(1)} %get-tuple-element.46.refs_0_, f32[312,128]{1,0:T(8,128)S(1)} %get-tuple-element.47.refs_1_, ...), custom_call_target="tpu_custom_call" | custom-call | flops 7247757312 | bytes 1572864 | tf_op jit(solution)/shard_map/pallas_call | solution.py:35
  27.0 0.1 collective-permute-start.8
  27.2 2.5 %shard_map.128 = (f32[3,16,512]{2,1,0:T(8,128)S(1)}, f32[16,80,512]{2,1,0:T(8,128)S(1)}) custom-call(s32[8,128]{1,0:T(8,128)S(1)} %get-tuple-element.45.facts, f32[312,128]{1,0:T(8,128)S(1)} %get-tuple-element.59.refs_0_, f32[3,128,512]{2,1,0:T(8,128)S(1)} %get-tuple-element.55.refs_2_.refs_1_, f32[3,128,512]{2,1,0:T(8,128)S(1)} %get-tuple-element.56.refs_3_.refs_2_), custom_call_target="tpu_custom_call" | custom-call | flops 2415919104 | bytes 1572864 | tf_op jit(solution)/shard_map/pallas_call | solution.py:35
  29.7 3.0 %collective-permute-done.9 = f32[3,24,512]{2,1,0:T(8,128)S(1)} collective-permute-done((f32[3,24,512]{2,1,0:T(8,128)S(1)}, f32[3,24,512]{2,1,0:T(8,128)S(1)}, u32[]{:S(2)}, u32[]{:S(2)}) %collective-permute-start.9) | collective-permute-done | bytes 147488 | tf_op jit(solution)/shard_map/ppermute | solution.py:49
  32.8 3.8 %collective-permute-start.11 = (f32[3,8,512]{2,1,0:T(8,128)S(1)}, f32[3,8,512]{2,1,0:T(8,128)S(1)}, u32[]{:S(2)}, u32[]{:S(2)}) collective-permute-start(f32[3,8,512]{2,1,0:T(8,128)S(1)} %get-tuple-element.81), channel_id=1, source_target_pairs={{0,28},{4,8},{8,4},{12,16},{16,12},{20,24},{24,20},{28,0},{1,29},{... | collective-permute-start | bytes 147464 | tf_op jit(solution)/shard_map/ppermute | solution.py:49
  36.5 0.8 shard_map.127
  37.3 2.7 %collective-permute-done.11 = f32[3,8,512]{2,1,0:T(8,128)S(1)} collective-permute-done((f32[3,8,512]{2,1,0:T(8,128)S(1)}, f32[3,8,512]{2,1,0:T(8,128)S(1)}, u32[]{:S(2)}, u32[]{:S(2)}) %collective-permute-start.11) | collective-permute-done | bytes 49184 | tf_op jit(solution)/shard_map/ppermute | solution.py:49
  40.0 0.8 collective-permute-done.10
  40.8 2.6 %collective-permute-start.13 = (f32[3,8,512]{2,1,0:T(8,128)S(1)}, f32[3,8,512]{2,1,0:T(8,128)S(1)}, u32[]{:S(2)}, u32[]{:S(2)}) collective-permute-start(f32[3,8,512]{2,1,0:T(8,128)S(1)} %fusion.1.push), channel_id=1, source_target_pairs={{0,28},{4,8},{8,4},{12,16},{16,12},{20,24},{24,20},{28,0},{1,29},{... | collective-permute-start | bytes 147464 | tf_op jit(solution)/shard_map/ppermute | solution.py:49
  43.4 0.8 shard_map.129.before
  44.2 4.0 %collective-permute-done.13 = f32[3,8,512]{2,1,0:T(8,128)S(1)} collective-permute-done((f32[3,8,512]{2,1,0:T(8,128)S(1)}, f32[3,8,512]{2,1,0:T(8,128)S(1)}, u32[]{:S(2)}, u32[]{:S(2)}) %collective-permute-start.13) | collective-permute-done | bytes 49184 | tf_op jit(solution)/shard_map/ppermute | solution.py:49
  48.2 0.3 collective-permute-done.12
  48.6 0.1 collective-permute-start.14
  48.6 1.1 %collective-permute-start.15 = (f32[3,24,512]{2,1,0:T(8,128)S(1)}, f32[3,24,512]{2,1,0:T(8,128)S(1)}, u32[]{:S(2)}, u32[]{:S(2)}) collective-permute-start(f32[3,24,512]{2,1,0:T(8,128)S(1)} %pad_maximum_fusion.push), channel_id=1, source_target_pairs={{0,3},{1,2},{2,1},{3,0},{4,7},{5,6},{6,5},{7,4},{8,11},{9,10},{10,... | collective-permute-start | bytes 442376 | tf_op jit(solution)/shard_map/ppermute | solution.py:49
  49.8 2.6 %shard_map.130.before = f32[3,128,512]{2,1,0:T(8,128)S(1)} custom-call(s32[8,128]{1,0:T(8,128)S(1)} %get-tuple-element.45.facts, f32[16,80,512]{2,1,0:T(8,128)S(1)} %get-tuple-element.64.saved, f32[3,24,512]{2,1,0:T(8,128)S(1)} %pad_maximum_fusion.push, f32[3,128,512]{2,1,0:T(8,128)S(1)} %shard_map.129.before), custom_call_target="tpu_custom_call" | custom-call | flops 2415919104 | bytes 1572864 | tf_op jit(solution)/shard_map/pallas_call | solution.py:35
  52.4 1.9 %collective-permute-done.15.push_1 = f32[3,24,512]{2,1,0:T(8,128)S(1)} collective-permute-done((f32[3,24,512]{2,1,0:T(8,128)S(1)}, f32[3,24,512]{2,1,0:T(8,128)S(1)}, u32[]{:S(2)}, u32[]{:S(2)}) %collective-permute-start.15) | collective-permute-done | bytes 147488 | tf_op jit(solution)/shard_map/ppermute | solution.py:49
  54.3 5.7 %shard_map.131 = (f32[3,16,32,128]{3,2,1,0:T(8,128)}, f32[32,640]{1,0:T(8,128)S(1)}, f32[32,640]{1,0:T(8,128)S(1)}, f32[32,640]{1,0:T(8,128)S(1)}, f32[32,640]{1,0:T(8,128)S(1)}) custom-call(s32[8,128]{1,0:T(8,128)S(1)} %get-tuple-element.45.facts, f32[24,80,512]{2,1,0:T(8,128)S(1)} %get-tuple-element.57.saved_0, ...), custom_call_target="tpu_custom_call" | custom-call | flops 7247757312 | bytes 2359296 | tf_op jit(solution)/shard_map/pallas_call | solution.py:35
  60.0 1.2 %collective-permute-start.17 = (f32[32,640]{1,0:T(8,128)S(1)}, f32[32,640]{1,0:T(8,128)S(1)}, u32[]{:S(2)}, u32[]{:S(2)}) collective-permute-start(f32[32,640]{1,0:T(8,128)S(1)} %get-tuple-element.70), channel_id=1, source_target_pairs={{0,2},{1,3},{2,0},{3,1},{4,6},{5,7},{6,4},{7,5},{8,10},{9,11},{10,... | collective-permute-start | bytes 245768 | tf_op jit(solution)/shard_map/ppermute | solution.py:908
  61.2 0.6 collective-permute-start.18
  61.8 2.9 %collective-permute-done.16.refs_1_ = f32[32,640]{1,0:T(8,128)S(1)} collective-permute-done((f32[32,640]{1,0:T(8,128)S(1)}, f32[32,640]{1,0:T(8,128)S(1)}, u32[]{:S(2)}, u32[]{:S(2)}) %collective-permute-start.16) | collective-permute-done | bytes 81952 | tf_op jit(solution)/shard_map/ppermute | solution.py:908
  64.7 1.3 %collective-permute-done.17.refs_2_ = f32[32,640]{1,0:T(8,128)S(1)} collective-permute-done((f32[32,640]{1,0:T(8,128)S(1)}, f32[32,640]{1,0:T(8,128)S(1)}, u32[]{:S(2)}, u32[]{:S(2)}) %collective-permute-start.17) | collective-permute-done | bytes 81952 | tf_op jit(solution)/shard_map/ppermute | solution.py:908
  66.0 1.1 %shard_map.132 = (f32[144,128]{1,0:T(8,128)S(1)}, f32[144,128]{1,0:T(8,128)S(1)}, f32[144,128]{1,0:T(8,128)S(1)}, f32[144,128]{1,0:T(8,128)S(1)}, f32[144,128]{1...) custom-call(bf16[256,256]{1,0:T(8,128)(2,1)S(1)} %copy-done.6, ...), custom_call_target="tpu_custom_call" | custom-call | flops 201326592 | bytes 786432 | tf_op jit(solution)/shard_map/pallas_call | solution.py:35
  67.1 2.7 %collective-permute-start.19 = (f32[144,128]{1,0:T(8,128)S(1)}, f32[144,128]{1,0:T(8,128)S(1)}, u32[]{:S(2)}, u32[]{:S(2)}) collective-permute-start(f32[144,128]{1,0:T(8,128)S(1)} %get-tuple-element.73), channel_id=1, source_target_pairs={{0,28},{4,24},{8,20},{12,16},{16,12},{20,8},{24,4},{28,0},{1,29},{... | collective-permute-start | bytes 221192 | tf_op jit(solution)/shard_map/ppermute | solution.py:908
  69.8 1.5 %collective-permute-start.20 = (f32[144,128]{1,0:T(8,128)S(1)}, f32[144,128]{1,0:T(8,128)S(1)}, u32[]{:S(2)}, u32[]{:S(2)}) collective-permute-start(f32[144,128]{1,0:T(8,128)S(1)} %get-tuple-element.74), channel_id=1, source_target_pairs={{0,24},{4,28},{8,16},{12,20},{16,8},{20,12},{24,0},{28,4},{1,25},{... | collective-permute-start | bytes 221192 | tf_op jit(solution)/shard_map/ppermute | solution.py:908
  71.3 3.5 %collective-permute-start.22 = (f32[144,128]{1,0:T(8,128)S(1)}, f32[144,128]{1,0:T(8,128)S(1)}, u32[]{:S(2)}, u32[]{:S(2)}) collective-permute-start(f32[144,128]{1,0:T(8,128)S(1)} %get-tuple-element.76), channel_id=1, source_target_pairs={{0,16},{4,20},{8,24},{12,28},{16,0},{20,4},{24,8},{28,12},{1,17},{... | collective-permute-start | bytes 221192 | tf_op jit(solution)/shard_map/ppermute | solution.py:908
  74.8 0.3 collective-permute-start.23
  75.1 2.0 %collective-permute-start.24 = (f32[144,128]{1,0:T(8,128)S(1)}, f32[144,128]{1,0:T(8,128)S(1)}, u32[]{:S(2)}, u32[]{:S(2)}) collective-permute-start(f32[144,128]{1,0:T(8,128)S(1)} %get-tuple-element.78), channel_id=1, source_target_pairs={{0,8},{4,12},{8,0},{12,4},{16,24},{20,28},{24,16},{28,20},{1,9},{5... | collective-permute-start | bytes 221192 | tf_op jit(solution)/shard_map/ppermute | solution.py:908
  77.2 1.1 %collective-permute-start.25 = (f32[144,128]{1,0:T(8,128)S(1)}, f32[144,128]{1,0:T(8,128)S(1)}, u32[]{:S(2)}, u32[]{:S(2)}) collective-permute-start(f32[144,128]{1,0:T(8,128)S(1)} %get-tuple-element.79), channel_id=1, source_target_pairs={{0,4},{4,0},{8,12},{12,8},{16,20},{20,16},{24,28},{28,24},{1,5},{5... | collective-permute-start | bytes 221192 | tf_op jit(solution)/shard_map/ppermute | solution.py:908
  78.3 2.4 %collective-permute-done.21.refs_3_ = f32[144,128]{1,0:T(8,128)S(1)} collective-permute-done((f32[144,128]{1,0:T(8,128)S(1)}, f32[144,128]{1,0:T(8,128)S(1)}, u32[]{:S(2)}, u32[]{:S(2)}) %collective-permute-start.21) | collective-permute-done | bytes 73760 | tf_op jit(solution)/shard_map/ppermute | solution.py:908
  80.7 1.4 %collective-permute-done.22.refs_4_ = f32[144,128]{1,0:T(8,128)S(1)} collective-permute-done((f32[144,128]{1,0:T(8,128)S(1)}, f32[144,128]{1,0:T(8,128)S(1)}, u32[]{:S(2)}, u32[]{:S(2)}) %collective-permute-start.22) | collective-permute-done | bytes 73760 | tf_op jit(solution)/shard_map/ppermute | solution.py:908
  82.1 0.6 collective-permute-done.23.refs_5_
  82.6 0.2 collective-permute-done.24.refs_6_
  82.9 1.8 %shard_map.133 = f32[2,32,16,128]{3,2,1,0:T(8,128)} custom-call(bf16[384,256]{1,0:T(8,128)(2,1)S(1)} %copy-done.1, bf16[384,256]{1,0:T(8,128)(2,1)S(1)} %copy-done.2, f32[144,128]{1,0:T(8,128)S(1)} %get-tuple-element.72.refs_0_, f32[144,128]{1,0:T(8,128)S(1)} %collective-permute-done.19.refs_1_, f32[144,128]{1,0:T(8,128)S(1)} %collective-permute-done.20.refs_2_, ...), custom_call_target="tpu_custom_call" | custom-call | flops 201326592 | bytes 1572864 | tf_op jit(solution)/shard_map/pallas_call | solution.py:35
  (37 shorter events, 0.2 us)
Async XLA Ops:
  2.7 6.6 %collective-permute-start = (f32[104,128]{1,0:T(8,128)}, f32[104,128]{1,0:T(8,128)S(1)}, u32[]{:S(2)}, u32[]{:S(2)}) collective-permute-start(f32[104,128]{1,0:T(8,128)} %get-tuple-element.41.own), channel_id=1, source_target_pairs={{0,4},{4,0},{8,12},{12,8},{16,20},{20,16},{24,28},{28,24},{1,5},{5... | collective-permute-start | bytes 159752 | tf_op jit(solution)/shard_map/ppermute | solution.py:49
  5.8 7.0 %collective-permute-start.1 = (f32[104,128]{1,0:T(8,128)}, f32[104,128]{1,0:T(8,128)S(1)}, u32[]{:S(2)}, u32[]{:S(2)}) collective-permute-start(f32[104,128]{1,0:T(8,128)} %get-tuple-element.41.own), channel_id=1, source_target_pairs={{0,28},{4,8},{8,4},{12,16},{16,12},{20,24},{24,20},{28,0},{1,29},{... | collective-permute-start | bytes 159752 | tf_op jit(solution)/shard_map/ppermute | solution.py:49
  9.3 5.8 %collective-permute-start.6 = (f32[128,128]{1,0:T(8,128)}, f32[128,128]{1,0:T(8,128)S(1)}, u32[]{:S(2)}, u32[]{:S(2)}) collective-permute-start(f32[128,128]{1,0:T(8,128)} %get-tuple-element.53), channel_id=1, source_target_pairs={{0,4},{4,0},{8,12},{12,8},{16,20},{20,16},{24,28},{28,24},{1,5},{5... | collective-permute-start | bytes 196616 | tf_op jit(solution)/shard_map/ppermute | solution.py:49
  12.8 9.8 %collective-permute-start.4 = (f32[208,128]{1,0:T(8,128)S(1)}, f32[208,128]{1,0:T(8,128)S(1)}, u32[]{:S(2)}, u32[]{:S(2)}) collective-permute-start(f32[208,128]{1,0:T(8,128)S(1)} %shard_map.123), channel_id=1, source_target_pairs={{0,1},{1,0},{2,3},{3,2},{4,5},{5,4},{6,7},{7,6},{8,9},{9,8},{10,11... | collective-permute-start | bytes 319496 | tf_op jit(solution)/shard_map/ppermute | solution.py:49
  12.9 9.8 %collective-permute-start.5 = (f32[208,128]{1,0:T(8,128)S(1)}, f32[208,128]{1,0:T(8,128)S(1)}, u32[]{:S(2)}, u32[]{:S(2)}) collective-permute-start(f32[208,128]{1,0:T(8,128)S(1)} %shard_map.123), channel_id=1, source_target_pairs={{0,3},{1,2},{2,1},{3,0},{4,7},{5,6},{6,5},{7,4},{8,11},{9,10},{10,... | collective-permute-start | bytes 319496 | tf_op jit(solution)/shard_map/ppermute | solution.py:49
  14.5 7.8 %collective-permute-start.2 = (f32[168,128]{1,0:T(8,128)}, f32[168,128]{1,0:T(8,128)S(1)}, u32[]{:S(2)}, u32[]{:S(2)}) collective-permute-start(f32[168,128]{1,0:T(8,128)} %get-tuple-element.43), channel_id=1, source_target_pairs={{0,1},{1,0},{2,3},{3,2},{4,5},{5,4},{6,7},{7,6},{8,9},{9,8},{10,11... | collective-permute-start | bytes 258056 | tf_op jit(solution)/shard_map/ppermute | solution.py:49
  14.6 7.8 %collective-permute-start.3 = (f32[168,128]{1,0:T(8,128)}, f32[168,128]{1,0:T(8,128)S(1)}, u32[]{:S(2)}, u32[]{:S(2)}) collective-permute-start(f32[168,128]{1,0:T(8,128)} %get-tuple-element.44), channel_id=1, source_target_pairs={{0,3},{1,2},{2,1},{3,0},{4,7},{5,6},{6,5},{7,4},{8,11},{9,10},{10,... | collective-permute-start | bytes 258056 | tf_op jit(solution)/shard_map/ppermute | solution.py:49
  15.1 7.2 %collective-permute-start.7 = (f32[128,128]{1,0:T(8,128)}, f32[128,128]{1,0:T(8,128)S(1)}, u32[]{:S(2)}, u32[]{:S(2)}) collective-permute-start(f32[128,128]{1,0:T(8,128)} %get-tuple-element.54), channel_id=1, source_target_pairs={{0,28},{4,8},{8,4},{12,16},{16,12},{20,24},{24,20},{28,0},{1,29},{... | collective-permute-start | bytes 196616 | tf_op jit(solution)/shard_map/ppermute | solution.py:49
  18.7 1.2 %copy-start = (f32[4,16,32,128]{3,2,1,0:T(8,128)S(1)}, f32[4,16,32,128]{3,2,1,0:T(8,128)}, u32[]{:S(2)}) copy-start(f32[4,16,32,128]{3,2,1,0:T(8,128)} %flow.3) | copy-start | bytes 3145732
  19.9 0.8 copy-start.3
  27.0 2.7 %collective-permute-start.8 = (f32[3,24,512]{2,1,0:T(8,128)S(1)}, f32[3,24,512]{2,1,0:T(8,128)S(1)}, u32[]{:S(2)}, u32[]{:S(2)}) collective-permute-start(f32[3,24,512]{2,1,0:T(8,128)S(1)} %get-tuple-element.61), channel_id=1, source_target_pairs={{0,1},{1,0},{2,3},{3,2},{4,5},{5,4},{6,7},{7,6},{8,9},{9,8},{10,11... | collective-permute-start | bytes 442376 | tf_op jit(solution)/shard_map/ppermute | solution.py:49
  27.1 5.6 %collective-permute-start.9 = (f32[3,24,512]{2,1,0:T(8,128)S(1)}, f32[3,24,512]{2,1,0:T(8,128)S(1)}, u32[]{:S(2)}, u32[]{:S(2)}) collective-permute-start(f32[3,24,512]{2,1,0:T(8,128)S(1)} %get-tuple-element.62), channel_id=1, source_target_pairs={{0,3},{1,2},{2,1},{3,0},{4,7},{5,6},{6,5},{7,4},{8,11},{9,10},{10,... | collective-permute-start | bytes 442376 | tf_op jit(solution)/shard_map/ppermute | solution.py:49
  27.2 9.3 %copy-start.4 = (f32[3,128]{1,0:T(4,128)S(1)}, f32[3,128]{1,0:T(4,128)}, u32[]{:S(2)}) copy-start(f32[3,128]{1,0:T(4,128)} %refs_3_.1) | copy-start | bytes 4612
  27.2 9.3 %copy-start.5 = (f32[3,128]{1,0:T(4,128)S(1)}, f32[3,128]{1,0:T(4,128)}, u32[]{:S(2)}) copy-start(f32[3,128]{1,0:T(4,128)} %refs_4_.1) | copy-start | bytes 4612
  32.8 7.2 %collective-permute-start.11 = (f32[3,8,512]{2,1,0:T(8,128)S(1)}, f32[3,8,512]{2,1,0:T(8,128)S(1)}, u32[]{:S(2)}, u32[]{:S(2)}) collective-permute-start(f32[3,8,512]{2,1,0:T(8,128)S(1)} %get-tuple-element.81), channel_id=1, source_target_pairs={{0,28},{4,8},{8,4},{12,16},{16,12},{20,24},{24,20},{28,0},{1,29},{... | collective-permute-start | bytes 147464 | tf_op jit(solution)/shard_map/ppermute | solution.py:49
  36.5 4.3 %collective-permute-start.10 = (f32[3,8,512]{2,1,0:T(8,128)S(1)}, f32[3,8,512]{2,1,0:T(8,128)S(1)}, u32[]{:S(2)}, u32[]{:S(2)}) collective-permute-start(f32[3,8,512]{2,1,0:T(8,128)S(1)} %get-tuple-element.80), channel_id=1, source_target_pairs={{0,4},{4,0},{8,12},{12,8},{16,20},{20,16},{24,28},{28,24},{1,5},{5... | collective-permute-start | bytes 147464 | tf_op jit(solution)/shard_map/ppermute | solution.py:49
  40.8 7.4 %collective-permute-start.13 = (f32[3,8,512]{2,1,0:T(8,128)S(1)}, f32[3,8,512]{2,1,0:T(8,128)S(1)}, u32[]{:S(2)}, u32[]{:S(2)}) collective-permute-start(f32[3,8,512]{2,1,0:T(8,128)S(1)} %fusion.1.push), channel_id=1, source_target_pairs={{0,28},{4,8},{8,4},{12,16},{16,12},{20,24},{24,20},{28,0},{1,29},{... | collective-permute-start | bytes 147464 | tf_op jit(solution)/shard_map/ppermute | solution.py:49
  43.4 5.1 %collective-permute-start.12 = (f32[3,8,512]{2,1,0:T(8,128)S(1)}, f32[3,8,512]{2,1,0:T(8,128)S(1)}, u32[]{:S(2)}, u32[]{:S(2)}) collective-permute-start(f32[3,8,512]{2,1,0:T(8,128)S(1)} %fusion.1.push), channel_id=1, source_target_pairs={{0,4},{4,0},{8,12},{12,8},{16,20},{20,16},{24,28},{28,24},{1,5},{5... | collective-permute-start | bytes 147464 | tf_op jit(solution)/shard_map/ppermute | solution.py:49
  48.6 3.8 %collective-permute-start.14 = (f32[3,24,512]{2,1,0:T(8,128)S(1)}, f32[3,24,512]{2,1,0:T(8,128)S(1)}, u32[]{:S(2)}, u32[]{:S(2)}) collective-permute-start(f32[3,24,512]{2,1,0:T(8,128)S(1)} %pad_maximum_fusion.push), channel_id=1, source_target_pairs={{0,1},{1,0},{2,3},{3,2},{4,5},{5,4},{6,7},{7,6},{8,9},{9,8},{10,11... | collective-permute-start | bytes 442376 | tf_op jit(solution)/shard_map/ppermute | solution.py:49
  48.6 5.6 %collective-permute-start.15 = (f32[3,24,512]{2,1,0:T(8,128)S(1)}, f32[3,24,512]{2,1,0:T(8,128)S(1)}, u32[]{:S(2)}, u32[]{:S(2)}) collective-permute-start(f32[3,24,512]{2,1,0:T(8,128)S(1)} %pad_maximum_fusion.push), channel_id=1, source_target_pairs={{0,3},{1,2},{2,1},{3,0},{4,7},{5,6},{6,5},{7,4},{8,11},{9,10},{10,... | collective-permute-start | bytes 442376 | tf_op jit(solution)/shard_map/ppermute | solution.py:49
  54.2 11.8 %copy-start.6 = (bf16[256,256]{1,0:T(8,128)(2,1)S(1)}, bf16[256,256]{1,0:T(8,128)(2,1)}, u32[]{:S(2)}) copy-start(bf16[256,256]{1,0:T(8,128)(2,1)} %constant.8.clone.table_high) | copy-start | bytes 393220
  54.2 11.8 %copy-start.7 = (bf16[256,256]{1,0:T(8,128)(2,1)S(1)}, bf16[256,256]{1,0:T(8,128)(2,1)}, u32[]{:S(2)}) copy-start(bf16[256,256]{1,0:T(8,128)(2,1)} %constant.9.clone.table_low) | copy-start | bytes 393220
  54.2 28.6 %copy-start.1 = (bf16[384,256]{1,0:T(8,128)(2,1)S(1)}, bf16[384,256]{1,0:T(8,128)(2,1)}, u32[]{:S(2)}) copy-start(bf16[384,256]{1,0:T(8,128)(2,1)} %constant.10.clone.table_high) | copy-start | bytes 589828
  54.2 28.6 %copy-start.2 = (bf16[384,256]{1,0:T(8,128)(2,1)S(1)}, bf16[384,256]{1,0:T(8,128)(2,1)}, u32[]{:S(2)}) copy-start(bf16[384,256]{1,0:T(8,128)(2,1)} %constant.11.clone.table_low) | copy-start | bytes 589828
  60.0 4.7 %collective-permute-start.16 = (f32[32,640]{1,0:T(8,128)S(1)}, f32[32,640]{1,0:T(8,128)S(1)}, u32[]{:S(2)}, u32[]{:S(2)}) collective-permute-start(f32[32,640]{1,0:T(8,128)S(1)} %get-tuple-element.69), channel_id=1, source_target_pairs={{0,3},{1,2},{2,1},{3,0},{4,7},{5,6},{6,5},{7,4},{8,11},{9,10},{10,... | collective-permute-start | bytes 245768 | tf_op jit(solution)/shard_map/ppermute | solution.py:908
  60.0 6.0 %collective-permute-start.17 = (f32[32,640]{1,0:T(8,128)S(1)}, f32[32,640]{1,0:T(8,128)S(1)}, u32[]{:S(2)}, u32[]{:S(2)}) collective-permute-start(f32[32,640]{1,0:T(8,128)S(1)} %get-tuple-element.70), channel_id=1, source_target_pairs={{0,2},{1,3},{2,0},{3,1},{4,6},{5,7},{6,4},{7,5},{8,10},{9,11},{10,... | collective-permute-start | bytes 245768 | tf_op jit(solution)/shard_map/ppermute | solution.py:908
  61.2 4.8 %collective-permute-start.18 = (f32[32,640]{1,0:T(8,128)S(1)}, f32[32,640]{1,0:T(8,128)S(1)}, u32[]{:S(2)}, u32[]{:S(2)}) collective-permute-start(f32[32,640]{1,0:T(8,128)S(1)} %get-tuple-element.71), channel_id=1, source_target_pairs={{0,1},{1,0},{2,3},{3,2},{4,5},{5,4},{6,7},{7,6},{8,9},{9,8},{10,11... | collective-permute-start | bytes 245768 | tf_op jit(solution)/shard_map/ppermute | solution.py:908
  67.1 8.0 %collective-permute-start.19 = (f32[144,128]{1,0:T(8,128)S(1)}, f32[144,128]{1,0:T(8,128)S(1)}, u32[]{:S(2)}, u32[]{:S(2)}) collective-permute-start(f32[144,128]{1,0:T(8,128)S(1)} %get-tuple-element.73), channel_id=1, source_target_pairs={{0,28},{4,24},{8,20},{12,16},{16,12},{20,8},{24,4},{28,0},{1,29},{... | collective-permute-start | bytes 221192 | tf_op jit(solution)/shard_map/ppermute | solution.py:908
  69.8 7.3 %collective-permute-start.20 = (f32[144,128]{1,0:T(8,128)S(1)}, f32[144,128]{1,0:T(8,128)S(1)}, u32[]{:S(2)}, u32[]{:S(2)}) collective-permute-start(f32[144,128]{1,0:T(8,128)S(1)} %get-tuple-element.74), channel_id=1, source_target_pairs={{0,24},{4,28},{8,16},{12,20},{16,8},{20,12},{24,0},{28,4},{1,25},{... | collective-permute-start | bytes 221192 | tf_op jit(solution)/shard_map/ppermute | solution.py:908
  71.3 9.4 %collective-permute-start.21 = (f32[144,128]{1,0:T(8,128)S(1)}, f32[144,128]{1,0:T(8,128)S(1)}, u32[]{:S(2)}, u32[]{:S(2)}) collective-permute-start(f32[144,128]{1,0:T(8,128)S(1)} %get-tuple-element.75), channel_id=1, source_target_pairs={{0,20},{4,16},{8,28},{12,24},{16,4},{20,0},{24,12},{28,8},{1,21},{... | collective-permute-start | bytes 221192 | tf_op jit(solution)/shard_map/ppermute | solution.py:908
  71.3 10.8 %collective-permute-start.22 = (f32[144,128]{1,0:T(8,128)S(1)}, f32[144,128]{1,0:T(8,128)S(1)}, u32[]{:S(2)}, u32[]{:S(2)}) collective-permute-start(f32[144,128]{1,0:T(8,128)S(1)} %get-tuple-element.76), channel_id=1, source_target_pairs={{0,16},{4,20},{8,24},{12,28},{16,0},{20,4},{24,8},{28,12},{1,17},{... | collective-permute-start | bytes 221192 | tf_op jit(solution)/shard_map/ppermute | solution.py:908
  74.8 7.8 %collective-permute-start.23 = (f32[144,128]{1,0:T(8,128)S(1)}, f32[144,128]{1,0:T(8,128)S(1)}, u32[]{:S(2)}, u32[]{:S(2)}) collective-permute-start(f32[144,128]{1,0:T(8,128)S(1)} %get-tuple-element.77), channel_id=1, source_target_pairs={{0,12},{4,8},{8,4},{12,0},{16,28},{20,24},{24,20},{28,16},{1,13},{... | collective-permute-start | bytes 221192 | tf_op jit(solution)/shard_map/ppermute | solution.py:908
  75.1 7.7 %collective-permute-start.24 = (f32[144,128]{1,0:T(8,128)S(1)}, f32[144,128]{1,0:T(8,128)S(1)}, u32[]{:S(2)}, u32[]{:S(2)}) collective-permute-start(f32[144,128]{1,0:T(8,128)S(1)} %get-tuple-element.78), channel_id=1, source_target_pairs={{0,8},{4,12},{8,0},{12,4},{16,24},{20,28},{24,16},{28,20},{1,9},{5... | collective-permute-start | bytes 221192 | tf_op jit(solution)/shard_map/ppermute | solution.py:908
  77.2 5.7 %collective-permute-start.25 = (f32[144,128]{1,0:T(8,128)S(1)}, f32[144,128]{1,0:T(8,128)S(1)}, u32[]{:S(2)}, u32[]{:S(2)}) collective-permute-start(f32[144,128]{1,0:T(8,128)S(1)} %get-tuple-element.79), channel_id=1, source_target_pairs={{0,4},{4,0},{8,12},{12,8},{16,20},{20,16},{24,28},{28,24},{1,5},{5... | collective-permute-start | bytes 221192 | tf_op jit(solution)/shard_map/ppermute | solution.py:908

commit v5 on v4

--- a/solution.py
+++ b/solution.py
@@ -711,10 +711,23 @@
         for i in range(count):
             if i & step == 0:
                 a, b = values[i], values[i + step]
+                if 2 * reach == LANES:
+                    crossed = pltpu.roll(jnp.where(keep, b, a), reach, 1)
+                    values[i] = jnp.where(keep, a, crossed)
+                    values[i + step] = jnp.where(keep, crossed, b)
+                    continue
                 values[i] = jnp.where(keep, a, pltpu.roll(b, reach, 1))
                 values[i + step] = jnp.where(keep, pltpu.roll(a, LANES - reach, 1), b)
         step //= 2
     return values
+
+
+def copy_kernel(source, target):
+    target[...] = source[...]
+
+
+def copied(array):
+    return call(copy_kernel, float32(*array.shape), [], [array], [], 1, 8 * array.size)
 
 
 def transform_z_kernel(sizes, counts, table_high, table_low, *refs):
@@ -744,14 +757,18 @@
                 part = pltpu.roll(part, moved, 1) if moved else part
                 layer = part if i == 0 else jnp.where(lane < i * size_z, layer, part)
             turned[block, pl.ds(columns + end, height, stride=2), :] = layer
-    for x in range(size_x):
-        ends = jnp.zeros((height, LANES), jnp.float32)
-        for i in range(parts_z):
-            part = pltpu.roll(edges[i], (2 * i - 2 * size_z - 2 * x) % LANES, 1)
-            ends = jnp.where((lane >= 2 * i) & (lane < 2 * i + 2), part, ends)
-        turned[blocks, pl.ds(x, height, stride=size_x), :] = ends
-    turned[blocks, columns:] = jnp.zeros((2 * height, LANES), jnp.float32)
-    lines = jnp.concatenate([turned[b] for b in range(blocks + 1)], axis=1)
+        for i in range(group):
+            moved = (i - 2) * size_z % LANES
+            part = edges[block * group + i]
+            part = pltpu.roll(part, moved, 1) if moved else part
+            ends = part if i == 0 else jnp.where(lane < i * size_z, ends, part)
+        for x in range(size_x):
+            moved = -2 * x % LANES
+            turned[blocks + block, pl.ds(x, height, stride=size_x), :] = (
+                pltpu.roll(ends, moved, 1) if moved else ends
+            )
+        turned[blocks + block, columns:] = jnp.zeros((2 * height, LANES), jnp.float32)
+    lines = jnp.concatenate([turned[b] for b in range(2 * blocks)], axis=1)
     high, low = split(lines)
     result = lax.dot_general(
         table_high[...], high, TRANSPOSED, preferred_element_type=jnp.float32
@@ -785,7 +802,7 @@
     length_z = size_z * parts_z
     height = size_y // parts_z
     columns = height * size_x
-    assert 2 * parts_z <= LANES and 4 * height <= LANES
+    assert 4 * height <= LANES
     rows = 2 * length_z // parts_x
     return call(
         functools.partial(transform_z_kernel, sizes, counts),
@@ -794,7 +811,7 @@
         [*table, *pieces],
         [
             pltpu.VMEM((parts_z, *pieces[0].shape), jnp.float32),
-            pltpu.VMEM((length_z // LANES + 1, columns + 2 * height, LANES), jnp.float32),
+            pltpu.VMEM((2 * length_z // LANES, columns + 2 * height, LANES), jnp.float32),
             pltpu.VMEM((2 * length_z, columns + LANES), jnp.float32),
         ],
         24 * length_z * length_z * columns,
@@ -880,10 +897,10 @@
     modes, size = length // blocks, length // parts
     table = np.stack([cosine, -sine]).reshape(2, blocks, modes, length)
     table = table.transpose(1, 0, 2, 3).reshape(2 * length, length)
-    ends = np.zeros((2 * length, LANES))
+    ends = np.zeros((2 * length, length))
     for part in range(parts):
-        ends[:, 2 * part] = 0.5 * table[:, (part * size - 1) % length]
-        ends[:, 2 * part + 1] = -0.5 * table[:, (part + 1) * size % length]
+        ends[:, part * size] = 0.5 * table[:, (part * size - 1) % length]
+        ends[:, part * size + 1] = -0.5 * table[:, (part + 1) * size % length]
     return split_table(np.concatenate([table, ends], axis=1))
 
 
@@ -904,10 +921,10 @@
 def exchange(pieces, axis):
     devices = lax.axis_size(axis)
     assert devices & (devices - 1) == 0
-    return [pieces[0]] + [
-        lax.ppermute(piece, axis, [(i, i ^ step) for i in range(devices)])
-        for piece, step in zip(pieces[1:], steps(devices)[1:])
-    ]
+    received = [pieces[0]]
+    for piece, step in zip(pieces[1:], steps(devices)[1:]):
+        received.append(lax.ppermute(piece, axis, [(i, i ^ step) for i in range(devices)]))
+    return received
 
 
 def on_device(
@@ -956,6 +973,7 @@
     pieces = exchange(pieces, "gz")
     pieces = transform_z(sizes, counts, table_z(length_z, *counts), pieces)
     pieces = exchange(pieces, "gx")
+    velocity = copied(velocity)
     scale = 1.0 / math.sqrt(length_x * length_z)
     table = table_x(length_x, counts[0], size_y // counts[1], scale)
     source = transform_x(sizes, counts, table, pieces)

time: 85 us -> 84.1 us (0.989)
  waiting for transfers between devices: 25.7 us -> 24.7 us
    ppermute x10, waiting for transfers between devices: 8.76 us -> 7.84 us  [exchange(): lax.ppermute(piece, axis, [(i, i ^ step) for i in range(devices)])]
    pallas_call x12 -> x13, Pallas kernels: 20.8 us -> 20.8 us  [call(): pl.pallas_call(kernel, out_shape=out_shape, in_specs=[IN_SMEM] * len(scal...]
  transfers between devices with their start and end apart: 26 -> 26, of which waited for: 14 -> 14; matrix products, arithmetic and copies ran while one was open for 0% -> 0% of each run, Pallas kernels for 9% -> 10%
where the time goes in v5:
time: 84.1 us; the launch traced here: 83.9 us
  starting transfers between devices  33.3 us (40%)
  waiting for transfers between devices  24.7 us (29%)
  Pallas kernels  22.9 us (27%)
  local copies, waits for them, and re-layouts  2.06 us (2%)
  between operations  0.85 us (1%)
    pallas_call x13, Pallas kernels, call(): pl.pallas_call(kernel, out_shape=out_shape, in_specs=[IN_SMEM] * len(scal...  20.8 us
    ppermute x16, starting transfers between devices, swap(): return lax.ppermute(array, axis, pairs)  20.1 us
    ppermute x16, waiting for transfers between devices, swap(): return lax.ppermute(array, axis, pairs)  16.9 us
    ppermute x10, starting transfers between devices, exchange(): lax.ppermute(piece, axis, [(i, i ^ step) for i in range(devices)])  13.1 us
    ppermute x10, waiting for transfers between devices, exchange(): lax.ppermute(piece, axis, [(i, i ^ step) for i in range(devices)])  7.84 us
    pallas_call x1, Pallas kernels, pack(): pl.pallas_call(functools.partial(pack_kernel, layout), out_shape=[float32...  2.06 us
    unnamed x16, local copies, waits for them, and re-layouts  2.06 us
  transfers between devices with their start and end apart: 26, of which 14 were waited for; matrix products, arithmetic and copies ran while one was open for 0% of the time, Pallas kernels for 10%

profile of v5, /device:TPU:0, one launch (start us, length us, event | category | flops | bytes accessed | tf_op | source)
XLA Modules:
  0.0 83.9 jit_solution(1577172332901580920)
XLA Ops:
  0.6 2.1 %pack.1 = (f32[104,128]{1,0:T(8,128)}, f32[128,128]{1,0:T(8,128)}, f32[128,128]{1,0:T(8,128)}, f32[168,128]{1,0:T(8,128)}, f32[168,128]{1,0:T(8,128)}) custom-call(s32[8]{0:T(128)} %slot_ids_hbm.1, s32[3,8]{1,0:T(4,128)} %corners_hbm.1, f32[4,16,32,128]{3,2,1,0:T(8,128)} %flow.3, s32[3,8,512]{2,1,0:T(8,128)} %cells_hbm.1, f32[3,8,512]{2,1,0:T(8,128)} %fraction_hbm.1), custom_call_target="tpu_custom_call" | custom-call | flops 262144 | bytes 262144 | tf_op jit(solution)/shard_map/pack/pallas_call | solution.py:474
  2.7 3.1 %collective-permute-start = (f32[104,128]{1,0:T(8,128)}, f32[104,128]{1,0:T(8,128)S(1)}, u32[]{:S(2)}, u32[]{:S(2)}) collective-permute-start(f32[104,128]{1,0:T(8,128)} %get-tuple-element.41.own), channel_id=1, source_target_pairs={{0,4},{4,0},{8,12},{12,8},{16,20},{20,16},{24,28},{28,24},{1,5},{5... | collective-permute-start | bytes 159752 | tf_op jit(solution)/shard_map/ppermute | solution.py:49
  5.8 3.5 %collective-permute-start.1 = (f32[104,128]{1,0:T(8,128)}, f32[104,128]{1,0:T(8,128)S(1)}, u32[]{:S(2)}, u32[]{:S(2)}) collective-permute-start(f32[104,128]{1,0:T(8,128)} %get-tuple-element.41.own), channel_id=1, source_target_pairs={{0,28},{4,8},{8,4},{12,16},{16,12},{20,24},{24,20},{28,0},{1,29},{... | collective-permute-start | bytes 159752 | tf_op jit(solution)/shard_map/ppermute | solution.py:49
  9.3 3.5 %collective-permute-done.1.right.side_1 = f32[104,128]{1,0:T(8,128)S(1)} collective-permute-done((f32[104,128]{1,0:T(8,128)}, f32[104,128]{1,0:T(8,128)S(1)}, u32[]{:S(2)}, u32[]{:S(2)}) %collective-permute-start.1) | collective-permute-done | bytes 53280 | tf_op jit(solution)/shard_map/ppermute | solution.py:49
  12.8 0.1 collective-permute-start.4
  12.9 1.6 %collective-permute-start.5 = (f32[208,128]{1,0:T(8,128)S(1)}, f32[208,128]{1,0:T(8,128)S(1)}, u32[]{:S(2)}, u32[]{:S(2)}) collective-permute-start(f32[208,128]{1,0:T(8,128)S(1)} %shard_map.123), channel_id=1, source_target_pairs={{0,3},{1,2},{2,1},{3,0},{4,7},{5,6},{6,5},{7,4},{8,11},{9,10},{10,... | collective-permute-start | bytes 319496 | tf_op jit(solution)/shard_map/ppermute | solution.py:49
  14.5 0.1 collective-permute-start.2
  14.6 0.6 collective-permute-start.3
  15.1 3.5 %collective-permute-start.7 = (f32[128,128]{1,0:T(8,128)}, f32[128,128]{1,0:T(8,128)S(1)}, u32[]{:S(2)}, u32[]{:S(2)}) collective-permute-start(f32[128,128]{1,0:T(8,128)} %get-tuple-element.54), channel_id=1, source_target_pairs={{0,28},{4,8},{8,4},{12,16},{16,12},{20,24},{24,20},{28,0},{1,29},{... | collective-permute-start | bytes 196616 | tf_op jit(solution)/shard_map/ppermute | solution.py:49
  18.7 1.2 %copy-done = f32[4,16,32,128]{3,2,1,0:T(8,128)S(1)} copy-done((f32[4,16,32,128]{3,2,1,0:T(8,128)S(1)}, f32[4,16,32,128]{3,2,1,0:T(8,128)}, u32[]{:S(2)}) %copy-start) | copy-done | bytes 1048600
  19.9 0.8 copy-done.3
  20.7 0.9 %shard_map.122 = (f32[3,16,32,128]{3,2,1,0:T(8,128)S(1)}, f32[32,128]{1,0:T(8,128)S(1)}, f32[32,128]{1,0:T(8,128)S(1)}, f32[16,128]{1,0:T(8,128)S(1)}, f32[16,128]{1,0:T(8,128)S(1)}, /*index=5*/f32[104,128]{1,0:T(8,128)S(1)}) custom-call(f32[4,16,32,128]{3,2,1,0:T(8,128)S(1)} %copy-done, f32[104,128]{1,0:T(8,128)S(1)} %copy-done.3), custom_call_target="tpu_custom_call" | custom-call | flops 52428800 | bytes 2097152 | tf_op jit(solution)/shard_map/pallas_call | solution.py:35
  21.6 0.7 collective-permute-done.7.x_1
  22.3 0.3 shard_map.125
  22.7 0.1 shard_map.124
  22.8 4.3 %shard_map.126 = (f32[3,24,512]{2,1,0:T(8,128)S(1)}, f32[3,24,512]{2,1,0:T(8,128)S(1)}, f32[24,80,512]{2,1,0:T(8,128)S(1)}, f32[24,80,512]{2,1,0:T(8,128)S(1)}) custom-call(s32[8,128]{1,0:T(8,128)S(1)} %get-tuple-element.45.facts, f32[312,128]{1,0:T(8,128)S(1)} %get-tuple-element.46.refs_0_, f32[312,128]{1,0:T(8,128)S(1)} %get-tuple-element.47.refs_1_, ...), custom_call_target="tpu_custom_call" | custom-call | flops 7247757312 | bytes 1572864 | tf_op jit(solution)/shard_map/pallas_call | solution.py:35
  27.0 0.1 collective-permute-start.8
  27.2 2.5 %shard_map.128 = (f32[3,16,512]{2,1,0:T(8,128)S(1)}, f32[16,80,512]{2,1,0:T(8,128)S(1)}) custom-call(s32[8,128]{1,0:T(8,128)S(1)} %get-tuple-element.45.facts, f32[312,128]{1,0:T(8,128)S(1)} %get-tuple-element.59.refs_0_, f32[3,128,512]{2,1,0:T(8,128)S(1)} %get-tuple-element.55.refs_2_.refs_1_, f32[3,128,512]{2,1,0:T(8,128)S(1)} %get-tuple-element.56.refs_3_.refs_2_), custom_call_target="tpu_custom_call" | custom-call | flops 2415919104 | bytes 1572864 | tf_op jit(solution)/shard_map/pallas_call | solution.py:35
  29.7 3.0 %collective-permute-done.9 = f32[3,24,512]{2,1,0:T(8,128)S(1)} collective-permute-done((f32[3,24,512]{2,1,0:T(8,128)S(1)}, f32[3,24,512]{2,1,0:T(8,128)S(1)}, u32[]{:S(2)}, u32[]{:S(2)}) %collective-permute-start.9) | collective-permute-done | bytes 147488 | tf_op jit(solution)/shard_map/ppermute | solution.py:49
  32.7 3.8 %collective-permute-start.11 = (f32[3,8,512]{2,1,0:T(8,128)S(1)}, f32[3,8,512]{2,1,0:T(8,128)S(1)}, u32[]{:S(2)}, u32[]{:S(2)}) collective-permute-start(f32[3,8,512]{2,1,0:T(8,128)S(1)} %get-tuple-element.81), channel_id=1, source_target_pairs={{0,28},{4,8},{8,4},{12,16},{16,12},{20,24},{24,20},{28,0},{1,29},{... | collective-permute-start | bytes 147464 | tf_op jit(solution)/shard_map/ppermute | solution.py:49
  36.5 0.8 shard_map.127
  37.3 2.7 %collective-permute-done.11 = f32[3,8,512]{2,1,0:T(8,128)S(1)} collective-permute-done((f32[3,8,512]{2,1,0:T(8,128)S(1)}, f32[3,8,512]{2,1,0:T(8,128)S(1)}, u32[]{:S(2)}, u32[]{:S(2)}) %collective-permute-start.11) | collective-permute-done | bytes 49184 | tf_op jit(solution)/shard_map/ppermute | solution.py:49
  40.0 0.8 collective-permute-done.10
  40.9 2.6 %collective-permute-start.13 = (f32[3,8,512]{2,1,0:T(8,128)S(1)}, f32[3,8,512]{2,1,0:T(8,128)S(1)}, u32[]{:S(2)}, u32[]{:S(2)}) collective-permute-start(f32[3,8,512]{2,1,0:T(8,128)S(1)} %fusion.1.push), channel_id=1, source_target_pairs={{0,28},{4,8},{8,4},{12,16},{16,12},{20,24},{24,20},{28,0},{1,29},{... | collective-permute-start | bytes 147464 | tf_op jit(solution)/shard_map/ppermute | solution.py:49
  43.4 0.8 shard_map.129.before
  44.2 4.0 %collective-permute-done.13 = f32[3,8,512]{2,1,0:T(8,128)S(1)} collective-permute-done((f32[3,8,512]{2,1,0:T(8,128)S(1)}, f32[3,8,512]{2,1,0:T(8,128)S(1)}, u32[]{:S(2)}, u32[]{:S(2)}) %collective-permute-start.13) | collective-permute-done | bytes 49184 | tf_op jit(solution)/shard_map/ppermute | solution.py:49
  48.3 0.3 collective-permute-done.12
  48.6 1.1 %collective-permute-start.15 = (f32[3,24,512]{2,1,0:T(8,128)S(1)}, f32[3,24,512]{2,1,0:T(8,128)S(1)}, u32[]{:S(2)}, u32[]{:S(2)}) collective-permute-start(f32[3,24,512]{2,1,0:T(8,128)S(1)} %pad_maximum_fusion.push), channel_id=1, source_target_pairs={{0,3},{1,2},{2,1},{3,0},{4,7},{5,6},{6,5},{7,4},{8,11},{9,10},{10,... | collective-permute-start | bytes 442376 | tf_op jit(solution)/shard_map/ppermute | solution.py:49
  49.8 2.6 %shard_map.130.before = f32[3,128,512]{2,1,0:T(8,128)S(1)} custom-call(s32[8,128]{1,0:T(8,128)S(1)} %get-tuple-element.45.facts, f32[16,80,512]{2,1,0:T(8,128)S(1)} %get-tuple-element.64.saved, f32[3,24,512]{2,1,0:T(8,128)S(1)} %pad_maximum_fusion.push, f32[3,128,512]{2,1,0:T(8,128)S(1)} %shard_map.129.before), custom_call_target="tpu_custom_call" | custom-call | flops 2415919104 | bytes 1572864 | tf_op jit(solution)/shard_map/pallas_call | solution.py:35
  52.4 1.9 %collective-permute-done.15.push_1 = f32[3,24,512]{2,1,0:T(8,128)S(1)} collective-permute-done((f32[3,24,512]{2,1,0:T(8,128)S(1)}, f32[3,24,512]{2,1,0:T(8,128)S(1)}, u32[]{:S(2)}, u32[]{:S(2)}) %collective-permute-start.15) | collective-permute-done | bytes 147488 | tf_op jit(solution)/shard_map/ppermute | solution.py:49
  54.3 5.0 %shard_map.131 = (f32[3,16,32,128]{3,2,1,0:T(8,128)S(1)}, f32[32,640]{1,0:T(8,128)S(1)}, f32[32,640]{1,0:T(8,128)S(1)}, f32[32,640]{1,0:T(8,128)S(1)}, f32[32,640]{1,0:T(8,128)S(1)}) custom-call(s32[8,128]{1,0:T(8,128)S(1)} %get-tuple-element.45.facts, f32[24,80,512]{2,1,0:T(8,128)S(1)} %get-tuple-element.57.saved_0, ...), custom_call_target="tpu_custom_call" | custom-call | flops 7247757312 | bytes 2359296 | tf_op jit(solution)/shard_map/pallas_call | solution.py:35
  59.3 1.2 %collective-permute-start.17 = (f32[32,640]{1,0:T(8,128)S(1)}, f32[32,640]{1,0:T(8,128)S(1)}, u32[]{:S(2)}, u32[]{:S(2)}) collective-permute-start(f32[32,640]{1,0:T(8,128)S(1)} %get-tuple-element.70), channel_id=1, source_target_pairs={{0,2},{1,3},{2,0},{3,1},{4,6},{5,7},{6,4},{7,5},{8,10},{9,11},{10,... | collective-permute-start | bytes 245768 | tf_op jit(solution)/shard_map/ppermute | solution.py:926
  60.5 0.7 collective-permute-start.18
  61.2 2.9 %collective-permute-done.16.refs_1_ = f32[32,640]{1,0:T(8,128)S(1)} collective-permute-done((f32[32,640]{1,0:T(8,128)S(1)}, f32[32,640]{1,0:T(8,128)S(1)}, u32[]{:S(2)}, u32[]{:S(2)}) %collective-permute-start.16) | collective-permute-done | bytes 81952 | tf_op jit(solution)/shard_map/ppermute | solution.py:926
  64.0 1.3 %collective-permute-done.17.refs_2_ = f32[32,640]{1,0:T(8,128)S(1)} collective-permute-done((f32[32,640]{1,0:T(8,128)S(1)}, f32[32,640]{1,0:T(8,128)S(1)}, u32[]{:S(2)}, u32[]{:S(2)}) %collective-permute-start.17) | collective-permute-done | bytes 81952 | tf_op jit(solution)/shard_map/ppermute | solution.py:926
  65.3 0.9 %shard_map.133 = (f32[144,128]{1,0:T(8,128)S(1)}, f32[144,128]{1,0:T(8,128)S(1)}, f32[144,128]{1,0:T(8,128)S(1)}, f32[144,128]{1,0:T(8,128)S(1)}, f32[144,128]{1...) custom-call(bf16[256,256]{1,0:T(8,128)(2,1)S(1)} %copy-done.6, ...), custom_call_target="tpu_custom_call" | custom-call | flops 201326592 | bytes 786432 | tf_op jit(solution)/shard_map/pallas_call | solution.py:35
  66.2 2.8 %collective-permute-start.19 = (f32[144,128]{1,0:T(8,128)S(1)}, f32[144,128]{1,0:T(8,128)S(1)}, u32[]{:S(2)}, u32[]{:S(2)}) collective-permute-start(f32[144,128]{1,0:T(8,128)S(1)} %get-tuple-element.73), channel_id=1, source_target_pairs={{0,28},{4,24},{8,20},{12,16},{16,12},{20,8},{24,4},{28,0},{1,29},{... | collective-permute-start | bytes 221192 | tf_op jit(solution)/shard_map/ppermute | solution.py:926
  69.0 1.6 %collective-permute-start.20 = (f32[144,128]{1,0:T(8,128)S(1)}, f32[144,128]{1,0:T(8,128)S(1)}, u32[]{:S(2)}, u32[]{:S(2)}) collective-permute-start(f32[144,128]{1,0:T(8,128)S(1)} %get-tuple-element.74), channel_id=1, source_target_pairs={{0,24},{4,28},{8,16},{12,20},{16,8},{20,12},{24,0},{28,4},{1,25},{... | collective-permute-start | bytes 221192 | tf_op jit(solution)/shard_map/ppermute | solution.py:926
  70.6 3.4 %collective-permute-start.22 = (f32[144,128]{1,0:T(8,128)S(1)}, f32[144,128]{1,0:T(8,128)S(1)}, u32[]{:S(2)}, u32[]{:S(2)}) collective-permute-start(f32[144,128]{1,0:T(8,128)S(1)} %get-tuple-element.76), channel_id=1, source_target_pairs={{0,16},{4,20},{8,24},{12,28},{16,0},{20,4},{24,8},{28,12},{1,17},{... | collective-permute-start | bytes 221192 | tf_op jit(solution)/shard_map/ppermute | solution.py:926
  73.9 0.4 collective-permute-start.23
  74.3 2.1 %collective-permute-start.24 = (f32[144,128]{1,0:T(8,128)S(1)}, f32[144,128]{1,0:T(8,128)S(1)}, u32[]{:S(2)}, u32[]{:S(2)}) collective-permute-start(f32[144,128]{1,0:T(8,128)S(1)} %get-tuple-element.78), channel_id=1, source_target_pairs={{0,8},{4,12},{8,0},{12,4},{16,24},{20,28},{24,16},{28,20},{1,9},{5... | collective-permute-start | bytes 221192 | tf_op jit(solution)/shard_map/ppermute | solution.py:926
  76.4 1.0 %collective-permute-start.25 = (f32[144,128]{1,0:T(8,128)S(1)}, f32[144,128]{1,0:T(8,128)S(1)}, u32[]{:S(2)}, u32[]{:S(2)}) collective-permute-start(f32[144,128]{1,0:T(8,128)S(1)} %get-tuple-element.79), channel_id=1, source_target_pairs={{0,4},{4,0},{8,12},{12,8},{16,20},{20,16},{24,28},{28,24},{1,5},{5... | collective-permute-start | bytes 221192 | tf_op jit(solution)/shard_map/ppermute | solution.py:926
  77.4 0.9 %shard_map.132 = f32[3,16,32,128]{3,2,1,0:T(8,128)} custom-call(f32[3,16,32,128]{3,2,1,0:T(8,128)S(1)} %get-tuple-element.67.source), custom_call_target="tpu_custom_call" | custom-call | flops 1 | bytes 1572864 | tf_op jit(solution)/shard_map/pallas_call | solution.py:35
  78.4 1.6 %collective-permute-done.21.refs_3_ = f32[144,128]{1,0:T(8,128)S(1)} collective-permute-done((f32[144,128]{1,0:T(8,128)S(1)}, f32[144,128]{1,0:T(8,128)S(1)}, u32[]{:S(2)}, u32[]{:S(2)}) %collective-permute-start.21) | collective-permute-done | bytes 73760 | tf_op jit(solution)/shard_map/ppermute | solution.py:926
  80.0 1.2 %collective-permute-done.22.refs_4_ = f32[144,128]{1,0:T(8,128)S(1)} collective-permute-done((f32[144,128]{1,0:T(8,128)S(1)}, f32[144,128]{1,0:T(8,128)S(1)}, u32[]{:S(2)}, u32[]{:S(2)}) %collective-permute-start.22) | collective-permute-done | bytes 73760 | tf_op jit(solution)/shard_map/ppermute | solution.py:926
  81.2 0.4 collective-permute-done.23.refs_5_
  81.6 0.5 collective-permute-done.24.refs_6_
  82.1 1.8 %shard_map.134 = f32[2,32,16,128]{3,2,1,0:T(8,128)} custom-call(bf16[384,256]{1,0:T(8,128)(2,1)S(1)} %copy-done.1, bf16[384,256]{1,0:T(8,128)(2,1)S(1)} %copy-done.2, f32[144,128]{1,0:T(8,128)S(1)} %get-tuple-element.72.refs_0_, f32[144,128]{1,0:T(8,128)S(1)} %collective-permute-done.19.refs_1_, f32[144,128]{1,0:T(8,128)S(1)} %collective-permute-done.20.refs_2_, ...), custom_call_target="tpu_custom_call" | custom-call | flops 201326592 | bytes 1572864 | tf_op jit(solution)/shard_map/pallas_call | solution.py:35
  (38 shorter events, 0.4 us)
Async XLA Ops:
  2.7 6.6 %collective-permute-start = (f32[104,128]{1,0:T(8,128)}, f32[104,128]{1,0:T(8,128)S(1)}, u32[]{:S(2)}, u32[]{:S(2)}) collective-permute-start(f32[104,128]{1,0:T(8,128)} %get-tuple-element.41.own), channel_id=1, source_target_pairs={{0,4},{4,0},{8,12},{12,8},{16,20},{20,16},{24,28},{28,24},{1,5},{5... | collective-permute-start | bytes 159752 | tf_op jit(solution)/shard_map/ppermute | solution.py:49
  5.8 7.0 %collective-permute-start.1 = (f32[104,128]{1,0:T(8,128)}, f32[104,128]{1,0:T(8,128)S(1)}, u32[]{:S(2)}, u32[]{:S(2)}) collective-permute-start(f32[104,128]{1,0:T(8,128)} %get-tuple-element.41.own), channel_id=1, source_target_pairs={{0,28},{4,8},{8,4},{12,16},{16,12},{20,24},{24,20},{28,0},{1,29},{... | collective-permute-start | bytes 159752 | tf_op jit(solution)/shard_map/ppermute | solution.py:49
  9.3 5.8 %collective-permute-start.6 = (f32[128,128]{1,0:T(8,128)}, f32[128,128]{1,0:T(8,128)S(1)}, u32[]{:S(2)}, u32[]{:S(2)}) collective-permute-start(f32[128,128]{1,0:T(8,128)} %get-tuple-element.53), channel_id=1, source_target_pairs={{0,4},{4,0},{8,12},{12,8},{16,20},{20,16},{24,28},{28,24},{1,5},{5... | collective-permute-start | bytes 196616 | tf_op jit(solution)/shard_map/ppermute | solution.py:49
  12.8 9.8 %collective-permute-start.4 = (f32[208,128]{1,0:T(8,128)S(1)}, f32[208,128]{1,0:T(8,128)S(1)}, u32[]{:S(2)}, u32[]{:S(2)}) collective-permute-start(f32[208,128]{1,0:T(8,128)S(1)} %shard_map.123), channel_id=1, source_target_pairs={{0,1},{1,0},{2,3},{3,2},{4,5},{5,4},{6,7},{7,6},{8,9},{9,8},{10,11... | collective-permute-start | bytes 319496 | tf_op jit(solution)/shard_map/ppermute | solution.py:49
  12.9 9.8 %collective-permute-start.5 = (f32[208,128]{1,0:T(8,128)S(1)}, f32[208,128]{1,0:T(8,128)S(1)}, u32[]{:S(2)}, u32[]{:S(2)}) collective-permute-start(f32[208,128]{1,0:T(8,128)S(1)} %shard_map.123), channel_id=1, source_target_pairs={{0,3},{1,2},{2,1},{3,0},{4,7},{5,6},{6,5},{7,4},{8,11},{9,10},{10,... | collective-permute-start | bytes 319496 | tf_op jit(solution)/shard_map/ppermute | solution.py:49
  14.5 7.8 %collective-permute-start.2 = (f32[168,128]{1,0:T(8,128)}, f32[168,128]{1,0:T(8,128)S(1)}, u32[]{:S(2)}, u32[]{:S(2)}) collective-permute-start(f32[168,128]{1,0:T(8,128)} %get-tuple-element.43), channel_id=1, source_target_pairs={{0,1},{1,0},{2,3},{3,2},{4,5},{5,4},{6,7},{7,6},{8,9},{9,8},{10,11... | collective-permute-start | bytes 258056 | tf_op jit(solution)/shard_map/ppermute | solution.py:49
  14.6 7.8 %collective-permute-start.3 = (f32[168,128]{1,0:T(8,128)}, f32[168,128]{1,0:T(8,128)S(1)}, u32[]{:S(2)}, u32[]{:S(2)}) collective-permute-start(f32[168,128]{1,0:T(8,128)} %get-tuple-element.44), channel_id=1, source_target_pairs={{0,3},{1,2},{2,1},{3,0},{4,7},{5,6},{6,5},{7,4},{8,11},{9,10},{10,... | collective-permute-start | bytes 258056 | tf_op jit(solution)/shard_map/ppermute | solution.py:49
  15.1 7.2 %collective-permute-start.7 = (f32[128,128]{1,0:T(8,128)}, f32[128,128]{1,0:T(8,128)S(1)}, u32[]{:S(2)}, u32[]{:S(2)}) collective-permute-start(f32[128,128]{1,0:T(8,128)} %get-tuple-element.54), channel_id=1, source_target_pairs={{0,28},{4,8},{8,4},{12,16},{16,12},{20,24},{24,20},{28,0},{1,29},{... | collective-permute-start | bytes 196616 | tf_op jit(solution)/shard_map/ppermute | solution.py:49
  18.7 1.2 %copy-start = (f32[4,16,32,128]{3,2,1,0:T(8,128)S(1)}, f32[4,16,32,128]{3,2,1,0:T(8,128)}, u32[]{:S(2)}) copy-start(f32[4,16,32,128]{3,2,1,0:T(8,128)} %flow.3) | copy-start | bytes 3145732
  19.9 0.8 copy-start.3
  27.0 2.7 %collective-permute-start.8 = (f32[3,24,512]{2,1,0:T(8,128)S(1)}, f32[3,24,512]{2,1,0:T(8,128)S(1)}, u32[]{:S(2)}, u32[]{:S(2)}) collective-permute-start(f32[3,24,512]{2,1,0:T(8,128)S(1)} %get-tuple-element.61), channel_id=1, source_target_pairs={{0,1},{1,0},{2,3},{3,2},{4,5},{5,4},{6,7},{7,6},{8,9},{9,8},{10,11... | collective-permute-start | bytes 442376 | tf_op jit(solution)/shard_map/ppermute | solution.py:49
  27.1 5.6 %collective-permute-start.9 = (f32[3,24,512]{2,1,0:T(8,128)S(1)}, f32[3,24,512]{2,1,0:T(8,128)S(1)}, u32[]{:S(2)}, u32[]{:S(2)}) collective-permute-start(f32[3,24,512]{2,1,0:T(8,128)S(1)} %get-tuple-element.62), channel_id=1, source_target_pairs={{0,3},{1,2},{2,1},{3,0},{4,7},{5,6},{6,5},{7,4},{8,11},{9,10},{10,... | collective-permute-start | bytes 442376 | tf_op jit(solution)/shard_map/ppermute | solution.py:49
  27.2 9.4 %copy-start.4 = (f32[3,128]{1,0:T(4,128)S(1)}, f32[3,128]{1,0:T(4,128)}, u32[]{:S(2)}) copy-start(f32[3,128]{1,0:T(4,128)} %refs_3_.1) | copy-start | bytes 4612
  27.2 9.3 %copy-start.5 = (f32[3,128]{1,0:T(4,128)S(1)}, f32[3,128]{1,0:T(4,128)}, u32[]{:S(2)}) copy-start(f32[3,128]{1,0:T(4,128)} %refs_4_.1) | copy-start | bytes 4612
  32.7 7.2 %collective-permute-start.11 = (f32[3,8,512]{2,1,0:T(8,128)S(1)}, f32[3,8,512]{2,1,0:T(8,128)S(1)}, u32[]{:S(2)}, u32[]{:S(2)}) collective-permute-start(f32[3,8,512]{2,1,0:T(8,128)S(1)} %get-tuple-element.81), channel_id=1, source_target_pairs={{0,28},{4,8},{8,4},{12,16},{16,12},{20,24},{24,20},{28,0},{1,29},{... | collective-permute-start | bytes 147464 | tf_op jit(solution)/shard_map/ppermute | solution.py:49
  36.5 4.3 %collective-permute-start.10 = (f32[3,8,512]{2,1,0:T(8,128)S(1)}, f32[3,8,512]{2,1,0:T(8,128)S(1)}, u32[]{:S(2)}, u32[]{:S(2)}) collective-permute-start(f32[3,8,512]{2,1,0:T(8,128)S(1)} %get-tuple-element.80), channel_id=1, source_target_pairs={{0,4},{4,0},{8,12},{12,8},{16,20},{20,16},{24,28},{28,24},{1,5},{5... | collective-permute-start | bytes 147464 | tf_op jit(solution)/shard_map/ppermute | solution.py:49
  40.9 7.4 %collective-permute-start.13 = (f32[3,8,512]{2,1,0:T(8,128)S(1)}, f32[3,8,512]{2,1,0:T(8,128)S(1)}, u32[]{:S(2)}, u32[]{:S(2)}) collective-permute-start(f32[3,8,512]{2,1,0:T(8,128)S(1)} %fusion.1.push), channel_id=1, source_target_pairs={{0,28},{4,8},{8,4},{12,16},{16,12},{20,24},{24,20},{28,0},{1,29},{... | collective-permute-start | bytes 147464 | tf_op jit(solution)/shard_map/ppermute | solution.py:49
  43.4 5.1 %collective-permute-start.12 = (f32[3,8,512]{2,1,0:T(8,128)S(1)}, f32[3,8,512]{2,1,0:T(8,128)S(1)}, u32[]{:S(2)}, u32[]{:S(2)}) collective-permute-start(f32[3,8,512]{2,1,0:T(8,128)S(1)} %fusion.1.push), channel_id=1, source_target_pairs={{0,4},{4,0},{8,12},{12,8},{16,20},{20,16},{24,28},{28,24},{1,5},{5... | collective-permute-start | bytes 147464 | tf_op jit(solution)/shard_map/ppermute | solution.py:49
  48.6 3.8 %collective-permute-start.14 = (f32[3,24,512]{2,1,0:T(8,128)S(1)}, f32[3,24,512]{2,1,0:T(8,128)S(1)}, u32[]{:S(2)}, u32[]{:S(2)}) collective-permute-start(f32[3,24,512]{2,1,0:T(8,128)S(1)} %pad_maximum_fusion.push), channel_id=1, source_target_pairs={{0,1},{1,0},{2,3},{3,2},{4,5},{5,4},{6,7},{7,6},{8,9},{9,8},{10,11... | collective-permute-start | bytes 442376 | tf_op jit(solution)/shard_map/ppermute | solution.py:49
  48.6 5.6 %collective-permute-start.15 = (f32[3,24,512]{2,1,0:T(8,128)S(1)}, f32[3,24,512]{2,1,0:T(8,128)S(1)}, u32[]{:S(2)}, u32[]{:S(2)}) collective-permute-start(f32[3,24,512]{2,1,0:T(8,128)S(1)} %pad_maximum_fusion.push), channel_id=1, source_target_pairs={{0,3},{1,2},{2,1},{3,0},{4,7},{5,6},{6,5},{7,4},{8,11},{9,10},{10,... | collective-permute-start | bytes 442376 | tf_op jit(solution)/shard_map/ppermute | solution.py:49
  54.2 11.1 %copy-start.6 = (bf16[256,256]{1,0:T(8,128)(2,1)S(1)}, bf16[256,256]{1,0:T(8,128)(2,1)}, u32[]{:S(2)}) copy-start(bf16[256,256]{1,0:T(8,128)(2,1)} %constant.8.clone.table_high) | copy-start | bytes 393220
  54.2 11.1 %copy-start.7 = (bf16[256,256]{1,0:T(8,128)(2,1)S(1)}, bf16[256,256]{1,0:T(8,128)(2,1)}, u32[]{:S(2)}) copy-start(bf16[256,256]{1,0:T(8,128)(2,1)} %constant.9.clone.table_low) | copy-start | bytes 393220
  54.2 27.8 %copy-start.1 = (bf16[384,256]{1,0:T(8,128)(2,1)S(1)}, bf16[384,256]{1,0:T(8,128)(2,1)}, u32[]{:S(2)}) copy-start(bf16[384,256]{1,0:T(8,128)(2,1)} %constant.10.clone.table_high) | copy-start | bytes 589828
  54.2 27.8 %copy-start.2 = (bf16[384,256]{1,0:T(8,128)(2,1)S(1)}, bf16[384,256]{1,0:T(8,128)(2,1)}, u32[]{:S(2)}) copy-start(bf16[384,256]{1,0:T(8,128)(2,1)} %constant.11.clone.table_low) | copy-start | bytes 589828
  59.2 4.8 %collective-permute-start.16 = (f32[32,640]{1,0:T(8,128)S(1)}, f32[32,640]{1,0:T(8,128)S(1)}, u32[]{:S(2)}, u32[]{:S(2)}) collective-permute-start(f32[32,640]{1,0:T(8,128)S(1)} %get-tuple-element.69), channel_id=1, source_target_pairs={{0,3},{1,2},{2,1},{3,0},{4,7},{5,6},{6,5},{7,4},{8,11},{9,10},{10,... | collective-permute-start | bytes 245768 | tf_op jit(solution)/shard_map/ppermute | solution.py:926
  59.3 6.0 %collective-permute-start.17 = (f32[32,640]{1,0:T(8,128)S(1)}, f32[32,640]{1,0:T(8,128)S(1)}, u32[]{:S(2)}, u32[]{:S(2)}) collective-permute-start(f32[32,640]{1,0:T(8,128)S(1)} %get-tuple-element.70), channel_id=1, source_target_pairs={{0,2},{1,3},{2,0},{3,1},{4,6},{5,7},{6,4},{7,5},{8,10},{9,11},{10,... | collective-permute-start | bytes 245768 | tf_op jit(solution)/shard_map/ppermute | solution.py:926
  60.5 4.8 %collective-permute-start.18 = (f32[32,640]{1,0:T(8,128)S(1)}, f32[32,640]{1,0:T(8,128)S(1)}, u32[]{:S(2)}, u32[]{:S(2)}) collective-permute-start(f32[32,640]{1,0:T(8,128)S(1)} %get-tuple-element.71), channel_id=1, source_target_pairs={{0,1},{1,0},{2,3},{3,2},{4,5},{5,4},{6,7},{7,6},{8,9},{9,8},{10,11... | collective-permute-start | bytes 245768 | tf_op jit(solution)/shard_map/ppermute | solution.py:926
  66.2 8.1 %collective-permute-start.19 = (f32[144,128]{1,0:T(8,128)S(1)}, f32[144,128]{1,0:T(8,128)S(1)}, u32[]{:S(2)}, u32[]{:S(2)}) collective-permute-start(f32[144,128]{1,0:T(8,128)S(1)} %get-tuple-element.73), channel_id=1, source_target_pairs={{0,28},{4,24},{8,20},{12,16},{16,12},{20,8},{24,4},{28,0},{1,29},{... | collective-permute-start | bytes 221192 | tf_op jit(solution)/shard_map/ppermute | solution.py:926
  69.0 7.4 %collective-permute-start.20 = (f32[144,128]{1,0:T(8,128)S(1)}, f32[144,128]{1,0:T(8,128)S(1)}, u32[]{:S(2)}, u32[]{:S(2)}) collective-permute-start(f32[144,128]{1,0:T(8,128)S(1)} %get-tuple-element.74), channel_id=1, source_target_pairs={{0,24},{4,28},{8,16},{12,20},{16,8},{20,12},{24,0},{28,4},{1,25},{... | collective-permute-start | bytes 221192 | tf_op jit(solution)/shard_map/ppermute | solution.py:926
  70.5 9.5 %collective-permute-start.21 = (f32[144,128]{1,0:T(8,128)S(1)}, f32[144,128]{1,0:T(8,128)S(1)}, u32[]{:S(2)}, u32[]{:S(2)}) collective-permute-start(f32[144,128]{1,0:T(8,128)S(1)} %get-tuple-element.75), channel_id=1, source_target_pairs={{0,20},{4,16},{8,28},{12,24},{16,4},{20,0},{24,12},{28,8},{1,21},{... | collective-permute-start | bytes 221192 | tf_op jit(solution)/shard_map/ppermute | solution.py:926
  70.6 10.7 %collective-permute-start.22 = (f32[144,128]{1,0:T(8,128)S(1)}, f32[144,128]{1,0:T(8,128)S(1)}, u32[]{:S(2)}, u32[]{:S(2)}) collective-permute-start(f32[144,128]{1,0:T(8,128)S(1)} %get-tuple-element.76), channel_id=1, source_target_pairs={{0,16},{4,20},{8,24},{12,28},{16,0},{20,4},{24,8},{28,12},{1,17},{... | collective-permute-start | bytes 221192 | tf_op jit(solution)/shard_map/ppermute | solution.py:926
  73.9 7.7 %collective-permute-start.23 = (f32[144,128]{1,0:T(8,128)S(1)}, f32[144,128]{1,0:T(8,128)S(1)}, u32[]{:S(2)}, u32[]{:S(2)}) collective-permute-start(f32[144,128]{1,0:T(8,128)S(1)} %get-tuple-element.77), channel_id=1, source_target_pairs={{0,12},{4,8},{8,4},{12,0},{16,28},{20,24},{24,20},{28,16},{1,13},{... | collective-permute-start | bytes 221192 | tf_op jit(solution)/shard_map/ppermute | solution.py:926
  74.3 7.8 %collective-permute-start.24 = (f32[144,128]{1,0:T(8,128)S(1)}, f32[144,128]{1,0:T(8,128)S(1)}, u32[]{:S(2)}, u32[]{:S(2)}) collective-permute-start(f32[144,128]{1,0:T(8,128)S(1)} %get-tuple-element.78), channel_id=1, source_target_pairs={{0,8},{4,12},{8,0},{12,4},{16,24},{20,28},{24,16},{28,20},{1,9},{5... | collective-permute-start | bytes 221192 | tf_op jit(solution)/shard_map/ppermute | solution.py:926
  76.4 5.7 %collective-permute-start.25 = (f32[144,128]{1,0:T(8,128)S(1)}, f32[144,128]{1,0:T(8,128)S(1)}, u32[]{:S(2)}, u32[]{:S(2)}) collective-permute-start(f32[144,128]{1,0:T(8,128)S(1)} %get-tuple-element.79), channel_id=1, source_target_pairs={{0,4},{4,0},{8,12},{12,8},{16,20},{20,16},{24,28},{28,24},{1,5},{5... | collective-permute-start | bytes 221192 | tf_op jit(solution)/shard_map/ppermute | solution.py:926

commit v6 on v5

--- a/solution.py
+++ b/solution.py
@@ -54,7 +54,8 @@
 
 
 def steps(devices):
-    return [0, *range(devices - 1, 0, -1)]
+    halves = [1 << bit for bit in reversed(range(devices.bit_length() - 1))]
+    return [0] + [step for half in halves for step in range(half, 2 * half)]
 
 
 def in_order(axis, shape):
@@ -962,7 +963,9 @@
     (own_part,), (own_saved,) = sample(layout, (((1,), 1),), facts, (row,), fields, motion)
     push = own_part - (from_z[:, slots : 2 * slots] + from_0 + from_1)
 
-    row_push = jnp.concatenate([swap(push, "gx", 0), push, swap(push, "gx", 1)], axis=1)
+    push_0 = swap(push, "gx", 0)
+    push_1 = swap(push, "gx", 1)
+    row_push = jnp.concatenate([push_0, push, push_1], axis=1)
     rows_push = swap(row_push, "gz", 0), swap(row_push, "gz", 1)
     forcing = spread_own(layout, facts, own_saved, push)
     forcing = spread_side(layout, facts, side_saved, row_push, forcing)

time: 84.1 us -> 86.1 us (1.024)
  waiting for transfers between devices: 24.7 us -> 28.4 us
  starting transfers between devices: 33.3 us -> 31.6 us
    ppermute x10, waiting for transfers between devices: 7.84 us -> 11.4 us  [exchange(): lax.ppermute(piece, axis, [(i, i ^ step) for i in range(devices)])]
    ppermute x10, starting transfers between devices: 13.1 us -> 11.4 us  [exchange(): lax.ppermute(piece, axis, [(i, i ^ step) for i in range(devices)])]
  transfers between devices with their start and end apart: 26 -> 26, of which waited for: 14 -> 13; matrix products, arithmetic and copies ran while one was open for 0% -> 0% of each run, Pallas kernels for 10% -> 10%
where the time goes in v6:
time: 86.1 us; the launch traced here: 85.8 us
  starting transfers between devices  31.6 us (37%)
  waiting for transfers between devices  28.4 us (33%)
  Pallas kernels  22.9 us (27%)
  local copies, waits for them, and re-layouts  2.06 us (2%)
    pallas_call x13, Pallas kernels, call(): pl.pallas_call(kernel, out_shape=out_shape, in_specs=[IN_SMEM] * len(scal...  20.8 us
    ppermute x16, starting transfers between devices, swap(): return lax.ppermute(array, axis, pairs)  20.1 us
    ppermute x16, waiting for transfers between devices, swap(): return lax.ppermute(array, axis, pairs)  16.9 us
    ppermute x10, waiting for transfers between devices, exchange(): lax.ppermute(piece, axis, [(i, i ^ step) for i in range(devices)])  11.4 us
    ppermute x10, starting transfers between devices, exchange(): lax.ppermute(piece, axis, [(i, i ^ step) for i in range(devices)])  11.4 us
    pallas_call x1, Pallas kernels, pack(): pl.pallas_call(functools.partial(pack_kernel, layout), out_shape=[float32...  2.06 us
    unnamed x16, local copies, waits for them, and re-layouts  2.06 us
  transfers between devices with their start and end apart: 26, of which 13 were waited for; matrix products, arithmetic and copies ran while one was open for 0% of the time, Pallas kernels for 10%

profile of v6, /device:TPU:0, one launch (start us, length us, event | category | flops | bytes accessed | tf_op | source)
XLA Modules:
  0.0 85.8 jit_solution(3246641209254588585)
XLA Ops:
  0.6 2.1 %pack.1 = (f32[104,128]{1,0:T(8,128)}, f32[128,128]{1,0:T(8,128)}, f32[128,128]{1,0:T(8,128)}, f32[168,128]{1,0:T(8,128)}, f32[168,128]{1,0:T(8,128)}) custom-call(s32[8]{0:T(128)} %slot_ids_hbm.1, s32[3,8]{1,0:T(4,128)} %corners_hbm.1, f32[4,16,32,128]{3,2,1,0:T(8,128)} %flow.3, s32[3,8,512]{2,1,0:T(8,128)} %cells_hbm.1, f32[3,8,512]{2,1,0:T(8,128)} %fraction_hbm.1), custom_call_target="tpu_custom_call" | custom-call | flops 262144 | bytes 262144 | tf_op jit(solution)/shard_map/pack/pallas_call | solution.py:475
  2.7 3.1 %collective-permute-start = (f32[104,128]{1,0:T(8,128)}, f32[104,128]{1,0:T(8,128)S(1)}, u32[]{:S(2)}, u32[]{:S(2)}) collective-permute-start(f32[104,128]{1,0:T(8,128)} %get-tuple-element.41.own), channel_id=1, source_target_pairs={{0,4},{4,0},{8,12},{12,8},{16,20},{20,16},{24,28},{28,24},{1,5},{5... | collective-permute-start | bytes 159752 | tf_op jit(solution)/shard_map/ppermute | solution.py:49
  5.8 3.5 %collective-permute-start.1 = (f32[104,128]{1,0:T(8,128)}, f32[104,128]{1,0:T(8,128)S(1)}, u32[]{:S(2)}, u32[]{:S(2)}) collective-permute-start(f32[104,128]{1,0:T(8,128)} %get-tuple-element.41.own), channel_id=1, source_target_pairs={{0,28},{4,8},{8,4},{12,16},{16,12},{20,24},{24,20},{28,0},{1,29},{... | collective-permute-start | bytes 159752 | tf_op jit(solution)/shard_map/ppermute | solution.py:49
  9.3 3.5 %collective-permute-done.1.right.side_1 = f32[104,128]{1,0:T(8,128)S(1)} collective-permute-done((f32[104,128]{1,0:T(8,128)}, f32[104,128]{1,0:T(8,128)S(1)}, u32[]{:S(2)}, u32[]{:S(2)}) %collective-permute-start.1) | collective-permute-done | bytes 53280 | tf_op jit(solution)/shard_map/ppermute | solution.py:49
  12.8 0.1 collective-permute-start.4
  12.9 1.6 %collective-permute-start.5 = (f32[208,128]{1,0:T(8,128)S(1)}, f32[208,128]{1,0:T(8,128)S(1)}, u32[]{:S(2)}, u32[]{:S(2)}) collective-permute-start(f32[208,128]{1,0:T(8,128)S(1)} %shard_map.123), channel_id=1, source_target_pairs={{0,3},{1,2},{2,1},{3,0},{4,7},{5,6},{6,5},{7,4},{8,11},{9,10},{10,... | collective-permute-start | bytes 319496 | tf_op jit(solution)/shard_map/ppermute | solution.py:49
  14.5 0.1 collective-permute-start.2
  14.6 0.6 collective-permute-start.3
  15.1 3.5 %collective-permute-start.7 = (f32[128,128]{1,0:T(8,128)}, f32[128,128]{1,0:T(8,128)S(1)}, u32[]{:S(2)}, u32[]{:S(2)}) collective-permute-start(f32[128,128]{1,0:T(8,128)} %get-tuple-element.54), channel_id=1, source_target_pairs={{0,28},{4,8},{8,4},{12,16},{16,12},{20,24},{24,20},{28,0},{1,29},{... | collective-permute-start | bytes 196616 | tf_op jit(solution)/shard_map/ppermute | solution.py:49
  18.7 1.2 %copy-done = f32[4,16,32,128]{3,2,1,0:T(8,128)S(1)} copy-done((f32[4,16,32,128]{3,2,1,0:T(8,128)S(1)}, f32[4,16,32,128]{3,2,1,0:T(8,128)}, u32[]{:S(2)}) %copy-start) | copy-done | bytes 1048600
  19.9 0.8 copy-done.3
  20.7 0.9 %shard_map.122 = (f32[3,16,32,128]{3,2,1,0:T(8,128)S(1)}, f32[32,128]{1,0:T(8,128)S(1)}, f32[32,128]{1,0:T(8,128)S(1)}, f32[16,128]{1,0:T(8,128)S(1)}, f32[16,128]{1,0:T(8,128)S(1)}, /*index=5*/f32[104,128]{1,0:T(8,128)S(1)}) custom-call(f32[4,16,32,128]{3,2,1,0:T(8,128)S(1)} %copy-done, f32[104,128]{1,0:T(8,128)S(1)} %copy-done.3), custom_call_target="tpu_custom_call" | custom-call | flops 52428800 | bytes 2097152 | tf_op jit(solution)/shard_map/pallas_call | solution.py:35
  21.6 0.7 collective-permute-done.7.x_1
  22.3 0.3 shard_map.125
  22.7 0.1 shard_map.124
  22.8 4.3 %shard_map.126 = (f32[3,24,512]{2,1,0:T(8,128)S(1)}, f32[3,24,512]{2,1,0:T(8,128)S(1)}, f32[24,80,512]{2,1,0:T(8,128)S(1)}, f32[24,80,512]{2,1,0:T(8,128)S(1)}) custom-call(s32[8,128]{1,0:T(8,128)S(1)} %get-tuple-element.45.facts, f32[312,128]{1,0:T(8,128)S(1)} %get-tuple-element.46.refs_0_, f32[312,128]{1,0:T(8,128)S(1)} %get-tuple-element.47.refs_1_, ...), custom_call_target="tpu_custom_call" | custom-call | flops 7247757312 | bytes 1572864 | tf_op jit(solution)/shard_map/pallas_call | solution.py:35
  27.0 0.1 collective-permute-start.8
  27.2 2.5 %shard_map.128 = (f32[3,16,512]{2,1,0:T(8,128)S(1)}, f32[16,80,512]{2,1,0:T(8,128)S(1)}) custom-call(s32[8,128]{1,0:T(8,128)S(1)} %get-tuple-element.45.facts, f32[312,128]{1,0:T(8,128)S(1)} %get-tuple-element.59.refs_0_, f32[3,128,512]{2,1,0:T(8,128)S(1)} %get-tuple-element.55.refs_2_.refs_1_, f32[3,128,512]{2,1,0:T(8,128)S(1)} %get-tuple-element.56.refs_3_.refs_2_), custom_call_target="tpu_custom_call" | custom-call | flops 2415919104 | bytes 1572864 | tf_op jit(solution)/shard_map/pallas_call | solution.py:35
  29.7 3.0 %collective-permute-done.9 = f32[3,24,512]{2,1,0:T(8,128)S(1)} collective-permute-done((f32[3,24,512]{2,1,0:T(8,128)S(1)}, f32[3,24,512]{2,1,0:T(8,128)S(1)}, u32[]{:S(2)}, u32[]{:S(2)}) %collective-permute-start.9) | collective-permute-done | bytes 147488 | tf_op jit(solution)/shard_map/ppermute | solution.py:49
  32.7 3.8 %collective-permute-start.11 = (f32[3,8,512]{2,1,0:T(8,128)S(1)}, f32[3,8,512]{2,1,0:T(8,128)S(1)}, u32[]{:S(2)}, u32[]{:S(2)}) collective-permute-start(f32[3,8,512]{2,1,0:T(8,128)S(1)} %get-tuple-element.81), channel_id=1, source_target_pairs={{0,28},{4,8},{8,4},{12,16},{16,12},{20,24},{24,20},{28,0},{1,29},{... | collective-permute-start | bytes 147464 | tf_op jit(solution)/shard_map/ppermute | solution.py:49
  36.5 0.8 shard_map.127
  37.3 2.7 %collective-permute-done.11 = f32[3,8,512]{2,1,0:T(8,128)S(1)} collective-permute-done((f32[3,8,512]{2,1,0:T(8,128)S(1)}, f32[3,8,512]{2,1,0:T(8,128)S(1)}, u32[]{:S(2)}, u32[]{:S(2)}) %collective-permute-start.11) | collective-permute-done | bytes 49184 | tf_op jit(solution)/shard_map/ppermute | solution.py:49
  40.0 0.8 collective-permute-done.10
  40.9 2.6 %collective-permute-start.13 = (f32[3,8,512]{2,1,0:T(8,128)S(1)}, f32[3,8,512]{2,1,0:T(8,128)S(1)}, u32[]{:S(2)}, u32[]{:S(2)}) collective-permute-start(f32[3,8,512]{2,1,0:T(8,128)S(1)} %fusion.1.push), channel_id=1, source_target_pairs={{0,28},{4,8},{8,4},{12,16},{16,12},{20,24},{24,20},{28,0},{1,29},{... | collective-permute-start | bytes 147464 | tf_op jit(solution)/shard_map/ppermute | solution.py:49
  43.4 0.8 shard_map.129.before
  44.2 4.0 %collective-permute-done.13 = f32[3,8,512]{2,1,0:T(8,128)S(1)} collective-permute-done((f32[3,8,512]{2,1,0:T(8,128)S(1)}, f32[3,8,512]{2,1,0:T(8,128)S(1)}, u32[]{:S(2)}, u32[]{:S(2)}) %collective-permute-start.13) | collective-permute-done | bytes 49184 | tf_op jit(solution)/shard_map/ppermute | solution.py:49
  48.3 0.3 collective-permute-done.12
  48.6 0.1 collective-permute-start.14
  48.6 1.1 %collective-permute-start.15 = (f32[3,24,512]{2,1,0:T(8,128)S(1)}, f32[3,24,512]{2,1,0:T(8,128)S(1)}, u32[]{:S(2)}, u32[]{:S(2)}) collective-permute-start(f32[3,24,512]{2,1,0:T(8,128)S(1)} %pad_maximum_fusion.push), channel_id=1, source_target_pairs={{0,3},{1,2},{2,1},{3,0},{4,7},{5,6},{6,5},{7,4},{8,11},{9,10},{10,... | collective-permute-start | bytes 442376 | tf_op jit(solution)/shard_map/ppermute | solution.py:49
  49.8 2.6 %shard_map.130.before = f32[3,128,512]{2,1,0:T(8,128)S(1)} custom-call(s32[8,128]{1,0:T(8,128)S(1)} %get-tuple-element.45.facts, f32[16,80,512]{2,1,0:T(8,128)S(1)} %get-tuple-element.64.saved, f32[3,24,512]{2,1,0:T(8,128)S(1)} %pad_maximum_fusion.push, f32[3,128,512]{2,1,0:T(8,128)S(1)} %shard_map.129.before), custom_call_target="tpu_custom_call" | custom-call | flops 2415919104 | bytes 1572864 | tf_op jit(solution)/shard_map/pallas_call | solution.py:35
  52.4 1.9 %collective-permute-done.15.push_1 = f32[3,24,512]{2,1,0:T(8,128)S(1)} collective-permute-done((f32[3,24,512]{2,1,0:T(8,128)S(1)}, f32[3,24,512]{2,1,0:T(8,128)S(1)}, u32[]{:S(2)}, u32[]{:S(2)}) %collective-permute-start.15) | collective-permute-done | bytes 147488 | tf_op jit(solution)/shard_map/ppermute | solution.py:49
  54.3 5.0 %shard_map.131 = (f32[3,16,32,128]{3,2,1,0:T(8,128)S(1)}, f32[32,640]{1,0:T(8,128)S(1)}, f32[32,640]{1,0:T(8,128)S(1)}, f32[32,640]{1,0:T(8,128)S(1)}, f32[32,640]{1,0:T(8,128)S(1)}) custom-call(s32[8,128]{1,0:T(8,128)S(1)} %get-tuple-element.45.facts, f32[24,80,512]{2,1,0:T(8,128)S(1)} %get-tuple-element.57.saved_0, ...), custom_call_target="tpu_custom_call" | custom-call | flops 7247757312 | bytes 2359296 | tf_op jit(solution)/shard_map/pallas_call | solution.py:35
  59.3 0.9 %collective-permute-start.17 = (f32[32,640]{1,0:T(8,128)S(1)}, f32[32,640]{1,0:T(8,128)S(1)}, u32[]{:S(2)}, u32[]{:S(2)}) collective-permute-start(f32[32,640]{1,0:T(8,128)S(1)} %get-tuple-element.70), channel_id=1, source_target_pairs={{0,3},{1,2},{2,1},{3,0},{4,7},{5,6},{6,5},{7,4},{8,11},{9,10},{10,... | collective-permute-start | bytes 245768 | tf_op jit(solution)/shard_map/ppermute | solution.py:927
  60.2 1.2 %collective-permute-start.18 = (f32[32,640]{1,0:T(8,128)S(1)}, f32[32,640]{1,0:T(8,128)S(1)}, u32[]{:S(2)}, u32[]{:S(2)}) collective-permute-start(f32[32,640]{1,0:T(8,128)S(1)} %get-tuple-element.71), channel_id=1, source_target_pairs={{0,1},{1,0},{2,3},{3,2},{4,5},{5,4},{6,7},{7,6},{8,9},{9,8},{10,11... | collective-permute-start | bytes 245768 | tf_op jit(solution)/shard_map/ppermute | solution.py:927
  61.4 2.7 %collective-permute-done.16.refs_1_ = f32[32,640]{1,0:T(8,128)S(1)} collective-permute-done((f32[32,640]{1,0:T(8,128)S(1)}, f32[32,640]{1,0:T(8,128)S(1)}, u32[]{:S(2)}, u32[]{:S(2)}) %collective-permute-start.16) | collective-permute-done | bytes 81952 | tf_op jit(solution)/shard_map/ppermute | solution.py:927
  64.1 0.9 %shard_map.133 = (f32[144,128]{1,0:T(8,128)S(1)}, f32[144,128]{1,0:T(8,128)S(1)}, f32[144,128]{1,0:T(8,128)S(1)}, f32[144,128]{1,0:T(8,128)S(1)}, f32[144,128]{1...) custom-call(bf16[256,256]{1,0:T(8,128)(2,1)S(1)} %copy-done.6, ...), custom_call_target="tpu_custom_call" | custom-call | flops 201326592 | bytes 786432 | tf_op jit(solution)/shard_map/pallas_call | solution.py:35
  65.1 0.8 collective-permute-start.19
  65.9 3.7 %collective-permute-start.20 = (f32[144,128]{1,0:T(8,128)S(1)}, f32[144,128]{1,0:T(8,128)S(1)}, u32[]{:S(2)}, u32[]{:S(2)}) collective-permute-start(f32[144,128]{1,0:T(8,128)S(1)} %get-tuple-element.74), channel_id=1, source_target_pairs={{0,20},{4,16},{8,28},{12,24},{16,4},{20,0},{24,12},{28,8},{1,21},{... | collective-permute-start | bytes 221192 | tf_op jit(solution)/shard_map/ppermute | solution.py:927
  69.6 1.8 %collective-permute-start.21 = (f32[144,128]{1,0:T(8,128)S(1)}, f32[144,128]{1,0:T(8,128)S(1)}, u32[]{:S(2)}, u32[]{:S(2)}) collective-permute-start(f32[144,128]{1,0:T(8,128)S(1)} %get-tuple-element.75), channel_id=1, source_target_pairs={{0,24},{4,28},{8,16},{12,20},{16,8},{20,12},{24,0},{28,4},{1,25},{... | collective-permute-start | bytes 221192 | tf_op jit(solution)/shard_map/ppermute | solution.py:927
  71.4 1.4 %collective-permute-start.22 = (f32[144,128]{1,0:T(8,128)S(1)}, f32[144,128]{1,0:T(8,128)S(1)}, u32[]{:S(2)}, u32[]{:S(2)}) collective-permute-start(f32[144,128]{1,0:T(8,128)S(1)} %get-tuple-element.76), channel_id=1, source_target_pairs={{0,28},{4,24},{8,20},{12,16},{16,12},{20,8},{24,4},{28,0},{1,29},{... | collective-permute-start | bytes 221192 | tf_op jit(solution)/shard_map/ppermute | solution.py:927
  72.8 3.2 %collective-permute-done.19.refs_1_ = f32[144,128]{1,0:T(8,128)S(1)} collective-permute-done((f32[144,128]{1,0:T(8,128)S(1)}, f32[144,128]{1,0:T(8,128)S(1)}, u32[]{:S(2)}, u32[]{:S(2)}) %collective-permute-start.19) | collective-permute-done | bytes 73760 | tf_op jit(solution)/shard_map/ppermute | solution.py:927
  76.0 0.3 collective-permute-start.24
  76.3 3.1 %collective-permute-done.20.refs_2_ = f32[144,128]{1,0:T(8,128)S(1)} collective-permute-done((f32[144,128]{1,0:T(8,128)S(1)}, f32[144,128]{1,0:T(8,128)S(1)}, u32[]{:S(2)}, u32[]{:S(2)}) %collective-permute-start.20) | collective-permute-done | bytes 73760 | tf_op jit(solution)/shard_map/ppermute | solution.py:927
  79.4 1.2 %collective-permute-start.25 = (f32[144,128]{1,0:T(8,128)S(1)}, f32[144,128]{1,0:T(8,128)S(1)}, u32[]{:S(2)}, u32[]{:S(2)}) collective-permute-start(f32[144,128]{1,0:T(8,128)S(1)} %get-tuple-element.79), channel_id=1, source_target_pairs={{0,4},{4,0},{8,12},{12,8},{16,20},{20,16},{24,28},{28,24},{1,5},{5... | collective-permute-start | bytes 221192 | tf_op jit(solution)/shard_map/ppermute | solution.py:927
  80.6 0.9 %shard_map.132 = f32[3,16,32,128]{3,2,1,0:T(8,128)} custom-call(f32[3,16,32,128]{3,2,1,0:T(8,128)S(1)} %get-tuple-element.67.source), custom_call_target="tpu_custom_call" | custom-call | flops 1 | bytes 1572864 | tf_op jit(solution)/shard_map/pallas_call | solution.py:35
  81.5 1.0 %collective-permute-done.24.refs_6_ = f32[144,128]{1,0:T(8,128)S(1)} collective-permute-done((f32[144,128]{1,0:T(8,128)S(1)}, f32[144,128]{1,0:T(8,128)S(1)}, u32[]{:S(2)}, u32[]{:S(2)}) %collective-permute-start.24) | collective-permute-done | bytes 73760 | tf_op jit(solution)/shard_map/ppermute | solution.py:927
  82.5 1.5 %collective-permute-done.25.refs_7_ = f32[144,128]{1,0:T(8,128)S(1)} collective-permute-done((f32[144,128]{1,0:T(8,128)S(1)}, f32[144,128]{1,0:T(8,128)S(1)}, u32[]{:S(2)}, u32[]{:S(2)}) %collective-permute-start.25) | collective-permute-done | bytes 73760 | tf_op jit(solution)/shard_map/ppermute | solution.py:927
  84.0 1.8 %shard_map.134 = f32[2,32,16,128]{3,2,1,0:T(8,128)} custom-call(bf16[384,256]{1,0:T(8,128)(2,1)S(1)} %copy-done.1, bf16[384,256]{1,0:T(8,128)(2,1)S(1)} %copy-done.2, f32[144,128]{1,0:T(8,128)S(1)} %get-tuple-element.72.refs_0_, f32[144,128]{1,0:T(8,128)S(1)} %collective-permute-done.19.refs_1_, f32[144,128]{1,0:T(8,128)S(1)} %collective-permute-done.20.refs_2_, ...), custom_call_target="tpu_custom_call" | custom-call | flops 201326592 | bytes 1572864 | tf_op jit(solution)/shard_map/pallas_call | solution.py:35
  (38 shorter events, 0.3 us)
Async XLA Ops:
  2.7 6.6 %collective-permute-start = (f32[104,128]{1,0:T(8,128)}, f32[104,128]{1,0:T(8,128)S(1)}, u32[]{:S(2)}, u32[]{:S(2)}) collective-permute-start(f32[104,128]{1,0:T(8,128)} %get-tuple-element.41.own), channel_id=1, source_target_pairs={{0,4},{4,0},{8,12},{12,8},{16,20},{20,16},{24,28},{28,24},{1,5},{5... | collective-permute-start | bytes 159752 | tf_op jit(solution)/shard_map/ppermute | solution.py:49
  5.8 7.0 %collective-permute-start.1 = (f32[104,128]{1,0:T(8,128)}, f32[104,128]{1,0:T(8,128)S(1)}, u32[]{:S(2)}, u32[]{:S(2)}) collective-permute-start(f32[104,128]{1,0:T(8,128)} %get-tuple-element.41.own), channel_id=1, source_target_pairs={{0,28},{4,8},{8,4},{12,16},{16,12},{20,24},{24,20},{28,0},{1,29},{... | collective-permute-start | bytes 159752 | tf_op jit(solution)/shard_map/ppermute | solution.py:49
  9.3 5.8 %collective-permute-start.6 = (f32[128,128]{1,0:T(8,128)}, f32[128,128]{1,0:T(8,128)S(1)}, u32[]{:S(2)}, u32[]{:S(2)}) collective-permute-start(f32[128,128]{1,0:T(8,128)} %get-tuple-element.53), channel_id=1, source_target_pairs={{0,4},{4,0},{8,12},{12,8},{16,20},{20,16},{24,28},{28,24},{1,5},{5... | collective-permute-start | bytes 196616 | tf_op jit(solution)/shard_map/ppermute | solution.py:49
  12.8 9.8 %collective-permute-start.4 = (f32[208,128]{1,0:T(8,128)S(1)}, f32[208,128]{1,0:T(8,128)S(1)}, u32[]{:S(2)}, u32[]{:S(2)}) collective-permute-start(f32[208,128]{1,0:T(8,128)S(1)} %shard_map.123), channel_id=1, source_target_pairs={{0,1},{1,0},{2,3},{3,2},{4,5},{5,4},{6,7},{7,6},{8,9},{9,8},{10,11... | collective-permute-start | bytes 319496 | tf_op jit(solution)/shard_map/ppermute | solution.py:49
  12.9 9.8 %collective-permute-start.5 = (f32[208,128]{1,0:T(8,128)S(1)}, f32[208,128]{1,0:T(8,128)S(1)}, u32[]{:S(2)}, u32[]{:S(2)}) collective-permute-start(f32[208,128]{1,0:T(8,128)S(1)} %shard_map.123), channel_id=1, source_target_pairs={{0,3},{1,2},{2,1},{3,0},{4,7},{5,6},{6,5},{7,4},{8,11},{9,10},{10,... | collective-permute-start | bytes 319496 | tf_op jit(solution)/shard_map/ppermute | solution.py:49
  14.5 7.8 %collective-permute-start.2 = (f32[168,128]{1,0:T(8,128)}, f32[168,128]{1,0:T(8,128)S(1)}, u32[]{:S(2)}, u32[]{:S(2)}) collective-permute-start(f32[168,128]{1,0:T(8,128)} %get-tuple-element.43), channel_id=1, source_target_pairs={{0,1},{1,0},{2,3},{3,2},{4,5},{5,4},{6,7},{7,6},{8,9},{9,8},{10,11... | collective-permute-start | bytes 258056 | tf_op jit(solution)/shard_map/ppermute | solution.py:49
  14.6 7.8 %collective-permute-start.3 = (f32[168,128]{1,0:T(8,128)}, f32[168,128]{1,0:T(8,128)S(1)}, u32[]{:S(2)}, u32[]{:S(2)}) collective-permute-start(f32[168,128]{1,0:T(8,128)} %get-tuple-element.44), channel_id=1, source_target_pairs={{0,3},{1,2},{2,1},{3,0},{4,7},{5,6},{6,5},{7,4},{8,11},{9,10},{10,... | collective-permute-start | bytes 258056 | tf_op jit(solution)/shard_map/ppermute | solution.py:49
  15.1 7.2 %collective-permute-start.7 = (f32[128,128]{1,0:T(8,128)}, f32[128,128]{1,0:T(8,128)S(1)}, u32[]{:S(2)}, u32[]{:S(2)}) collective-permute-start(f32[128,128]{1,0:T(8,128)} %get-tuple-element.54), channel_id=1, source_target_pairs={{0,28},{4,8},{8,4},{12,16},{16,12},{20,24},{24,20},{28,0},{1,29},{... | collective-permute-start | bytes 196616 | tf_op jit(solution)/shard_map/ppermute | solution.py:49
  18.7 1.2 %copy-start = (f32[4,16,32,128]{3,2,1,0:T(8,128)S(1)}, f32[4,16,32,128]{3,2,1,0:T(8,128)}, u32[]{:S(2)}) copy-start(f32[4,16,32,128]{3,2,1,0:T(8,128)} %flow.3) | copy-start | bytes 3145732
  19.9 0.8 copy-start.3
  27.0 2.7 %collective-permute-start.8 = (f32[3,24,512]{2,1,0:T(8,128)S(1)}, f32[3,24,512]{2,1,0:T(8,128)S(1)}, u32[]{:S(2)}, u32[]{:S(2)}) collective-permute-start(f32[3,24,512]{2,1,0:T(8,128)S(1)} %get-tuple-element.61), channel_id=1, source_target_pairs={{0,1},{1,0},{2,3},{3,2},{4,5},{5,4},{6,7},{7,6},{8,9},{9,8},{10,11... | collective-permute-start | bytes 442376 | tf_op jit(solution)/shard_map/ppermute | solution.py:49
  27.1 5.6 %collective-permute-start.9 = (f32[3,24,512]{2,1,0:T(8,128)S(1)}, f32[3,24,512]{2,1,0:T(8,128)S(1)}, u32[]{:S(2)}, u32[]{:S(2)}) collective-permute-start(f32[3,24,512]{2,1,0:T(8,128)S(1)} %get-tuple-element.62), channel_id=1, source_target_pairs={{0,3},{1,2},{2,1},{3,0},{4,7},{5,6},{6,5},{7,4},{8,11},{9,10},{10,... | collective-permute-start | bytes 442376 | tf_op jit(solution)/shard_map/ppermute | solution.py:49
  27.2 9.4 %copy-start.4 = (f32[3,128]{1,0:T(4,128)S(1)}, f32[3,128]{1,0:T(4,128)}, u32[]{:S(2)}) copy-start(f32[3,128]{1,0:T(4,128)} %refs_3_.1) | copy-start | bytes 4612
  27.2 9.3 %copy-start.5 = (f32[3,128]{1,0:T(4,128)S(1)}, f32[3,128]{1,0:T(4,128)}, u32[]{:S(2)}) copy-start(f32[3,128]{1,0:T(4,128)} %refs_4_.1) | copy-start | bytes 4612
  32.7 7.2 %collective-permute-start.11 = (f32[3,8,512]{2,1,0:T(8,128)S(1)}, f32[3,8,512]{2,1,0:T(8,128)S(1)}, u32[]{:S(2)}, u32[]{:S(2)}) collective-permute-start(f32[3,8,512]{2,1,0:T(8,128)S(1)} %get-tuple-element.81), channel_id=1, source_target_pairs={{0,28},{4,8},{8,4},{12,16},{16,12},{20,24},{24,20},{28,0},{1,29},{... | collective-permute-start | bytes 147464 | tf_op jit(solution)/shard_map/ppermute | solution.py:49
  36.5 4.3 %collective-permute-start.10 = (f32[3,8,512]{2,1,0:T(8,128)S(1)}, f32[3,8,512]{2,1,0:T(8,128)S(1)}, u32[]{:S(2)}, u32[]{:S(2)}) collective-permute-start(f32[3,8,512]{2,1,0:T(8,128)S(1)} %get-tuple-element.80), channel_id=1, source_target_pairs={{0,4},{4,0},{8,12},{12,8},{16,20},{20,16},{24,28},{28,24},{1,5},{5... | collective-permute-start | bytes 147464 | tf_op jit(solution)/shard_map/ppermute | solution.py:49
  40.9 7.4 %collective-permute-start.13 = (f32[3,8,512]{2,1,0:T(8,128)S(1)}, f32[3,8,512]{2,1,0:T(8,128)S(1)}, u32[]{:S(2)}, u32[]{:S(2)}) collective-permute-start(f32[3,8,512]{2,1,0:T(8,128)S(1)} %fusion.1.push), channel_id=1, source_target_pairs={{0,28},{4,8},{8,4},{12,16},{16,12},{20,24},{24,20},{28,0},{1,29},{... | collective-permute-start | bytes 147464 | tf_op jit(solution)/shard_map/ppermute | solution.py:49
  43.4 5.1 %collective-permute-start.12 = (f32[3,8,512]{2,1,0:T(8,128)S(1)}, f32[3,8,512]{2,1,0:T(8,128)S(1)}, u32[]{:S(2)}, u32[]{:S(2)}) collective-permute-start(f32[3,8,512]{2,1,0:T(8,128)S(1)} %fusion.1.push), channel_id=1, source_target_pairs={{0,4},{4,0},{8,12},{12,8},{16,20},{20,16},{24,28},{28,24},{1,5},{5... | collective-permute-start | bytes 147464 | tf_op jit(solution)/shard_map/ppermute | solution.py:49
  48.6 3.8 %collective-permute-start.14 = (f32[3,24,512]{2,1,0:T(8,128)S(1)}, f32[3,24,512]{2,1,0:T(8,128)S(1)}, u32[]{:S(2)}, u32[]{:S(2)}) collective-permute-start(f32[3,24,512]{2,1,0:T(8,128)S(1)} %pad_maximum_fusion.push), channel_id=1, source_target_pairs={{0,1},{1,0},{2,3},{3,2},{4,5},{5,4},{6,7},{7,6},{8,9},{9,8},{10,11... | collective-permute-start | bytes 442376 | tf_op jit(solution)/shard_map/ppermute | solution.py:49
  48.6 5.6 %collective-permute-start.15 = (f32[3,24,512]{2,1,0:T(8,128)S(1)}, f32[3,24,512]{2,1,0:T(8,128)S(1)}, u32[]{:S(2)}, u32[]{:S(2)}) collective-permute-start(f32[3,24,512]{2,1,0:T(8,128)S(1)} %pad_maximum_fusion.push), channel_id=1, source_target_pairs={{0,3},{1,2},{2,1},{3,0},{4,7},{5,6},{6,5},{7,4},{8,11},{9,10},{10,... | collective-permute-start | bytes 442376 | tf_op jit(solution)/shard_map/ppermute | solution.py:49
  54.2 9.9 %copy-start.6 = (bf16[256,256]{1,0:T(8,128)(2,1)S(1)}, bf16[256,256]{1,0:T(8,128)(2,1)}, u32[]{:S(2)}) copy-start(bf16[256,256]{1,0:T(8,128)(2,1)} %constant.8.clone.table_high) | copy-start | bytes 393220
  54.2 9.9 %copy-start.7 = (bf16[256,256]{1,0:T(8,128)(2,1)S(1)}, bf16[256,256]{1,0:T(8,128)(2,1)}, u32[]{:S(2)}) copy-start(bf16[256,256]{1,0:T(8,128)(2,1)} %constant.9.clone.table_low) | copy-start | bytes 393220
  54.2 29.7 %copy-start.1 = (bf16[384,256]{1,0:T(8,128)(2,1)S(1)}, bf16[384,256]{1,0:T(8,128)(2,1)}, u32[]{:S(2)}) copy-start(bf16[384,256]{1,0:T(8,128)(2,1)} %constant.10.clone.table_high) | copy-start | bytes 589828
  54.2 29.7 %copy-start.2 = (bf16[384,256]{1,0:T(8,128)(2,1)S(1)}, bf16[384,256]{1,0:T(8,128)(2,1)}, u32[]{:S(2)}) copy-start(bf16[384,256]{1,0:T(8,128)(2,1)} %constant.11.clone.table_low) | copy-start | bytes 589828
  59.2 4.9 %collective-permute-start.16 = (f32[32,640]{1,0:T(8,128)S(1)}, f32[32,640]{1,0:T(8,128)S(1)}, u32[]{:S(2)}, u32[]{:S(2)}) collective-permute-start(f32[32,640]{1,0:T(8,128)S(1)} %get-tuple-element.69), channel_id=1, source_target_pairs={{0,2},{1,3},{2,0},{3,1},{4,6},{5,7},{6,4},{7,5},{8,10},{9,11},{10,... | collective-permute-start | bytes 245768 | tf_op jit(solution)/shard_map/ppermute | solution.py:927
  59.3 4.8 %collective-permute-start.17 = (f32[32,640]{1,0:T(8,128)S(1)}, f32[32,640]{1,0:T(8,128)S(1)}, u32[]{:S(2)}, u32[]{:S(2)}) collective-permute-start(f32[32,640]{1,0:T(8,128)S(1)} %get-tuple-element.70), channel_id=1, source_target_pairs={{0,3},{1,2},{2,1},{3,0},{4,7},{5,6},{6,5},{7,4},{8,11},{9,10},{10,... | collective-permute-start | bytes 245768 | tf_op jit(solution)/shard_map/ppermute | solution.py:927
  60.2 3.9 %collective-permute-start.18 = (f32[32,640]{1,0:T(8,128)S(1)}, f32[32,640]{1,0:T(8,128)S(1)}, u32[]{:S(2)}, u32[]{:S(2)}) collective-permute-start(f32[32,640]{1,0:T(8,128)S(1)} %get-tuple-element.71), channel_id=1, source_target_pairs={{0,1},{1,0},{2,3},{3,2},{4,5},{5,4},{6,7},{7,6},{8,9},{9,8},{10,11... | collective-permute-start | bytes 245768 | tf_op jit(solution)/shard_map/ppermute | solution.py:927
  65.1 10.9 %collective-permute-start.19 = (f32[144,128]{1,0:T(8,128)S(1)}, f32[144,128]{1,0:T(8,128)S(1)}, u32[]{:S(2)}, u32[]{:S(2)}) collective-permute-start(f32[144,128]{1,0:T(8,128)S(1)} %get-tuple-element.73), channel_id=1, source_target_pairs={{0,16},{4,20},{8,24},{12,28},{16,0},{20,4},{24,8},{28,12},{1,17},{... | collective-permute-start | bytes 221192 | tf_op jit(solution)/shard_map/ppermute | solution.py:927
  65.9 13.5 %collective-permute-start.20 = (f32[144,128]{1,0:T(8,128)S(1)}, f32[144,128]{1,0:T(8,128)S(1)}, u32[]{:S(2)}, u32[]{:S(2)}) collective-permute-start(f32[144,128]{1,0:T(8,128)S(1)} %get-tuple-element.74), channel_id=1, source_target_pairs={{0,20},{4,16},{8,28},{12,24},{16,4},{20,0},{24,12},{28,8},{1,21},{... | collective-permute-start | bytes 221192 | tf_op jit(solution)/shard_map/ppermute | solution.py:927
  69.6 11.9 %collective-permute-start.21 = (f32[144,128]{1,0:T(8,128)S(1)}, f32[144,128]{1,0:T(8,128)S(1)}, u32[]{:S(2)}, u32[]{:S(2)}) collective-permute-start(f32[144,128]{1,0:T(8,128)S(1)} %get-tuple-element.75), channel_id=1, source_target_pairs={{0,24},{4,28},{8,16},{12,20},{16,8},{20,12},{24,0},{28,4},{1,25},{... | collective-permute-start | bytes 221192 | tf_op jit(solution)/shard_map/ppermute | solution.py:927
  71.4 10.1 %collective-permute-start.22 = (f32[144,128]{1,0:T(8,128)S(1)}, f32[144,128]{1,0:T(8,128)S(1)}, u32[]{:S(2)}, u32[]{:S(2)}) collective-permute-start(f32[144,128]{1,0:T(8,128)S(1)} %get-tuple-element.76), channel_id=1, source_target_pairs={{0,28},{4,24},{8,20},{12,16},{16,12},{20,8},{24,4},{28,0},{1,29},{... | collective-permute-start | bytes 221192 | tf_op jit(solution)/shard_map/ppermute | solution.py:927
  72.8 8.7 %collective-permute-start.23 = (f32[144,128]{1,0:T(8,128)S(1)}, f32[144,128]{1,0:T(8,128)S(1)}, u32[]{:S(2)}, u32[]{:S(2)}) collective-permute-start(f32[144,128]{1,0:T(8,128)S(1)} %get-tuple-element.77), channel_id=1, source_target_pairs={{0,8},{4,12},{8,0},{12,4},{16,24},{20,28},{24,16},{28,20},{1,9},{5... | collective-permute-start | bytes 221192 | tf_op jit(solution)/shard_map/ppermute | solution.py:927
  76.0 6.5 %collective-permute-start.24 = (f32[144,128]{1,0:T(8,128)S(1)}, f32[144,128]{1,0:T(8,128)S(1)}, u32[]{:S(2)}, u32[]{:S(2)}) collective-permute-start(f32[144,128]{1,0:T(8,128)S(1)} %get-tuple-element.78), channel_id=1, source_target_pairs={{0,12},{4,8},{8,4},{12,0},{16,28},{20,24},{24,20},{28,16},{1,13},{... | collective-permute-start | bytes 221192 | tf_op jit(solution)/shard_map/ppermute | solution.py:927
  79.4 4.6 %collective-permute-start.25 = (f32[144,128]{1,0:T(8,128)S(1)}, f32[144,128]{1,0:T(8,128)S(1)}, u32[]{:S(2)}, u32[]{:S(2)}) collective-permute-start(f32[144,128]{1,0:T(8,128)S(1)} %get-tuple-element.79), channel_id=1, source_target_pairs={{0,4},{4,0},{8,12},{12,8},{16,20},{20,16},{24,28},{28,24},{1,5},{5... | collective-permute-start | bytes 221192 | tf_op jit(solution)/shard_map/ppermute | solution.py:927
